TPU v7x, 128 devices: a whole 4x4x4 slice. The times are simulated.
128 devices in a mesh: dp: 32 (over y_lo, z, x), tensor: 4 (over y_hi, core).
Axes of the slice: x: 4, y: 4 (y_hi: 2, y_lo: 2; y = y_hi * 2 + y_lo), z: 4, core: 2. Of those that a mesh axis runs over, the one named last changes fastest.
Arguments:
- tokens_in: bfloat16 [16384, 2048], P(('dp', 'tensor')), may hold values from -6 to 6
- cotangent: bfloat16 [16384, 2048], P(('dp', 'tensor')), may hold values from -6 to 6
- seq_ids: int32 [16384], P('dp'), may hold values from 0 to 1, as said below
- block_ids: int32 [16384], P('dp'), may hold values from 0 to 1, as said below
- positions: int32 [16384], P('dp'), may hold values from 0 to 383, as said below
- attn_gain: bfloat16 [2048], P('dp'), may hold values from 0.5 to 1.5
- ffn_gain: bfloat16 [2048], P('dp'), may hold values from 0.5 to 1.5
- w_query: bfloat16 [2048, 2048], P('dp', 'tensor'), may hold values from -0.125 to 0.125
- w_key: bfloat16 [2048, 256], P('dp', 'tensor'), may hold values from -0.125 to 0.125
- w_value: bfloat16 [2048, 256], P('dp', 'tensor'), may hold values from -0.125 to 0.125
- w_out: bfloat16 [2048, 2048], P('tensor', 'dp'), may hold values from -1 to 1
- w_gate: bfloat16 [2048, 5632], P('dp', 'tensor'), may hold values from -0.125 to 0.125
- w_up: bfloat16 [2048, 5632], P('dp', 'tensor'), may hold values from -0.125 to 0.125
- w_down: bfloat16 [5632, 2048], P('tensor', 'dp'), may hold values from -0.15625 to 0.15625
Outputs:
- result: bfloat16 [16384, 2048], P(('dp', 'tensor'))
- grad_tokens: bfloat16 [16384, 2048], P(('dp', 'tensor'))
- grad_attn_gain: float32 [2048], P('dp')
- grad_ffn_gain: float32 [2048], P('dp')
- grad_w_query: float32 [2048, 2048], P('dp', 'tensor')
- grad_w_key: float32 [2048, 256], P('dp', 'tensor')
- grad_w_value: float32 [2048, 256], P('dp', 'tensor')
- grad_w_out: float32 [2048, 2048], P('tensor', 'dp')
- grad_w_gate: float32 [2048, 5632], P('dp', 'tensor')
- grad_w_up: float32 [2048, 5632], P('dp', 'tensor')
- grad_w_down: float32 [5632, 2048], P('tensor', 'dp')
Inputs may be any that keep to these rules, and one draw needn't show every extreme that they name: `seq_ids`: each run of 512 tokens holds two documents, 0 then 1, each of 128 to 384 tokens; never falls within a run. `positions`: counted from 0 at the start of each document; some document has 384 tokens. `block_ids`: the attention block of the token's place in its document, of 256 places each; some document has 384 tokens.
All inputs are finite; a program needn't handle non-finite values.
Results may differ from a plain program's by a relative error of at most 0.03.
Values may be sent and summed in bfloat16 or wider, within the bound.
A program may use at most 128 MiB of HBM per device.

v0:
```python
import math

import jax
import jax.numpy as jnp
from jax import lax
from jax.sharding import PartitionSpec as P

HD = 64


EPSILON = 1e-05
ROPE_BASE = 10000.0


def rms_scaled(values, gain_row):
    return values * lax.rsqrt(jnp.mean(values * values, -1, keepdims=True) + EPSILON) * gain_row


def rope_tables(places, head_width):
    half_width = head_width // 2
    inv_freq = 1.0 / ROPE_BASE ** (jnp.arange(half_width, dtype=jnp.float32) * 2.0 / head_width)
    angles = places.astype(jnp.float32)[:, None] * inv_freq[None, :]
    angles = jnp.concatenate([angles, angles], -1)
    return (jnp.cos(angles), jnp.sin(angles))


def rotate(values, cosine, sine_rows):
    half_width = values.shape[-1] // 2
    turned = jnp.concatenate([-values[..., half_width:], values[..., :half_width]], -1)
    return values * cosine[:, None, :] + turned * sine_rows[:, None, :]


def rotate_back(grad_rows, cosine, sine_rows):
    half_width = grad_rows.shape[-1] // 2
    scaled = grad_rows * sine_rows[:, None, :]
    turned = jnp.concatenate([scaled[..., half_width:], -scaled[..., :half_width]], -1)
    return grad_rows * cosine[:, None, :] + turned


def matmul(left_op, right_op):
    return jnp.dot(left_op, right_op, preferred_element_type=jnp.float32)


def times_t(left_op, right_op):
    return lax.dot_general(
        left_op, right_op, (((1,), (1,)), ((), ())), preferred_element_type=jnp.float32
    )


def t_times(left_op, right_op):
    return lax.dot_general(
        left_op, right_op, (((0,), (0,)), ((), ())), preferred_element_type=jnp.float32
    )


def gated(gate_rows, up_rows):
    return jax.nn.silu(gate_rows) * up_rows


def per_device(
    tokens_in,
    cotangent,
    seq_ids,
    block_ids,
    positions,
    attn_gain,
    ffn_gain,
    w_query,
    w_key,
    w_value,
    w_out,
    w_gate,
    w_up,
    w_down,
):
    gathered = (
        lax.all_gather(attn_gain, "dp", axis=0, tiled=True),
        lax.all_gather(ffn_gain, "dp", axis=0, tiled=True),
        lax.all_gather(w_query, "dp", axis=0, tiled=True),
        lax.all_gather(w_key, "dp", axis=0, tiled=True),
        lax.all_gather(w_value, "dp", axis=0, tiled=True),
        lax.all_gather(w_out, "dp", axis=1, tiled=True),
        lax.all_gather(w_gate, "dp", axis=0, tiled=True),
        lax.all_gather(w_up, "dp", axis=0, tiled=True),
        lax.all_gather(w_down, "dp", axis=1, tiled=True),
    )
    full_g1, full_g2, full_q, full_k, full_v, full_o, full_gate, full_up, full_down = gathered
    group_len = seq_ids.shape[0]
    heads_here = full_q.shape[1] // HD
    kv_here = full_k.shape[1] // HD
    per_kv = heads_here // kv_here
    block_rows = min(512, group_len)
    blocks = group_len // block_rows
    score_scale = 1.0 / math.sqrt(HD)
    gain_one = full_g1.astype(jnp.float32)
    gain_two = full_g2.astype(jnp.float32)
    inputs = tokens_in.astype(jnp.float32)
    normed_one = rms_scaled(inputs, gain_one).astype(jnp.bfloat16)
    attn_rows = lax.all_gather(normed_one, "tensor", axis=0, tiled=True)
    cosine, sine_rows = rope_tables(positions, HD)
    queries = rotate(
        matmul(attn_rows, full_q).reshape(group_len, heads_here, HD), cosine, sine_rows
    ).astype(jnp.bfloat16)
    key_rows = rotate(
        matmul(attn_rows, full_k).reshape(group_len, kv_here, HD), cosine, sine_rows
    ).astype(jnp.bfloat16)
    value_rows = matmul(attn_rows, full_v).astype(jnp.bfloat16).reshape(group_len, kv_here, HD)
    queries_g = queries.reshape(group_len, kv_here, per_kv, HD)
    allowed = (seq_ids[:, None] == seq_ids[None, :]) & (block_ids[None, :] <= block_ids[:, None])
    starts = jnp.arange(blocks, dtype=jnp.int32) * block_rows

    def forward_block(offset):
        raw_scores = (
            jnp.einsum("tkhd,skd->khts", queries_g, key_rows, preferred_element_type=jnp.float32)
            * score_scale
        )
        masked = jnp.where(allowed[None, None], raw_scores, -1e30)
        row_max = jnp.max(masked, -1, keepdims=True)
        exp_terms = jnp.exp(masked - row_max)
        row_total = jnp.sum(exp_terms, -1, keepdims=True)
        prob_low = (exp_terms / row_total).astype(jnp.bfloat16)
        mixed_rows = jnp.einsum(
            "khts,skd->tkhd", prob_low, value_rows, preferred_element_type=jnp.float32
        )
        return (mixed_rows.astype(jnp.bfloat16), (row_max + jnp.log(row_total))[..., 0])

    att_blocks, lse_blocks = lax.map(forward_block, starts)
    attended = att_blocks.reshape(group_len, heads_here * HD)
    attn_sum = lax.psum_scatter(matmul(attended, full_o), "tensor", scatter_dimension=0, tiled=True)
    middle = inputs + attn_sum
    normed_two = rms_scaled(middle, gain_two).astype(jnp.bfloat16)
    ffn_rows = lax.all_gather(normed_two, "tensor", axis=0, tiled=True)
    gate_pre = matmul(ffn_rows, full_gate)
    up_pre = matmul(ffn_rows, full_up)
    hidden = gated(gate_pre, up_pre).astype(jnp.bfloat16)
    ffn_sum = lax.psum_scatter(
        matmul(hidden, full_down).astype(jnp.bfloat16), "tensor", scatter_dimension=0, tiled=True
    ).astype(jnp.float32)
    result = (middle + ffn_sum).astype(jnp.bfloat16)
    regathered = (
        lax.all_gather(attn_gain, "dp", axis=0, tiled=True),
        lax.all_gather(ffn_gain, "dp", axis=0, tiled=True),
        lax.all_gather(w_query, "dp", axis=0, tiled=True),
        lax.all_gather(w_key, "dp", axis=0, tiled=True),
        lax.all_gather(w_value, "dp", axis=0, tiled=True),
        lax.all_gather(w_out, "dp", axis=1, tiled=True),
        lax.all_gather(w_gate, "dp", axis=0, tiled=True),
        lax.all_gather(w_up, "dp", axis=0, tiled=True),
        lax.all_gather(w_down, "dp", axis=1, tiled=True),
    )
    full_g1, full_g2, full_q, full_k, full_v, full_o, full_gate, full_up, full_down = regathered
    gain_one = full_g1.astype(jnp.float32)
    gain_two = full_g2.astype(jnp.float32)
    grad_out = cotangent.astype(jnp.float32)
    down_in = lax.all_gather(cotangent, "tensor", axis=0, tiled=True)
    grad_hidden = times_t(down_in, full_down)
    grad_w_down = t_times(hidden, down_in)
    unused_gated, pull_gate = jax.vjp(gated, gate_pre, up_pre)
    grad_gate, grad_up = pull_gate(grad_hidden)
    grad_gate = grad_gate.astype(jnp.bfloat16)
    grad_up = grad_up.astype(jnp.bfloat16)
    grad_w_gate = t_times(ffn_rows, grad_gate)
    grad_w_up = t_times(ffn_rows, grad_up)
    ffn_back = times_t(grad_gate, full_gate) + times_t(grad_up, full_up)
    grad_normed_two = lax.psum_scatter(
        ffn_back.astype(jnp.bfloat16), "tensor", scatter_dimension=0, tiled=True
    ).astype(jnp.float32)
    unused_two, pull_two = jax.vjp(rms_scaled, middle, gain_two)
    grad_middle_norm, grad_gain_two = pull_two(grad_normed_two)
    grad_middle = grad_out + grad_middle_norm
    ffn_grads = (
        lax.psum_scatter(
            grad_w_gate.astype(jnp.bfloat16), "dp", scatter_dimension=0, tiled=True
        ).astype(jnp.float32),
        lax.psum_scatter(
            grad_w_up.astype(jnp.bfloat16), "dp", scatter_dimension=0, tiled=True
        ).astype(jnp.float32),
        lax.psum_scatter(
            grad_w_down.astype(jnp.bfloat16), "dp", scatter_dimension=1, tiled=True
        ).astype(jnp.float32),
        lax.psum_scatter(
            grad_gain_two.astype(jnp.bfloat16), "dp", scatter_dimension=0, tiled=True
        ).astype(jnp.float32),
    )
    out_in = lax.all_gather(grad_middle.astype(jnp.bfloat16), "tensor", axis=0, tiled=True)
    grad_att = times_t(out_in, full_o).astype(jnp.bfloat16)
    grad_w_out = t_times(attended, out_in)
    grad_att_rows = grad_att.reshape(group_len, kv_here, per_kv, HD)

    def backward_step(sums_kv, step_in):
        offset, lse_block = step_in
        raw_scores = (
            jnp.einsum("tkhd,skd->khts", queries_g, key_rows, preferred_element_type=jnp.float32)
            * score_scale
        )
        masked = jnp.where(allowed[None, None], raw_scores, -1e30)
        prob_rows = jnp.exp(masked - lse_block[..., None])
        grad_probs = jnp.einsum(
            "tkhd,skd->khts", grad_att_rows, value_rows, preferred_element_type=jnp.float32
        )
        grad_val_block = jnp.einsum(
            "khts,tkhd->skd",
            prob_rows.astype(jnp.bfloat16),
            grad_att_rows,
            preferred_element_type=jnp.float32,
        )
        row_inner = jnp.sum(prob_rows * grad_probs, -1, keepdims=True)
        grad_raw = (prob_rows * (grad_probs - row_inner) * score_scale).astype(jnp.bfloat16)
        grad_q_block = jnp.einsum(
            "khts,skd->tkhd", grad_raw, key_rows, preferred_element_type=jnp.float32
        )
        grad_key_block = jnp.einsum(
            "khts,tkhd->skd", grad_raw, queries_g, preferred_element_type=jnp.float32
        )
        return ((sums_kv[0] + grad_key_block, sums_kv[1] + grad_val_block), grad_q_block)

    zero_rows = jnp.zeros((group_len, kv_here, HD), jnp.float32)
    kv_sums, grad_q_blocks = lax.scan(backward_step, (zero_rows, zero_rows), (starts, lse_blocks))
    grad_queries = grad_q_blocks.reshape(group_len, heads_here, HD)
    grad_q_pre = (
        rotate_back(grad_queries, cosine, sine_rows)
        .reshape(group_len, heads_here * HD)
        .astype(jnp.bfloat16)
    )
    grad_k_pre = (
        rotate_back(kv_sums[0], cosine, sine_rows)
        .reshape(group_len, kv_here * HD)
        .astype(jnp.bfloat16)
    )
    grad_v_pre = kv_sums[1].reshape(group_len, kv_here * HD).astype(jnp.bfloat16)
    grad_w_query = t_times(attn_rows, grad_q_pre)
    grad_w_key = t_times(attn_rows, grad_k_pre)
    grad_w_value = t_times(attn_rows, grad_v_pre)
    attn_back = (
        times_t(grad_q_pre, full_q) + times_t(grad_k_pre, full_k) + times_t(grad_v_pre, full_v)
    )
    grad_normed_one = lax.psum_scatter(
        attn_back.astype(jnp.bfloat16), "tensor", scatter_dimension=0, tiled=True
    ).astype(jnp.float32)
    unused_one, pull_one = jax.vjp(rms_scaled, inputs, gain_one)
    grad_inputs_norm, grad_gain_one = pull_one(grad_normed_one)
    grad_tokens = (grad_middle + grad_inputs_norm).astype(jnp.bfloat16)
    attn_grads = (
        lax.psum_scatter(
            grad_w_query.astype(jnp.bfloat16), "dp", scatter_dimension=0, tiled=True
        ).astype(jnp.float32),
        lax.psum_scatter(
            grad_w_key.astype(jnp.bfloat16), "dp", scatter_dimension=0, tiled=True
        ).astype(jnp.float32),
        lax.psum_scatter(
            grad_w_value.astype(jnp.bfloat16), "dp", scatter_dimension=0, tiled=True
        ).astype(jnp.float32),
        lax.psum_scatter(
            grad_w_out.astype(jnp.bfloat16), "dp", scatter_dimension=1, tiled=True
        ).astype(jnp.float32),
        lax.psum_scatter(
            grad_gain_one.astype(jnp.bfloat16), "dp", scatter_dimension=0, tiled=True
        ).astype(jnp.float32),
    )
    gain_one_sum, gain_two_sum = lax.psum((attn_grads[4], ffn_grads[3]), "tensor")
    return (
        result,
        grad_tokens,
        gain_one_sum,
        gain_two_sum,
        attn_grads[0],
        attn_grads[1],
        attn_grads[2],
        attn_grads[3],
        ffn_grads[0],
        ffn_grads[1],
        ffn_grads[2],
    )


def solution(mesh):
    placed = (
        P(("dp", "tensor"), None),
        P(("dp", "tensor"), None),
        P("dp"),
        P("dp"),
        P("dp"),
        P("dp"),
        P("dp"),
        P("dp", "tensor"),
        P("dp", "tensor"),
        P("dp", "tensor"),
        P("tensor", "dp"),
        P("dp", "tensor"),
        P("dp", "tensor"),
        P("tensor", "dp"),
    )
    return jax.shard_map(
        per_device,
        mesh=mesh,
        in_specs=placed,
        out_specs=(
            P(("dp", "tensor"), None),
            P(("dp", "tensor"), None),
            P("dp"),
            P("dp"),
            P("dp", "tensor"),
            P("dp", "tensor"),
            P("dp", "tensor"),
            P("tensor", "dp"),
            P("dp", "tensor"),
            P("dp", "tensor"),
            P("tensor", "dp"),
        ),
        check_vma=False,
    )
```

profile of v0, /device:TPU:1, one launch (start us, length us, event | category | flops | bytes accessed | tf_op | source)
XLA Modules:
  0.0 2441.9 jit_solution(5355026027028310788)
XLA Ops:
  12.2 71.7 %all-reduce.6 = (bf16[2048]{0:T(1024)(128)(2,1)S(1)}, bf16[2048]{0:T(1024)(128)(2,1)S(1)}) all-reduce(bf16[2048]{0:T(1024)(128)(2,1)S(1)} %dynamic-update-slice, bf16[2048]{0:T(1024)(128)(2,1)S(1)} %dynamic-update-slice.1), channel_id=1, replica_groups=mesh['dp'=32,'tensor'=4] {'dp'}, use_global_device_ids=true, to_apply=%add | all-reduce | flops 4096 | bytes 16384
  88.3 65.6 %all_gather.51 = bf16[2048,64]{1,0:T(8,128)(2,1)S(1)} all-gather(bf16[64,64]{1,0:T(8,128)(2,1)} %param.22), channel_id=1, replica_groups=mesh['dp'=32,'tensor'=4] {'dp'}, dimensions={0}, use_global_device_ids=true | all-gather | bytes 270336 | tf_op jit(solution)/shard_map/all_gather | solution.py:80
  155.7 68.0 %all_gather.50 = bf16[2048,64]{1,0:T(8,128)(2,1)S(1)} all-gather(bf16[64,64]{1,0:T(8,128)(2,1)S(1)} %copy-done.32), channel_id=1, replica_groups=mesh['dp'=32,'tensor'=4] {'dp'}, dimensions={0}, use_global_device_ids=true | all-gather | bytes 270336 | tf_op jit(solution)/shard_map/all_gather | solution.py:81
  227.3 29.5 %all-gather.12.cloned.1.call-done = bf16[2048,512]{1,0:T(8,128)(2,1)} async-done(((bf16[64,512]{1,0:T(8,128)(2,1)}), bf16[2048,512]{1,0:T(8,128)(2,1)}) %all-gather.12.cloned.1.call-update) | async-done | bytes 2097168 | tf_op jit(solution)/shard_map/all_gather | solution.py:79
  267.5 144.3 %all-gather.14.cloned.1.call-done = bf16[512,2048]{0,1:T(8,128)(2,1)} async-done(((bf16[512,64]{0,1:T(8,128)(2,1)}), bf16[512,2048]{0,1:T(8,128)(2,1)}) %all-gather.14.cloned.1.call-update) | async-done | bytes 2097168 | tf_op jit(solution)/shard_map/all_gather | solution.py:82
  417.3 72.1 %reduce-scatter.12.cloned.1.call-done = f32[128,2048]{1,0:T(8,128)} async-done(((f32[512,2048]{1,0:T(8,128)}), f32[128,2048]{1,0:T(8,128)}) %reduce-scatter.12.cloned.1.call-update) | async-done | bytes 1048592 | tf_op jit(solution)/shard_map/reduce_scatter | solution.py:129
  494.8 138.7 %all-gather.20.cloned.1.call-done = bf16[2048,1408]{1,0:T(8,128)(2,1)} async-done(((bf16[64,1408]{1,0:T(8,128)(2,1)}), bf16[2048,1408]{1,0:T(8,128)(2,1)}) %all-gather.20.cloned.1.call-update) | async-done | bytes 5767184 | tf_op jit(solution)/shard_map/all_gather | solution.py:84
  633.5 48.8 %all-gather.16.cloned.1.call-done = bf16[512,2048]{1,0:T(8,128)(2,1)} async-done(((bf16[128,2048]{1,0:T(8,128)(2,1)}), bf16[512,2048]{1,0:T(8,128)(2,1)}) %all-gather.16.cloned.1.call-update) | async-done | bytes 2097168 | tf_op jit(solution)/shard_map/all_gather | solution.py:132
  682.2 8.2 fusion.75
  690.5 135.5 %all-gather.18.cloned.1.call-done = bf16[2048,1408]{1,0:T(8,128)(2,1)} async-done(((bf16[64,1408]{1,0:T(8,128)(2,1)}), bf16[2048,1408]{1,0:T(8,128)(2,1)}) %all-gather.18.cloned.1.call-update) | async-done | bytes 5767184 | tf_op jit(solution)/shard_map/all_gather | solution.py:83
  826.0 8.3 fusion.74
  834.3 40.1 %all-gather.24.cloned.1.call-done = bf16[512,2048]{1,0:T(8,128)(2,1)} async-done(((bf16[128,2048]{1,0:T(8,128)(2,1)}), bf16[512,2048]{1,0:T(8,128)(2,1)}) %all-gather.24.cloned.1.call-update) | async-done | bytes 2097168 | tf_op jit(solution)/shard_map/all_gather | solution.py:155
  874.3 143.8 %all-gather.22.cloned.1.call-done = bf16[1408,2048]{0,1:T(8,128)(2,1)} async-done(((bf16[1408,64]{0,1:T(8,128)(2,1)}), bf16[1408,2048]{0,1:T(8,128)(2,1)}) %all-gather.22.cloned.1.call-update) | async-done | bytes 5767184 | tf_op jit(solution)/shard_map/all_gather | solution.py:85
  1018.1 10.5 multiply_convert_fusion
  1032.0 7.3 add_convert_fusion.1
  1039.4 57.9 %reduce-scatter.16.cloned.1.call-done = bf16[128,2048]{1,0:T(8,128)(2,1)} async-done(((bf16[512,2048]{1,0:T(8,128)(2,1)}), bf16[128,2048]{1,0:T(8,128)(2,1)}) %reduce-scatter.16.cloned.1.call-update) | async-done | bytes 524304 | tf_op jit(solution)/shard_map/reduce_scatter | solution.py:165
  1102.0 26.4 %all-gather.26.cloned.1.call-done = bf16[512,2048]{1,0:T(8,128)(2,1)} async-done(((bf16[128,2048]{1,0:T(8,128)(2,1)}), bf16[512,2048]{1,0:T(8,128)(2,1)}) %all-gather.26.cloned.1.call-update) | async-done | bytes 2097168 | tf_op jit(solution)/shard_map/all_gather | solution.py:185
  1136.7 8.8 fusion
  1163.3 8.0 convolution_convert_fusion
  1171.4 8.0 convolution_convert_fusion.1
  1179.4 8.0 convolution_convert_fusion.2
  1200.3 7.3 convolution_convert_fusion.5
  1208.4 72.6 %reduce-scatter.24.cloned.1.call-done = bf16[64,64]{1,0:T(8,128)(2,1)} async-done(((bf16[2048,64]{1,0:T(8,128)(2,1)}), bf16[64,64]{1,0:T(8,128)(2,1)}) %reduce-scatter.24.cloned.1.call-update) | async-done | bytes 8208 | tf_op jit(solution)/shard_map/reduce_scatter | solution.py:250
  1282.4 157.0 %reduce-scatter.22.cloned.1.call-done = bf16[64,64]{1,0:T(8,128)(2,1)} async-done(((bf16[2048,64]{1,0:T(8,128)(2,1)}), bf16[64,64]{1,0:T(8,128)(2,1)}) %reduce-scatter.22.cloned.1.call-update) | async-done | bytes 8208 | tf_op jit(solution)/shard_map/reduce_scatter | solution.py:247
  1440.8 162.4 %reduce-scatter.26.cloned.1.call-done = bf16[512,64]{0,1:T(8,128)(2,1)} async-done(((bf16[512,2048]{0,1:T(8,128)(2,1)}), bf16[512,64]{0,1:T(8,128)(2,1)}) %reduce-scatter.26.cloned.1.call-update) | async-done | bytes 65552 | tf_op jit(solution)/shard_map/reduce_scatter | solution.py:253
  1604.6 171.6 %reduce-scatter.32.cloned.1.call-done = bf16[1408,64]{0,1:T(8,128)(2,1)} async-done(((bf16[1408,2048]{0,1:T(8,128)(2,1)}), bf16[1408,64]{0,1:T(8,128)(2,1)}) %reduce-scatter.32.cloned.1.call-update) | async-done | bytes 180240 | tf_op jit(solution)/shard_map/reduce_scatter | solution.py:178
  1777.9 169.2 %reduce-scatter.30.cloned.1.call-done = bf16[64,1408]{1,0:T(8,128)(2,1)} async-done(((bf16[2048,1408]{1,0:T(8,128)(2,1)}), bf16[64,1408]{1,0:T(8,128)(2,1)}) %reduce-scatter.30.cloned.1.call-update) | async-done | bytes 180240 | tf_op jit(solution)/shard_map/reduce_scatter | solution.py:175
  1948.8 169.5 %reduce-scatter.28.cloned.1.call-done = bf16[64,1408]{1,0:T(8,128)(2,1)} async-done(((bf16[2048,1408]{1,0:T(8,128)(2,1)}), bf16[64,1408]{1,0:T(8,128)(2,1)}) %reduce-scatter.28.cloned.1.call-update) | async-done | bytes 180240 | tf_op jit(solution)/shard_map/reduce_scatter | solution.py:172
  2119.9 158.8 %reduce-scatter.20.cloned.1.call-done = bf16[64,512]{1,0:T(8,128)(2,1)} async-done(((bf16[2048,512]{1,0:T(8,128)(2,1)}), bf16[64,512]{1,0:T(8,128)(2,1)}) %reduce-scatter.20.cloned.1.call-update) | async-done | bytes 65552 | tf_op jit(solution)/shard_map/reduce_scatter | solution.py:244
  2280.2 59.0 %reduce-scatter.18.cloned.1.call-done = bf16[128,2048]{1,0:T(8,128)(2,1)} async-done(((bf16[512,2048]{1,0:T(8,128)(2,1)}), bf16[128,2048]{1,0:T(8,128)(2,1)}) %reduce-scatter.18.cloned.1.call-update) | async-done | bytes 524304 | tf_op jit(solution)/shard_map/reduce_scatter | solution.py:237
  2340.9 69.0 %all-reduce.5 = (bf16[2048]{0:T(1024)(128)(2,1)S(1)}, bf16[2048]{0:T(1024)(128)(2,1)S(1)}) all-reduce(bf16[2048]{0:T(1024)(128)(2,1)S(1)} %get-tuple-element.54, bf16[2048]{0:T(1024)(128)(2,1)S(1)} %copy-done.31), channel_id=6, replica_groups=mesh['dp'=32,'tensor'=4] {'dp'}, use_global_device_ids=true, to_apply=%region_12.13.clone | all-reduce | flops 4096 | bytes 16384
  2410.0 21.9 all-reduce.4
  (198 shorter events, 97.4 us)
Async XLA Ops:
  7.2 216.5 %all-gather.10.cloned.1.call-start = ((), (), s32[]{:S(2)}) async-start(), calls=%async_computation.11 | async-start | bytes 2621440 | tf_op jit(solution)/shard_map/all_gather | solution.py:99
  86.0 170.8 %all-gather.12.cloned.1.call-start = ((), (), s32[]{:S(2)}) async-start(), calls=%async_computation.12 | async-start | bytes 2162688 | tf_op jit(solution)/shard_map/all_gather | solution.py:79
  86.8 325.0 %all-gather.14.cloned.1.call-start = ((), (), s32[]{:S(2)}) async-start(), calls=%async_computation.13 | async-start | bytes 2162688 | tf_op jit(solution)/shard_map/all_gather | solution.py:82
  87.5 401.9 %reduce-scatter.12.cloned.1.call-start = ((), (), s32[]{:S(2)}) async-start(), calls=%async_computation.14 | async-start | bytes 5242880 | tf_op jit(solution)/shard_map/reduce_scatter | solution.py:129
  416.7 216.8 %all-gather.20.cloned.1.call-start = ((), (), s32[]{:S(2)}) async-start(), calls=%async_computation.17 | async-start | bytes 5947392 | tf_op jit(solution)/shard_map/all_gather | solution.py:84
  417.3 265.0 %all-gather.16.cloned.1.call-start = ((), (), s32[]{:S(2)}) async-start(), calls=%async_computation.15 | async-start | bytes 2621440 | tf_op jit(solution)/shard_map/all_gather | solution.py:132
  417.3 682.0 %copy-start.23 = (f32[2048]{0:T(1024)}, f32[2048]{0:T(1024)S(1)}, u32[]{:S(2)}) copy-start(f32[2048]{0:T(1024)S(1)} %convert_element_type.189) | copy-start | bytes 24580
  491.0 608.3 %copy-start.35 = (f32[128]{0:T(128)}, f32[128]{0:T(128)S(1)}, u32[]{:S(2)}) copy-start(f32[128]{0:T(128)S(1)} %fusion.65) | copy-start | bytes 1540
  492.0 334.0 %all-gather.18.cloned.1.call-start = ((), (), s32[]{:S(2)}) async-start(), calls=%async_computation.16 | async-start | bytes 5947392 | tf_op jit(solution)/shard_map/all_gather | solution.py:83
  492.8 381.6 %all-gather.24.cloned.1.call-start = ((), (), s32[]{:S(2)}) async-start(), calls=%async_computation.20 | async-start | bytes 2621440 | tf_op jit(solution)/shard_map/all_gather | solution.py:155
  493.5 524.6 %all-gather.22.cloned.1.call-start = ((), (), s32[]{:S(2)}) async-start(), calls=%async_computation.18 | async-start | bytes 5947392 | tf_op jit(solution)/shard_map/all_gather | solution.py:85
  494.2 603.1 %reduce-scatter.16.cloned.1.call-start = ((), (), s32[]{:S(2)}) async-start(), calls=%async_computation.21 | async-start | bytes 2621440 | tf_op jit(solution)/shard_map/reduce_scatter | solution.py:165
  1039.4 89.0 %all-gather.26.cloned.1.call-start = ((), (), s32[]{:S(2)}) async-start(), calls=%async_computation.22 | async-start | bytes 2621440 | tf_op jit(solution)/shard_map/all_gather | solution.py:185
  1101.7 179.3 %reduce-scatter.24.cloned.1.call-start = ((), (), s32[]{:S(2)}) async-start(), calls=%async_computation.26 | async-start | bytes 540672 | tf_op jit(solution)/shard_map/reduce_scatter | solution.py:250
  1147.1 292.3 %reduce-scatter.22.cloned.1.call-start = ((), (), s32[]{:S(2)}) async-start(), calls=%async_computation.25 | async-start | bytes 540672 | tf_op jit(solution)/shard_map/reduce_scatter | solution.py:247
  1158.6 444.5 %reduce-scatter.26.cloned.1.call-start = ((), (), s32[]{:S(2)}) async-start(), calls=%async_computation.27 | async-start | bytes 2162688 | tf_op jit(solution)/shard_map/reduce_scatter | solution.py:253
  1163.0 613.2 %reduce-scatter.32.cloned.1.call-start = ((), (), s32[]{:S(2)}) async-start(), calls=%async_computation.30 | async-start | bytes 5947392 | tf_op jit(solution)/shard_map/reduce_scatter | solution.py:178
  1171.3 775.8 %reduce-scatter.30.cloned.1.call-start = ((), (), s32[]{:S(2)}) async-start(), calls=%async_computation.29 | async-start | bytes 5947392 | tf_op jit(solution)/shard_map/reduce_scatter | solution.py:175
  1179.4 938.9 %reduce-scatter.28.cloned.1.call-start = ((), (), s32[]{:S(2)}) async-start(), calls=%async_computation.28 | async-start | bytes 5947392 | tf_op jit(solution)/shard_map/reduce_scatter | solution.py:172
  1187.4 1091.3 %reduce-scatter.20.cloned.1.call-start = ((), (), s32[]{:S(2)}) async-start(), calls=%async_computation.24 | async-start | bytes 2162688 | tf_op jit(solution)/shard_map/reduce_scatter | solution.py:244
  1194.7 1144.6 %reduce-scatter.18.cloned.1.call-start = ((), (), s32[]{:S(2)}) async-start(), calls=%async_computation.23 | async-start | bytes 2621440 | tf_op jit(solution)/shard_map/reduce_scatter | solution.py:237
  1200.2 1231.7 %reduce-scatter.14.cloned.1.call-start = ((), (), s32[]{:S(2)}) async-start(), calls=%async_computation.19 | async-start | bytes 2621440 | tf_op jit(solution)/shard_map/reduce_scatter | solution.py:136
  1207.6 1131.7 %copy-start.3 = (bf16[128,2048]{1,0:T(8,128)(2,1)S(1)}, bf16[128,2048]{1,0:T(8,128)(2,1)}, u32[]{:S(2)}) copy-start(bf16[128,2048]{1,0:T(8,128)(2,1)} %param.14) | copy-start | bytes 1572868
  1207.6 1131.7 %copy-start.28 = (f32[2048]{0:T(1024)S(1)}, f32[2048]{0:T(1024)}, u32[]{:S(2)}) copy-start(f32[2048]{0:T(1024)} %copy-done.27) | copy-start | bytes 24580
  1207.6 1131.7 %copy-start.38 = (f32[128]{0:T(128)S(1)}, f32[128]{0:T(128)}, u32[]{:S(2)}) copy-start(f32[128]{0:T(128)} %copy-done.37) | copy-start | bytes 1540
  1207.6 1133.3 %copy-start.31 = (bf16[2048]{0:T(1024)(128)(2,1)S(1)}, bf16[2048]{0:T(1024)(128)(2,1)}, u32[]{:S(2)}) copy-start(bf16[2048]{0:T(1024)(128)(2,1)} %get-tuple-element.52) | copy-start | bytes 12292
  1207.6 1224.3 %copy-start.42 = (f32[128]{0:T(128)S(1)}, f32[128]{0:T(128)}, u32[]{:S(2)}) copy-start(f32[128]{0:T(128)} %copy-done.41) | copy-start | bytes 1540
  1207.6 1224.3 %copy-start.8 = (bf16[128,2048]{1,0:T(8,128)(2,1)S(1)}, bf16[128,2048]{1,0:T(8,128)(2,1)}, u32[]{:S(2)}) copy-start(bf16[128,2048]{1,0:T(8,128)(2,1)} %param.15) | copy-start | bytes 1572868
  1207.6 1224.3 %copy-start.9 = (bf16[128,2048]{1,0:T(8,128)(2,1)S(1)}, bf16[128,2048]{1,0:T(8,128)(2,1)}, u32[]{:S(2)}) copy-start(bf16[128,2048]{1,0:T(8,128)(2,1)} %reduce-scatter.16.cloned.1.call-done) | copy-start | bytes 1572868
  1207.6 1224.3 %copy-start.24 = (f32[2048]{0:T(1024)S(1)}, f32[2048]{0:T(1024)}, u32[]{:S(2)}) copy-start(f32[2048]{0:T(1024)} %copy-done.23) | copy-start | bytes 24580
  1207.6 1224.3 %copy-start.36 = (f32[128]{0:T(128)S(1)}, f32[128]{0:T(128)}, u32[]{:S(2)}) copy-start(f32[128]{0:T(128)} %copy-done.35) | copy-start | bytes 1540
  1207.6 1224.3 %copy-start.40 = (f32[128]{0:T(128)S(1)}, f32[128]{0:T(128)}, u32[]{:S(2)}) copy-start(f32[128]{0:T(128)} %copy-done.39) | copy-start | bytes 1540
  (35 other events, 1233.1 us)
Sparse Core Ops, SparseCore 0:
  86.2 37.3 all-gather.9
  125.2 131.6 all-gather.11
  258.5 153.2 all-gather.13
  416.8 72.5 reduce-scatter.11
  491.0 142.3 all-gather.19
  635.7 46.5 all-gather.15
  684.0 141.9 all-gather.17
  827.8 46.5 all-gather.23
  876.1 141.9 all-gather.21
  1039.5 57.8 reduce-scatter.15
  1101.9 26.4 all-gather.25
  1147.2 133.7 reduce-scatter.23
  1283.5 155.8 reduce-scatter.21
  1441.6 161.4 reduce-scatter.25
  1605.5 170.6 reduce-scatter.31
  1778.6 168.4 reduce-scatter.29
  1949.5 168.7 reduce-scatter.27
  2120.6 158.0 reduce-scatter.19
  2281.4 57.8 reduce-scatter.17
  2341.9 37.7 reduce-scatter.13
where the time goes:
time: 2450 us; the launch traced here: 2440 us
  waiting for transfers between devices  1960 us (80%)
  blocking collectives  296 us (12%)
  matrix products  120 us (5%)
  other arithmetic  37.4 us (2%)
    reduce_scatter x1, waiting for transfers between devices, per_device(): lax.psum_scatter(grad_w_down.astype(jnp.bfloat16), 'dp', scatter_dimensio...  172 us
    reduce_scatter x1, waiting for transfers between devices, per_device(): lax.psum_scatter(grad_w_gate.astype(jnp.bfloat16), 'dp', scatter_dimensio...  169 us
    reduce_scatter x1, waiting for transfers between devices, per_device(): lax.psum_scatter(grad_w_up.astype(jnp.bfloat16), 'dp', scatter_dimension=...  169 us
    reduce_scatter x1, waiting for transfers between devices, per_device(): lax.psum_scatter(grad_w_out.astype(jnp.bfloat16), 'dp', scatter_dimension...  162 us
    reduce_scatter x1, waiting for transfers between devices, per_device(): lax.psum_scatter(grad_w_query.astype(jnp.bfloat16), 'dp', scatter_dimensi...  159 us
    reduce_scatter x1, waiting for transfers between devices, per_device(): lax.psum_scatter(grad_w_key.astype(jnp.bfloat16), 'dp', scatter_dimension...  157 us
    all_gather x1, waiting for transfers between devices, per_device(): lax.all_gather(w_out, 'dp', axis=1, tiled=True)  144 us
    all_gather x1, waiting for transfers between devices, per_device(): lax.all_gather(w_down, 'dp', axis=1, tiled=True)  144 us
  transfers between devices with their start and end apart: 20, of which 18 were waited for; matrix products, arithmetic and copies ran while one was open for 4% of the time, Pallas kernels for 0%

commit v1 on v0

v1 whole, which is shorter than its diff:
```python
import functools
import math

import jax
import jax.numpy as jnp
from jax import lax
from jax.experimental import pallas as pl
from jax.experimental.pallas import tpu as pltpu
from jax.sharding import PartitionSpec as P

HD = 64
EPSILON = 1e-05
ROPE_BASE = 10000.0
MESH = pl.DeviceIdType.MESH
BF = jnp.bfloat16
F32 = jnp.float32
ANY = pl.BlockSpec(memory_space=pl.ANY)
VM = pl.BlockSpec(memory_space=pltpu.VMEM)
FH = 768


class Net:
    def __init__(self, send, recv, loc):
        self.send, self.recv, self.loc = send, recv, loc
        self.n = self.m = 0
        dp, t = lax.axis_index("dp"), lax.axis_index("tensor")
        self.a = lax.div(dp, 16)
        self.z = lax.rem(lax.div(dp, 4), 4)
        self.x = lax.rem(dp, 4)
        self.hi = lax.div(t, 2)
        self.c = lax.rem(t, 2)
        self.t = t
        self.sends = []

    def dev(self, a=None, z=None, x=None, hi=None, c=None):
        a = self.a if a is None else a
        z = self.z if z is None else z
        x = self.x if x is None else x
        hi = self.hi if hi is None else hi
        c = self.c if c is None else c
        return (a * 16 + z * 4 + x, hi * 2 + c)

    def xp(self, s):
        return self.dev(x=lax.rem(self.x + s, 4))

    def zp(self, s):
        return self.dev(z=lax.rem(self.z + s, 4))

    def first(self, s, own):
        k = self.a if own else 1 - self.a
        return self.dev(z=lax.rem(self.z + s * k, 4), x=lax.rem(self.x + s * (1 - k), 4))

    def flip(self, da, dh):
        return self.dev(a=1 - self.a if da else None, hi=1 - self.hi if dh else None)

    def sib(self):
        return self.dev(c=1 - self.c)

    def greet(self, peers):
        bar = pltpu.get_barrier_semaphore()
        for p in peers:
            pl.semaphore_signal(bar, inc=1, device_id=p, device_id_type=MESH)
        pl.semaphore_wait(bar, len(peers))

    def put(self, src, dst, dev):
        i = self.n
        self.n += 1
        cp = pltpu.make_async_remote_copy(
            src_ref=src, dst_ref=dst, send_sem=self.send.at[i], recv_sem=self.recv.at[i],
            device_id=dev, device_id_type=MESH,
        )
        cp.start()
        self.sends.append(cp)
        return cp

    def copy(self, src, dst):
        i = self.m
        self.m += 1
        cp = pltpu.make_async_copy(src, dst, self.loc.at[i])
        cp.start()
        return cp

    def finish(self):
        for cp in self.sends:
            cp.wait_send()


FLIP4 = ((0, 1),)
FLIP8 = ((1, 0), (1, 1), (0, 1))
ORDER = (1, 3, 2)


def sems(n, m):
    return [pltpu.SemaphoreType.DMA((n,)), pltpu.SemaphoreType.DMA((n,)), pltpu.SemaphoreType.DMA((m,))]


def all_peers(net):
    return (
        [net.xp(s) for s in ORDER]
        + [net.zp(s) for s in ORDER]
        + [net.sib()]
        + [net.flip(*f) for f in FLIP8]
    )


def k1_body(tok, cot, wq, wo, wg, wu, wd, gn, tok_all, cot_all, aq, ao, ag, au, ad, an, send, recv, loc):
    net = Net(send, recv, loc)
    a, z, x, t, hi, c = net.a, net.z, net.x, net.t, net.hi, net.c
    net.greet(all_peers(net))
    items = [(gn, an, False), (wq, aq, False), (wo, ao, False), (wg, ag, True), (wu, au, True), (wd, ad, True)]
    state = []
    waits = [net.copy(tok, tok_all.at[t]), net.copy(cot, cot_all.at[a, t])]
    got_t = [net.put(tok, tok_all.at[t], net.flip(0, 1))]
    got_c = []
    tail = [net.put(tok, tok_all.at[t], net.sib()), net.put(cot, cot_all.at[a, t], net.sib())]
    for src, dst, half in items:
        own = src.at[a] if half else src
        other = src.at[1 - a] if half else src
        here = dst.at[a, z, x]
        lc = net.copy(own, here)
        yc = net.put(other, here, net.flip(1, 0))
        st = [net.put(own, here, net.first(s, True)) for s in ORDER]
        state.append((dst, lc, yc, st))
    for f in FLIP8:
        got_c.append(net.put(cot, cot_all.at[a, t], net.flip(*f)))
    more = []
    for dst, lc, yc, st in state:
        yc.wait_recv()
        there = dst.at[1 - a, z, x]
        more.append([net.put(there, there, net.first(s, False)) for s in ORDER])
    for (dst, lc, yc, st), so in zip(state, more):
        lc.wait()
        for cp in st + so:
            cp.wait_recv()
        for s in ORDER:
            tail.append(net.put(dst.at[0, z], dst.at[0, z], net.zp(s)))
            tail.append(net.put(dst.at[1, :, x], dst.at[1, :, x], net.xp(s)))
    got_t[0].wait_recv()
    th = (1 - hi) * 2 + c
    tail.append(net.put(tok_all.at[th], tok_all.at[th], net.sib()))
    for (da, dh), cp in zip(FLIP8, got_c):
        cp.wait_recv()
        at = 1 - a if da else a
        tt = th if dh else t
        tail.append(net.put(cot_all.at[at, tt], cot_all.at[at, tt], net.sib()))
    for w in waits:
        w.wait()
    for cp in tail:
        cp.wait_recv()
    net.finish()


def k1(tok, cot, wq, wo, wg, wu, wd, gn):
    def full(w, half):
        return jax.ShapeDtypeStruct((2, 4, 4) + (w.shape[1:] if half else w.shape), BF)

    rows, d = tok.shape
    return pl.pallas_call(
        k1_body,
        out_shape=[
            jax.ShapeDtypeStruct((4, rows, d), BF),
            jax.ShapeDtypeStruct((2, 4, rows, d), BF),
            full(wq, False), full(wo, False), full(wg, True), full(wu, True), full(wd, True), full(gn, False),
        ],
        in_specs=[ANY] * 8,
        out_specs=[ANY] * 8,
        scratch_shapes=sems(96, 10),
        compiler_params=pltpu.CompilerParams(collective_id=1, has_side_effects=True),
        name="gather_all",
    )(tok, cot, wq, wo, wg, wu, wd, gn)


def rms_unit(u):
    return lax.rsqrt(jnp.mean(u * u, -1, keepdims=True) + EPSILON)


def add_to(dst, terms, rows, step=32):
    @pl.loop(0, rows // step)
    def _(i):
        sl = pl.ds(pl.multiple_of(i * step, step), step)
        total = terms[0][sl, :].astype(F32)
        for ref in terms[1:]:
            total += ref[sl, :].astype(F32)
        dst[sl, :] = total.astype(dst.dtype)


def k2_body(part, tok, gain, out, mid, ploc, rc, rh, send, recv, loc):
    net = Net(send, recv, loc)
    a, t, hi, c = net.a, net.t, net.hi, net.c
    net.greet([net.sib()] + [net.flip(*f) for f in FLIP8])
    rows = tok.shape[0]
    far, near = 1 - hi, hi
    cc = [net.put(part.at[h * 2 + (1 - c)], rc.at[i], net.sib()) for i, h in enumerate((far, near))]
    lc = [net.copy(part.at[h * 2 + c], ploc.at[i]) for i, h in enumerate((far, near))]
    lc[0].wait()
    cc[0].wait_recv()
    add_to(ploc.at[0], [ploc.at[0], rc.at[0]], rows)
    ch = net.put(ploc.at[0], rh, net.flip(0, 1))
    lc[1].wait()
    cc[1].wait_recv()
    ch.wait_recv()
    step = 32

    @pl.loop(0, rows // step)
    def _(i):
        sl = pl.ds(pl.multiple_of(i * step, step), step)
        m = (
            tok[sl, :].astype(F32)
            + (ploc[1, sl, :].astype(F32) + rc[1, sl, :].astype(F32))
            + rh[sl, :].astype(F32)
        )
        mid[sl, :] = m
        out[a, t, sl, :] = (m * rms_unit(m) * gain[...]).astype(BF)

    mine = out.at[a, t]
    got = [net.put(mine, mine, net.flip(*f)) for f in FLIP8]
    tail = [net.put(mine, mine, net.sib())]
    th = far * 2 + c
    for (da, dh), cp in zip(FLIP8, got):
        cp.wait_recv()
        blk = out.at[1 - a if da else a, th if dh else t]
        tail.append(net.put(blk, blk, net.sib()))
    for cp in tail:
        cp.wait_recv()
    net.finish()


def k2(part, tok, gain):
    rows, d = tok.shape
    return pl.pallas_call(
        k2_body,
        out_shape=[jax.ShapeDtypeStruct((2, 4, rows, d), BF), jax.ShapeDtypeStruct((rows, d), F32)],
        in_specs=[ANY, VM, VM],
        out_specs=[VM, VM],
        scratch_shapes=[
            pltpu.VMEM((2, rows, d), BF), pltpu.VMEM((2, rows, d), BF), pltpu.VMEM((rows, d), BF),
        ] + sems(12, 2),
        compiler_params=pltpu.CompilerParams(collective_id=2, has_side_effects=True, vmem_limit_bytes=40 << 20),
        name="sum_norm_gather",
    )(part, tok, gain)


def scatter8_start(net, part, ploc, rc):
    a, hi, c = net.a, net.hi, net.c
    chips = [(1 - a if da else a, 1 - hi if dh else hi) for da, dh in FLIP8 + ((0, 0),)]
    cc = [net.put(part.at[b, h * 2 + (1 - c)], rc.at[i], net.sib()) for i, (b, h) in enumerate(chips)]
    lc = [net.copy(part.at[b, h * 2 + c], ploc.at[i]) for i, (b, h) in enumerate(chips)]
    return cc, lc


def scatter8_send(net, cc, lc, ploc, rc, ry, rows):
    out = []
    for i, f in enumerate(FLIP8):
        lc[i].wait()
        cc[i].wait_recv()
        add_to(ploc.at[i], [ploc.at[i], rc.at[i]], rows)
        out.append(net.put(ploc.at[i], ry.at[i], net.flip(*f)))
    lc[3].wait()
    cc[3].wait_recv()
    return out


def norm_back(u, g, gain):
    r = rms_unit(u)
    unit = u * r
    gvec = g * gain
    return r * (gvec - unit * jnp.mean(gvec * unit, -1, keepdims=True))


def k3_body(part, mid, cot, gain, out, gmid, ploc, rc, ry, send, recv, loc):
    net = Net(send, recv, loc)
    t, hi, c = net.t, net.hi, net.c
    net.greet([net.sib()] + [net.flip(*f) for f in FLIP8])
    rows = cot.shape[0]
    cc, lc = scatter8_start(net, part, ploc, rc)
    for cp in scatter8_send(net, cc, lc, ploc, rc, ry, rows):
        cp.wait_recv()
    step = 32

    @pl.loop(0, rows // step)
    def _(i):
        sl = pl.ds(pl.multiple_of(i * step, step), step)
        g = ploc[3, sl, :].astype(F32) + rc[3, sl, :].astype(F32)
        for j in range(3):
            g += ry[j, sl, :].astype(F32)
        gm = cot[sl, :].astype(F32) + norm_back(mid[sl, :], g, gain[...])
        gmid[sl, :] = gm
        out[t, sl, :] = gm.astype(BF)

    mine = out.at[t]
    got = net.put(mine, mine, net.flip(0, 1))
    tail = [net.put(mine, mine, net.sib())]
    got.wait_recv()
    blk = out.at[(1 - hi) * 2 + c]
    tail.append(net.put(blk, blk, net.sib()))
    for cp in tail:
        cp.wait_recv()
    net.finish()


def k3(part, mid, cot, gain):
    rows, d = cot.shape
    return pl.pallas_call(
        k3_body,
        out_shape=[jax.ShapeDtypeStruct((4, rows, d), BF), jax.ShapeDtypeStruct((rows, d), F32)],
        in_specs=[ANY, VM, VM, VM],
        out_specs=[VM, VM],
        scratch_shapes=[
            pltpu.VMEM((4, rows, d), BF), pltpu.VMEM((4, rows, d), BF), pltpu.VMEM((3, rows, d), BF),
        ] + sems(12, 4),
        compiler_params=pltpu.CompilerParams(collective_id=3, has_side_effects=True, vmem_limit_bytes=40 << 20),
        name="sum_normback_gather",
    )(part, mid, cot, gain)


def k4_body(
    pg, pu, pd, po, pq, fpart, apart, mid, tok, gmid, gain,
    og, ou, od, oo, oq, res, gtok,
    lg, lu, ld, lo, lq, r1g, r1u, r1d, r1o, r1q, r2g, r2u, r2d, r2o, r2q, ryo, ryq,
    ploc, rc, ry, aloc, arc, arh, send, recv, loc,
):
    net = Net(send, recv, loc)
    a, z, x, hi, c = net.a, net.z, net.x, net.hi, net.c
    net.greet(all_peers(net))
    rows = tok.shape[0]
    items = [
        (pg, og, lg, r1g, r2g, None), (pu, ou, lu, r1u, r2u, None), (pd, od, ld, r1d, r2d, None),
        (po, oo, lo, r1o, r2o, ryo), (pq, oq, lq, r1q, r2q, ryq),
    ]
    far, near = 1 - hi, hi
    acc = [net.put(apart.at[h * 2 + (1 - c)], arc.at[i], net.sib()) for i, h in enumerate((far, near))]
    alc = [net.copy(apart.at[h * 2 + c], aloc.at[i]) for i, h in enumerate((far, near))]
    st1 = []
    for p, o, l, r1, r2, _ in items:
        lc = [net.copy(p.at[0, z], l.at[0]), net.copy(p.at[1, :, x], l.at[1])]
        got = [[], []]
        for k, s in enumerate(ORDER):
            zz, xx = lax.rem(z + s, 4), lax.rem(x + s, 4)
            got[0].append(net.put(p.at[0, zz], r1.at[0, k], net.zp(s)))
            got[1].append(net.put(p.at[1, :, xx], r1.at[1, k], net.xp(s)))
        st1.append((lc, got))
    fcc, flc = scatter8_start(net, fpart, ploc, rc)
    alc[0].wait()
    acc[0].wait_recv()
    add_to(aloc.at[0], [aloc.at[0], arc.at[0]], rows)
    ach = net.put(aloc.at[0], arh, net.flip(0, 1))
    fgot = scatter8_send(net, fcc, flc, ploc, rc, ry, rows)
    alc[1].wait()
    acc[1].wait_recv()
    ach.wait_recv()
    step = 32

    @pl.loop(0, rows // step)
    def _(i):
        sl = pl.ds(pl.multiple_of(i * step, step), step)
        g = aloc[1, sl, :].astype(F32) + arc[1, sl, :].astype(F32) + arh[sl, :].astype(F32)
        gtok[sl, :] = (gmid[sl, :] + norm_back(tok[sl, :].astype(F32), g, gain[...])).astype(BF)

    for cp in fgot:
        cp.wait_recv()

    @pl.loop(0, rows // step)
    def _(i):
        sl = pl.ds(pl.multiple_of(i * step, step), step)
        g = ploc[3, sl, :].astype(F32) + rc[3, sl, :].astype(F32)
        for j in range(3):
            g += ry[j, sl, :].astype(F32)
        res[sl, :] = (mid[sl, :] + g).astype(BF)

    st2 = []
    for (p, o, l, r1, r2, _), (lc, got) in zip(items, st1):
        nxt = []
        for h in range(2):
            lc[h].wait()
            for cp in got[h]:
                cp.wait_recv()
            for b in range(4):
                add_to(l.at[h, b], [l.at[h, b]] + [r1.at[h, k, b] for k in range(3)], 64)
            me = x if h == 0 else z
            nxt.append([
                net.put(l.at[h, lax.rem(me + s, 4)], r2.at[h, k], net.xp(s) if h == 0 else net.zp(s))
                for k, s in enumerate(ORDER)
            ])
        st2.append(nxt)
    st3 = []
    for (p, o, l, r1, r2, r3), nxt in zip(items, st2):
        for h in range(2):
            for cp in nxt[h]:
                cp.wait_recv()
            me = x if h == 0 else z
            add_to(r2.at[h, 0], [l.at[h, me]] + [r2.at[h, k] for k in range(3)], 64)
        if r3 is None:
            st3.append(net.put(r2.at[1 - a, 0], o.at[a], net.flip(1, 0)))
            o[a, :, :] = r2[a, 0]
        else:
            st3.append(net.put(r2.at[1 - a, 0], r3, net.flip(1, 0)))
    for (p, o, l, r1, r2, r3), cp in zip(items, st3):
        cp.wait_recv()
        if r3 is not None:
            add_to(o, [r2.at[a, 0], r3], 64)
    net.finish()


def k4(grads, fpart, apart, mid, tok, gmid, gain):
    rows, d = tok.shape
    widths = [g.shape[-1] for g in grads]
    outs = [jax.ShapeDtypeStruct((2, 64, w), BF) for w in widths[:3]]
    outs += [jax.ShapeDtypeStruct((64, w), F32) for w in widths[3:]]
    outs += [jax.ShapeDtypeStruct((rows, d), BF)] * 2
    scratch = [pltpu.VMEM((2, 4, 64, w), BF) for w in widths]
    scratch += [pltpu.VMEM((2, 3, 4, 64, w), BF) for w in widths]
    scratch += [pltpu.VMEM((2, 3, 64, w), BF) for w in widths]
    scratch += [pltpu.VMEM((64, w), BF) for w in widths[3:]]
    scratch += [
        pltpu.VMEM((4, rows, d), BF), pltpu.VMEM((4, rows, d), BF), pltpu.VMEM((3, rows, d), BF),
        pltpu.VMEM((2, rows, d), BF), pltpu.VMEM((2, rows, d), BF), pltpu.VMEM((rows, d), BF),
    ]
    return pl.pallas_call(
        k4_body,
        out_shape=outs,
        in_specs=[ANY] * 7 + [VM] * 4,
        out_specs=[VM] * 7,
        scratch_shapes=scratch + sems(96, 24),
        compiler_params=pltpu.CompilerParams(collective_id=4, has_side_effects=True, vmem_limit_bytes=56 << 20),
        name="scatter_all",
    )(*grads, fpart, apart, mid, tok, gmid, gain)


def rope_tables(places, head_width):
    half_width = head_width // 2
    inv_freq = 1.0 / ROPE_BASE ** (jnp.arange(half_width, dtype=F32) * 2.0 / head_width)
    angles = places.astype(F32)[:, None] * inv_freq[None, :]
    angles = jnp.concatenate([angles, angles], -1)
    return (jnp.cos(angles), jnp.sin(angles))


def rotate(values, cosine, sine_rows):
    half_width = values.shape[-1] // 2
    turned = jnp.concatenate([-values[..., half_width:], values[..., :half_width]], -1)
    return values * cosine[:, None, :] + turned * sine_rows[:, None, :]


def rotate_back(grad_rows, cosine, sine_rows):
    half_width = grad_rows.shape[-1] // 2
    scaled = grad_rows * sine_rows[:, None, :]
    turned = jnp.concatenate([scaled[..., half_width:], -scaled[..., :half_width]], -1)
    return grad_rows * cosine[:, None, :] + turned


def mm(l, r, dims=((1,), (0,))):
    return lax.dot_general(l, r, (dims, ((), ())), preferred_element_type=F32)


NT = ((1,), (1,))
TN = ((0,), (0,))


def ein(eq, l, r):
    return jnp.einsum(eq, l, r, preferred_element_type=F32)


def halves(w):
    w = jnp.pad(w, ((0, 0), (0, 2 * FH - w.shape[1])))
    return jnp.stack([w[:, :FH], w[:, FH:]])


def per_device(
    tokens_in, cotangent, seq_ids, block_ids, positions, attn_gain, ffn_gain,
    w_query, w_key, w_value, w_out, w_gate, w_up, w_down,
):
    rows, d = tokens_in.shape
    n = seq_ids.shape[0]
    ff = w_gate.shape[1]
    hq = w_query.shape[1] // HD
    scale = 1.0 / math.sqrt(HD)
    wq = jnp.concatenate([w_query, w_key, w_value], 1)
    wo = w_out.T
    gn = jnp.pad(jnp.stack([attn_gain, ffn_gain]), ((0, 14), (0, 64)))
    tok, cot, wqkv, wot, wg, wu, wdt, gains = k1(
        tokens_in, cotangent, wq, wo, halves(w_gate), halves(w_up), halves(w_down.T), gn
    )
    tok = tok.reshape(n, d)
    cot = cot.reshape(2 * n, d)
    wqkv = wqkv.reshape(d, -1)
    wot = wot.reshape(d, -1)
    wg, wu, wdt = (w.reshape(d, FH) for w in (wg, wu, wdt))
    gains = gains[..., :2, :64].astype(F32)
    g1 = gains[..., 0, :].reshape(1, d)
    g2 = gains[..., 1, :].reshape(1, d)

    inputs = tok.astype(F32)
    xn = (inputs * rms_unit(inputs) * g1).astype(BF)
    qkv = mm(xn, wqkv)
    cosine, sine = rope_tables(positions, HD)
    q = rotate(qkv[:, : hq * HD].reshape(n, hq, HD), cosine, sine).astype(BF)
    k = rotate(qkv[:, hq * HD : hq * HD + HD].reshape(n, 1, HD), cosine, sine).astype(BF)[:, 0]
    v = qkv[:, hq * HD + HD :].astype(BF)
    allowed = (seq_ids[:, None] == seq_ids[None, :]) & (block_ids[None, :] <= block_ids[:, None])
    s = jnp.where(allowed[None], ein("thd,sd->hts", q, k) * scale, -1e30)
    top = jnp.max(s, -1, keepdims=True)
    e = jnp.exp(s - top)
    total = jnp.sum(e, -1, keepdims=True)
    p = e / total
    plow = p.astype(BF)
    att = ein("hts,sd->thd", plow, v).astype(BF).reshape(n, hq * HD)
    part = mm(att, wot, NT).astype(BF).reshape(4, rows, d)
    xf, mid = k2(part, tokens_in, g2)
    xf = xf.reshape(2 * n, d)
    gate = mm(xf, wg)
    up = mm(xf, wu)
    sig = jax.nn.sigmoid(gate)
    silu = gate * sig
    hid = (silu * up).astype(BF)
    gh = mm(cot, wdt)
    dgate = (gh * up * (sig * (1.0 + gate * (1.0 - sig)))).astype(BF)
    dup = (gh * silu).astype(BF)
    fback = (mm(dgate, wg, NT) + mm(dup, wu, NT)).astype(BF)
    gm_all, gmid = k3(fback.reshape(2, 4, rows, d), mid, cotangent, g2)
    gm_all = gm_all.reshape(n, d)
    fout = mm(hid, wdt, NT).astype(BF)
    pd = mm(cot, hid, TN).astype(BF)
    pg = mm(xf, dgate, TN).astype(BF)
    pu = mm(xf, dup, TN).astype(BF)

    gatt = mm(gm_all, wot).astype(BF)
    po = mm(gm_all, att, TN).astype(BF)
    gatt3 = gatt.reshape(n, hq, HD)
    gp = ein("thd,sd->hts", gatt3, v)
    gv = ein("hts,thd->sd", plow, gatt3).astype(BF)
    inner = jnp.sum(p * gp, -1, keepdims=True)
    graw = (p * (gp - inner) * scale).astype(BF)
    gq = ein("hts,sd->thd", graw, k)
    gk = ein("hts,thd->sd", graw, q)
    dq = rotate_back(gq, cosine, sine).reshape(n, hq * HD).astype(BF)
    dk = rotate_back(gk[:, None], cosine, sine)[:, 0].astype(BF)
    dqkv = jnp.concatenate([dq, dk, gv], 1)
    aback = mm(dqkv, wqkv, NT).astype(BF)
    pq = mm(xn, dqkv, TN).astype(BF)

    grads = [w.reshape(2, 4, 4, 64, w.shape[1]) for w in (pg, pu, pd, po, pq)]
    og, ou, od, oo, oq, res, gtok = k4(
        grads, fout.reshape(2, 4, rows, d), aback.reshape(4, rows, d), mid, tokens_in, gmid, g1
    )

    def join(o):
        return jnp.concatenate([o[0], o[1]], 1)[:, :ff].astype(F32)

    og, ou, od = join(og), join(ou), join(od)
    dg1 = jnp.sum(oq * wq.astype(F32), 1) / attn_gain.astype(F32)
    dg2 = jnp.sum(og * w_gate.astype(F32) + ou * w_up.astype(F32), 1) / ffn_gain.astype(F32)
    dg1, dg2 = lax.psum((dg1, dg2), "tensor")
    nq = hq * HD
    return (
        res, gtok, dg1, dg2, oq[:, :nq], oq[:, nq : nq + HD], oq[:, nq + HD :], oo.T, og, ou, od.T,
    )


def solution(mesh):
    both, dp, cols, rows = P(("dp", "tensor"), None), P("dp"), P("dp", "tensor"), P("tensor", "dp")
    return jax.shard_map(
        per_device,
        mesh=mesh,
        in_specs=(both, both, dp, dp, dp, dp, dp, cols, cols, cols, rows, cols, cols, rows),
        out_specs=(both, both, dp, dp, cols, cols, cols, rows, cols, cols, rows),
        check_vma=False,
    )
```

time: 2450 us -> 486 us (0.20)
  waiting for transfers between devices: 1960 us -> 0 us
  Pallas kernels: 0 us -> 321 us
  blocking collectives: 296 us -> 8.85 us
    reduce_scatter x11 -> x0, waiting for transfers between devices: 1250 us -> none  [the longest x1 172 us: per_device(): lax.psum_scatter(grad_w_down.astype(jnp.bfloat16), 'dp', scatter_dimensio...]
    all_gather x9 -> x0, waiting for transfers between devices: 707 us -> none  [the longest x1 144 us: per_device(): lax.all_gather(w_out, 'dp', axis=1, tiled=True)]
    pallas_call x0 -> x4, Pallas kernels: none -> 321 us  [the longest x1 121 us: k1(): pl.pallas_call(k1_body, out_shape=[jax.ShapeDtypeStruct((4, rows, d), BF)...]
    unnamed x2 -> x0, blocking collectives: 141 us -> none
    all_gather x2 -> x0, blocking collectives: 134 us -> none  [the longest x1 68 us: per_device(): lax.all_gather(w_value, 'dp', axis=0, tiled=True)]
    dot_general x27 -> x20, matrix products: 120 us -> 99.3 us  [the longest x15 62.1 us: mm(): return lax.dot_general(l, r, (dims, ((), ())), preferred_element_type=F32)]
  transfers between devices with their start and end apart: 20 -> 0, of which waited for: 18 -> 0; matrix products, arithmetic and copies ran while one was open for 4% -> 0% of each run, Pallas kernels for 0% -> 0%
where the time goes in v1:
time: 486 us; the launch traced here: 478 us
  Pallas kernels  321 us (66%)
  matrix products  105 us (22%)
  other arithmetic  21.1 us (4%)
  local copies, waits for them, and re-layouts  20.4 us (4%)
  blocking collectives  8.85 us (2%)
    pallas_call x1, Pallas kernels, k1(): pl.pallas_call(k1_body, out_shape=[jax.ShapeDtypeStruct((4, rows, d), BF)...  121 us
    pallas_call x1, Pallas kernels, k4(): pl.pallas_call(k4_body, out_shape=outs, in_specs=[ANY] * 7 + [VM] * 4, ou...  107 us
    dot_general x15, matrix products, mm(): return lax.dot_general(l, r, (dims, ((), ())), preferred_element_type=F32)  62.1 us
    pallas_call x1, Pallas kernels, k2(): pl.pallas_call(k2_body, out_shape=[jax.ShapeDtypeStruct((2, 4, rows, d),...  46.3 us
    pallas_call x1, Pallas kernels, k3(): pl.pallas_call(k3_body, out_shape=[jax.ShapeDtypeStruct((4, rows, d), BF)...  46.3 us
    dot_general x5, matrix products, ein(): return jnp.einsum(eq, l, r, preferred_element_type=F32)  37.2 us

profile of v1, /device:TPU:1, one launch (start us, length us, event | category | flops | bytes accessed | tf_op | source)
XLA Modules:
  0.0 477.9 jit_solution(9432503908915271829)
XLA Ops:
  3.3 1.6 pad_maximum_fusion.10.wq
  9.2 1.7 compare_and_fusion
  11.0 121.2 %gather_all.1 = (bf16[4,128,2048]{2,1,0:T(8,128)(2,1)}, bf16[2,4,128,2048]{3,2,1,0:T(8,128)(2,1)}, bf16[2,4,4,64,640]{4,3,2,1,0:T(8,128)(2,1)}, bf16[2,4,4,64,51...) custom-call(bf16[128,2048]{1,0:T(8,128)(2,1)} %tok.5, ...), custom_call_target="tpu_custom_call" | custom-call | tf_op jit(solution)/shard_map/gather_all/pallas_call | solution.py:158
  133.2 2.1 multiply_reduce_fusion
  136.3 1.9 fusion.7
  139.8 1.8 fusion.71
  144.4 1.6 copy.63
  146.0 2.2 maximum_multiply_fusion
  148.2 1.6 copy.64
  152.1 8.3 %fusion.72 = f32[1024,768]{1,0:T(8,128)} fusion(bf16[1024,2048]{1,0:T(8,128)(2,1)} %bitcast.205, bf16[2048,768]{1,0:T(8,128)(2,1)} %bitcast.211), kind=kOutput, calls=%fused_computation.133 | convolution fusion | flops 3221225472 | bytes 10485760 | tf_op jit(solution)/shard_map/dot_general | solution.py:451
  160.4 5.9 %fusion.70 = (f32[8,512]{1,0:T(8,128)}, f32[8,512,512]{1,2,0:T(8,128)}) fusion(pred[512,512]{0,1:T(8,128)(4,1)S(1)} %copy-done.16, bf16[512,64,1]{0,1,2:T(8,128)(2,1)S(1)} %copy-done.19, bf16[512,8,64]{0,2,1:T(8,128)(2,1)S(1)} %bitcast.196), kind=kOutput, calls=%fused_computation.131 | convolution fusion | flops 276824576 | bytes 9256960 | tf_op jit(solution)/shard_map/sub | solution.py:501
  166.3 4.5 fusion.20
  172.2 46.3 %sum_norm_gather.1 = (bf16[2,4,128,2048]{3,2,1,0:T(8,128)(2,1)S(1)}, f32[128,2048]{1,0:T(8,128)S(1)}) custom-call(bf16[4,128,2048]{2,1,0:T(8,128)(2,1)S(1)} %bitcast.174, bf16[128,2048]{1,0:T(8,128)(2,1)S(1)} %copy-done, f32[1,2048]{1,0:T(1,128)S(1)} %reshape_squeeze.6.gain), custom_call_target="tpu_custom_call" | custom-call | tf_op jit(solution)/shard_map/sum_norm_gather/pallas_call | solution.py:230
  218.6 3.4 fusion.73
  222.0 4.5 multiply_convert_fusion.1
  226.6 5.0 %convolution_convert_fusion.1 = bf16[2048,768]{1,0:T(8,128)(2,1)} fusion(bf16[1024,2048]{1,0:T(8,128)(2,1)S(1)} %bitcast.206, bf16[1024,768]{1,0:T(8,128)(2,1)S(1)} %get-tuple-element.56), kind=kOutput, calls=%fused_computation.24 | convolution fusion | flops 3222798336 | bytes 8912896 | tf_op jit(solution)/shard_map/dot_general | solution.py:451
  231.6 5.4 %convolution_convert_fusion = bf16[1024,2048]{1,0:T(8,128)(2,1)} fusion(bf16[1024,768]{1,0:T(8,128)(2,1)S(1)} %get-tuple-element.56, bf16[2048,768]{1,0:T(8,128)(2,1)S(1)} %bitcast.212), kind=kOutput, calls=%fused_computation.20 | convolution fusion | flops 3223322624 | bytes 8912896 | tf_op jit(solution)/shard_map/dot_general | solution.py:451
  237.0 5.0 %convolution_convert_fusion.3 = bf16[2048,768]{1,0:T(8,128)(2,1)} fusion(bf16[1024,2048]{1,0:T(8,128)(2,1)S(1)} %bitcast.177, bf16[1024,768]{1,0:T(8,128)(2,1)S(1)} %get-tuple-element.57), kind=kOutput, calls=%fused_computation.26 | convolution fusion | flops 3222798336 | bytes 8912896 | tf_op jit(solution)/shard_map/dot_general | solution.py:451
  242.0 5.1 %convolution_convert_fusion.2 = bf16[2048,768]{1,0:T(8,128)(2,1)} fusion(bf16[1024,2048]{1,0:T(8,128)(2,1)S(1)} %bitcast.178, bf16[1024,768]{1,0:T(8,128)(2,1)S(1)} %get-tuple-element.58), kind=kOutput, calls=%fused_computation.25 | convolution fusion | flops 3222798336 | bytes 8912896 | tf_op jit(solution)/shard_map/dot_general | solution.py:451
  247.1 5.7 %fusion.74 = f32[1024,2048]{1,0:T(8,128)} fusion(bf16[1024,768]{1,0:T(8,128)(2,1)S(1)} %get-tuple-element.57, bf16[2048,768]{1,0:T(8,128)(2,1)S(1)} %bitcast.210), kind=kOutput, calls=%fused_computation.135 | convolution fusion | flops 3221225472 | bytes 13107200 | tf_op jit(solution)/shard_map/dot_general | solution.py:451
  252.8 6.0 %add_convert_fusion = bf16[1024,2048]{1,0:T(8,128)(2,1)S(1)} fusion(f32[1024,2048]{1,0:T(8,128)} %fusion.74, bf16[1024,768]{1,0:T(8,128)(2,1)S(1)} %copy-done.34, bf16[2048,768]{1,0:T(8,128)(2,1)S(1)} %bitcast.208), kind=kOutput, calls=%fused_computation.8 | convolution fusion | flops 3225419776 | bytes 17301504 | tf_op jit(solution)/shard_map/dot_general | solution.py:451
  258.8 46.3 %sum_normback_gather.1 = (bf16[4,128,2048]{2,1,0:T(8,128)(2,1)S(1)}, f32[128,2048]{1,0:T(8,128)S(1)}) custom-call(bf16[2,4,128,2048]{3,2,1,0:T(8,128)(2,1)S(1)} %bitcast.173, f32[128,2048]{1,0:T(8,128)S(1)} %get-tuple-element.39.mid, bf16[128,2048]{1,0:T(8,128)(2,1)S(1)} %copy-done.2, f32[1,2048]{1,0:T(1,128)S(1)} %reshape_squeeze.6.gain), custom_call_target="tpu_custom_call" | custom-call | tf_op jit(solution)/shard_map/sum_normback_gather/pallas_call | solution.py:303
  306.5 2.7 convolution_convert_fusion.5
  309.2 2.0 fusion.27
  311.2 4.5 fusion.48
  315.8 13.7 %fusion.26 = f32[512,64]{0,1:T(8,128)} fusion(f32[512,512,8]{1,0,2:T(8,128)} %fusion.48, f32[512,8,64]{0,2,1:T(8,128)S(1)} %copy-done.7, f32[512,8,64]{0,2,1:T(8,128)S(1)} %bitcast.182, f32[512,64]{0,1:T(8,128)S(1)} %get-tuple-element.81, f32[8,512,512]{1,2,0:T(8,128)} %get-tuple-element.88, f32[8,512]{1,0:T(8,128)} %get-tuple-element.87), kind=kOutput, calls=%fused_computation.44 | convolution fusion | flops 283906560 | bytes 19152896 | tf_op jit(solution)/shard_map/hts,thd->sd/dot_general | solution.py:459
  329.5 12.4 %broadcast_multiply_fusion = (f32[512,8,64]{0,2,1:T(8,128)S(1)}, f32[512,8,64]{0,2,1:T(8,128)S(1)}) fusion(f32[512,64]{0,1:T(8,128)} %get-tuple-element.83, bf16[512,64,1]{0,1,2:T(8,128)(2,1)} %get-tuple-element.82, f32[512,512,8]{1,0,2:T(8,128)} %fusion.48, f32[8,512,512]{1,2,0:T(8,128)} %get-tuple-element.88, f32[8,512]{1,0:T(8,128)} %get-tuple-element.87), kind=kOutput, calls=%fused_computation.56 | convolution fusion | flops 283382272 | bytes 19087360 | tf_op jit(solution)/shard_map/hts,sd->thd/dot_general | solution.py:459
  343.8 3.2 convolution_convert_fusion.7
  346.9 3.4 convolution_convert_fusion.4
  350.3 107.1 %scatter_all.1 = (bf16[2,64,768]{2,1,0:T(8,128)(2,1)}, bf16[2,64,768]{2,1,0:T(8,128)(2,1)}, bf16[2,64,768]{2,1,0:T(8,128)(2,1)}, f32[64,512]{1,0:T(8,128)}, f32[...) custom-call(bf16[2,4,4,64,768]{4,3,2,1,0:T(8,128)(2,1)} %bitcast.187, ...), custom_call_target="tpu_custom_call" | custom-call | tf_op jit(solution)/shard_map/scatter_all/pallas_call | solution.py:418
  460.3 1.6 slice.126
  466.5 8.8 %all-reduce.4 = (f32[64]{0:T(128)}, f32[64]{0:T(128)}) all-reduce(f32[64]{0:T(128)S(1)} %convert_divide_fusion.1, f32[64]{0:T(128)S(1)} %convert_divide_fusion), channel_id=1, replica_groups=mesh['dp'=32,'tensor'=4] {'tensor'}, use_global_device_ids=true, to_apply=%region_5.6 | all-reduce | flops 128 | bytes 1024 | tf_op jit(solution)/shard_map/psum | solution.py:551
  (122 shorter events, 30.0 us)
Async XLA Ops:
  132.2 4.1 copy-start.4
  139.8 2.0 copy-start.11
  145.9 2.3 copy-start.5
  152.1 8.3 %copy-start.16 = (pred[512,512]{0,1:T(8,128)(4,1)S(1)}, pred[512,512]{0,1:T(8,128)(4,1)}, u32[]{:S(2)}) copy-start(pred[512,512]{0,1:T(8,128)(4,1)} %compare_and_fusion) | copy-start | bytes 786436
  152.1 8.3 %copy-start.19 = (bf16[512,64,1]{0,1,2:T(8,128)(2,1)S(1)}, bf16[512,64,1]{0,1,2:T(8,128)(2,1)}, u32[]{:S(2)}) copy-start(bf16[512,64,1]{0,1,2:T(8,128)(2,1)} %get-tuple-element.82) | copy-start | bytes 196612
  166.3 4.5 copy-start.30
  170.8 47.7 %copy-start.26 = (bf16[2,4,4,64,768]{4,3,2,1,0:T(8,128)(2,1)S(1)}, bf16[2,4,4,64,768]{4,3,2,1,0:T(8,128)(2,1)}, u32[]{:S(2)}) copy-start(bf16[2,4,4,64,768]{4,3,2,1,0:T(8,128)(2,1)} %get-tuple-element.38) | copy-start | bytes 9437188
  218.5 40.3 %copy-start.1 = (f32[128,2048]{1,0:T(8,128)}, f32[128,2048]{1,0:T(8,128)S(1)}, u32[]{:S(2)}) copy-start(f32[128,2048]{1,0:T(8,128)S(1)} %get-tuple-element.39.mid) | copy-start | bytes 3145732
  218.5 3.4 copy-start.25
  218.5 3.4 copy-start.31
  222.0 4.6 copy-start.24
  226.5 15.5 %copy-start.33 = (bf16[1024,768]{1,0:T(8,128)(2,1)}, bf16[1024,768]{1,0:T(8,128)(2,1)S(1)}, u32[]{:S(2)}) copy-start(bf16[1024,768]{1,0:T(8,128)(2,1)S(1)} %get-tuple-element.58) | copy-start | bytes 4718596
  226.6 5.0 %copy-start.27 = (bf16[2,4,4,64,768]{4,3,2,1,0:T(8,128)(2,1)S(1)}, bf16[2,4,4,64,768]{4,3,2,1,0:T(8,128)(2,1)}, u32[]{:S(2)}) copy-start(bf16[2,4,4,64,768]{4,3,2,1,0:T(8,128)(2,1)} %get-tuple-element.36) | copy-start | bytes 9437188
  247.1 5.7 %copy-start.34 = (bf16[1024,768]{1,0:T(8,128)(2,1)S(1)}, bf16[1024,768]{1,0:T(8,128)(2,1)}, u32[]{:S(2)}) copy-start(bf16[1024,768]{1,0:T(8,128)(2,1)} %copy-done.33) | copy-start | bytes 4718596
  252.8 6.0 %copy-start.2 = (bf16[128,2048]{1,0:T(8,128)(2,1)S(1)}, bf16[128,2048]{1,0:T(8,128)(2,1)}, u32[]{:S(2)}) copy-start(bf16[128,2048]{1,0:T(8,128)(2,1)} %cot.3) | copy-start | bytes 1572868
  258.8 50.4 %slice-start = ((s8[8388608]{0:T(1024)(128)(4,1)}), s8[4194304]{0:T(1024)(128)(4,1)S(1)}, s32[]{:S(2)}) async-start(s8[8388608]{0:T(1024)(128)(4,1)} %bitcast.219), calls=%async_computation | async-start | bytes 8388608
  305.1 4.1 slice-start.1
  306.5 2.7 copy-start.35
  311.2 4.6 copy-start.6
  311.2 4.6 copy-start.7
  341.9 1.8 copy-start.29
  343.8 3.2 copy-start.8
  350.3 107.2 %copy-start.17 = (bf16[64,512]{1,0:T(8,128)(2,1)S(1)}, bf16[64,512]{1,0:T(8,128)(2,1)}, u32[]{:S(2)}) copy-start(bf16[64,512]{1,0:T(8,128)(2,1)} %param.21) | copy-start | bytes 196612
  350.3 107.2 %copy-start.20 = (bf16[64,64]{1,0:T(8,128)(2,1)S(1)}, bf16[64,64]{1,0:T(8,128)(2,1)}, u32[]{:S(2)}) copy-start(bf16[64,64]{1,0:T(8,128)(2,1)} %param.23) | copy-start | bytes 24580
  350.3 107.2 %copy-start.21 = (bf16[64,64]{1,0:T(8,128)(2,1)S(1)}, bf16[64,64]{1,0:T(8,128)(2,1)}, u32[]{:S(2)}) copy-start(bf16[64,64]{1,0:T(8,128)(2,1)} %param.22) | copy-start | bytes 24580
  350.3 108.4 %copy-start.22 = (bf16[64]{0:T(256)(128)(2,1)S(1)}, bf16[64]{0:T(256)(128)(2,1)}, u32[]{:S(2)}) copy-start(bf16[64]{0:T(256)(128)(2,1)} %param.19) | copy-start | bytes 388
  350.3 115.2 %copy-start.9 = (bf16[64,1408]{1,0:T(8,128)(2,1)S(1)}, bf16[64,1408]{1,0:T(8,128)(2,1)}, u32[]{:S(2)}) copy-start(bf16[64,1408]{1,0:T(8,128)(2,1)} %param.25) | copy-start | bytes 540676
  350.3 115.1 %copy-start.10 = (bf16[64,1408]{1,0:T(8,128)(2,1)S(1)}, bf16[64,1408]{1,0:T(8,128)(2,1)}, u32[]{:S(2)}) copy-start(bf16[64,1408]{1,0:T(8,128)(2,1)} %param.26) | copy-start | bytes 540676
  457.4 9.1 %copy-start.23 = (bf16[64]{0:T(256)(128)(2,1)S(1)}, bf16[64]{0:T(256)(128)(2,1)}, u32[]{:S(2)}) copy-start(bf16[64]{0:T(256)(128)(2,1)} %param.20) | copy-start | bytes 388
  457.5 17.9 %copy-start.15 = (bf16[128,2048]{1,0:T(8,128)(2,1)S(1)}, bf16[128,2048]{1,0:T(8,128)(2,1)}, u32[]{:S(2)}) copy-start(bf16[128,2048]{1,0:T(8,128)(2,1)} %get-tuple-element.104) | copy-start | bytes 1572868
  457.5 18.7 %copy-start.14 = (bf16[128,2048]{1,0:T(8,128)(2,1)S(1)}, bf16[128,2048]{1,0:T(8,128)(2,1)}, u32[]{:S(2)}) copy-start(bf16[128,2048]{1,0:T(8,128)(2,1)} %get-tuple-element.105) | copy-start | bytes 1572868
  457.5 19.5 %copy-start.18 = (f32[64,512]{1,0:T(8,128)S(1)}, f32[64,512]{1,0:T(8,128)}, u32[]{:S(2)}) copy-start(f32[64,512]{1,0:T(8,128)} %get-tuple-element.47) | copy-start | bytes 393220
  (6 other events, 8.0 us)

commit v2 on v1

--- a/solution.py
+++ b/solution.py
@@ -103,73 +103,6 @@
     )
 
 
-def k1_body(tok, cot, wq, wo, wg, wu, wd, gn, tok_all, cot_all, aq, ao, ag, au, ad, an, send, recv, loc):
-    net = Net(send, recv, loc)
-    a, z, x, t, hi, c = net.a, net.z, net.x, net.t, net.hi, net.c
-    net.greet(all_peers(net))
-    items = [(gn, an, False), (wq, aq, False), (wo, ao, False), (wg, ag, True), (wu, au, True), (wd, ad, True)]
-    state = []
-    waits = [net.copy(tok, tok_all.at[t]), net.copy(cot, cot_all.at[a, t])]
-    got_t = [net.put(tok, tok_all.at[t], net.flip(0, 1))]
-    got_c = []
-    tail = [net.put(tok, tok_all.at[t], net.sib()), net.put(cot, cot_all.at[a, t], net.sib())]
-    for src, dst, half in items:
-        own = src.at[a] if half else src
-        other = src.at[1 - a] if half else src
-        here = dst.at[a, z, x]
-        lc = net.copy(own, here)
-        yc = net.put(other, here, net.flip(1, 0))
-        st = [net.put(own, here, net.first(s, True)) for s in ORDER]
-        state.append((dst, lc, yc, st))
-    for f in FLIP8:
-        got_c.append(net.put(cot, cot_all.at[a, t], net.flip(*f)))
-    more = []
-    for dst, lc, yc, st in state:
-        yc.wait_recv()
-        there = dst.at[1 - a, z, x]
-        more.append([net.put(there, there, net.first(s, False)) for s in ORDER])
-    for (dst, lc, yc, st), so in zip(state, more):
-        lc.wait()
-        for cp in st + so:
-            cp.wait_recv()
-        for s in ORDER:
-            tail.append(net.put(dst.at[0, z], dst.at[0, z], net.zp(s)))
-            tail.append(net.put(dst.at[1, :, x], dst.at[1, :, x], net.xp(s)))
-    got_t[0].wait_recv()
-    th = (1 - hi) * 2 + c
-    tail.append(net.put(tok_all.at[th], tok_all.at[th], net.sib()))
-    for (da, dh), cp in zip(FLIP8, got_c):
-        cp.wait_recv()
-        at = 1 - a if da else a
-        tt = th if dh else t
-        tail.append(net.put(cot_all.at[at, tt], cot_all.at[at, tt], net.sib()))
-    for w in waits:
-        w.wait()
-    for cp in tail:
-        cp.wait_recv()
-    net.finish()
-
-
-def k1(tok, cot, wq, wo, wg, wu, wd, gn):
-    def full(w, half):
-        return jax.ShapeDtypeStruct((2, 4, 4) + (w.shape[1:] if half else w.shape), BF)
-
-    rows, d = tok.shape
-    return pl.pallas_call(
-        k1_body,
-        out_shape=[
-            jax.ShapeDtypeStruct((4, rows, d), BF),
-            jax.ShapeDtypeStruct((2, 4, rows, d), BF),
-            full(wq, False), full(wo, False), full(wg, True), full(wu, True), full(wd, True), full(gn, False),
-        ],
-        in_specs=[ANY] * 8,
-        out_specs=[ANY] * 8,
-        scratch_shapes=sems(96, 10),
-        compiler_params=pltpu.CompilerParams(collective_id=1, has_side_effects=True),
-        name="gather_all",
-    )(tok, cot, wq, wo, wg, wu, wd, gn)
-
-
 def rms_unit(u):
     return lax.rsqrt(jnp.mean(u * u, -1, keepdims=True) + EPSILON)
 
@@ -184,60 +117,232 @@
         dst[sl, :] = total.astype(dst.dtype)
 
 
-def k2_body(part, tok, gain, out, mid, ploc, rc, rh, send, recv, loc):
+def dot(l, r, dims=((1,), (0,))):
+    return lax.dot_general(l, r, (dims, ((), ())), preferred_element_type=F32)
+
+
+NT = ((1,), (1,))
+TN = ((0,), (0,))
+
+
+def low_half(shape):
+    return lax.broadcasted_iota(jnp.int32, shape, 1) < HD
+
+
+def first_quarter(shape):
+    lane = lax.broadcasted_iota(jnp.int32, shape, 1)
+    return lax.rem(lane, HD) < HD // 2
+
+
+def rot(u, cos, sin):
+    near = jnp.where(first_quarter(u.shape), pltpu.roll(u, 96, 1), pltpu.roll(u, 32, 1))
+    return u * cos + near * sin
+
+
+def rot_back(w, cos, sin):
+    y = w * sin
+    near = jnp.where(first_quarter(w.shape), pltpu.roll(y, 96, 1), pltpu.roll(y, 32, 1))
+    return w * cos + near
+
+
+class Gather:
+    def __init__(self, net, src, dst, half):
+        self.net, self.dst = net, dst
+        self.own = src.at[net.a] if half else src
+        self.other = src.at[1 - net.a] if half else src
+        self.here = dst.at[net.a, net.z, net.x]
+
+    def local(self):
+        self.lc = self.net.copy(self.own, self.here)
+
+    def over_y(self):
+        self.yc = self.net.put(self.other, self.here, self.net.flip(1, 0))
+
+    def stage_own(self):
+        self.st = [self.net.put(self.own, self.here, self.net.first(s, True)) for s in ORDER]
+
+    def stage_other(self):
+        net = self.net
+        self.yc.wait_recv()
+        there = self.dst.at[1 - net.a, net.z, net.x]
+        self.st += [net.put(there, there, net.first(s, False)) for s in ORDER]
+
+    def stage_two(self):
+        net, dst = self.net, self.dst
+        self.lc.wait()
+        for cp in self.st:
+            cp.wait_recv()
+        z, x = net.z, net.x
+        self.last = []
+        for s in ORDER:
+            self.last.append(net.put(dst.at[0, z], dst.at[0, z], net.zp(s)))
+            self.last.append(net.put(dst.at[1, :, x], dst.at[1, :, x], net.xp(s)))
+
+    def done(self):
+        for cp in self.last:
+            cp.wait_recv()
+
+
+def m1_body(
+    tok, cot, wq, wo, wg, wu, wd, gn, cos, sin, seqr, seqc, blkr, blkc,
+    xf, mid, xn, q, kv4, att, gains, aq, ao, cot_all, ag, au, ad,
+    tall, an, bias, ones2, kvf, part, rc, rh, send, recv, loc,
+):
     net = Net(send, recv, loc)
-    a, t, hi, c = net.a, net.t, net.hi, net.c
-    net.greet([net.sib()] + [net.flip(*f) for f in FLIP8])
-    rows = tok.shape[0]
+    a, z, x, t, hi, c = net.a, net.z, net.x, net.t, net.hi, net.c
+    rows, d = tok.shape
+    n = 4 * rows
+    net.greet(all_peers(net))
     far, near = 1 - hi, hi
-    cc = [net.put(part.at[h * 2 + (1 - c)], rc.at[i], net.sib()) for i, h in enumerate((far, near))]
-    lc = [net.copy(part.at[h * 2 + c], ploc.at[i]) for i, h in enumerate((far, near))]
-    lc[0].wait()
+    tt = far * 2 + c
+    sib, chip = net.sib(), net.flip(0, 1)
+    tl = net.copy(tok, tall.at[t])
+    tf = net.put(tok, tall.at[t], chip)
+    ts = [net.put(tok, tall.at[t], sib)]
+    gg, gq, go = Gather(net, gn, an, False), Gather(net, wq, aq, False), Gather(net, wo, ao, False)
+    ffn = [Gather(net, w, o, True) for w, o in ((wg, ag), (wu, au), (wd, ad))]
+    for g in (gg, gq, go):
+        g.over_y()
+        g.local()
+        g.stage_own()
+    for g in ffn:
+        g.local()
+    cl = net.copy(cot, cot_all.at[a, t])
+    bias[...] = jnp.where(
+        (seqc[...] == seqr[...]) & (blkr[...] <= blkc[...]), jnp.float32(0.0), jnp.float32(-1e30)
+    )
+    for g in (gg, gq, go):
+        g.stage_other()
+    for g in (gg, gq, go):
+        g.stage_two()
+    tf.wait_recv()
+    ts.append(net.put(tall.at[tt], tall.at[tt], sib))
+    cf = [net.put(cot, cot_all.at[a, t], net.flip(*f)) for f in FLIP8]
+    cs = [net.put(cot, cot_all.at[a, t], sib)]
+    for g in ffn:
+        g.over_y()
+    tl.wait()
+    for cp in ts:
+        cp.wait_recv()
+    gg.done()
+    for i in range(16):
+        k = 2 * i
+        pair = an[k // 16, k // 4 % 4, k % 4] + an[k // 16, k // 4 % 4, k % 4 + 1]
+        gains[:, 128 * i : 128 * i + 128] = pair
+    step = 32
+
+    @pl.loop(0, n // step)
+    def _(i):
+        b = lax.div(i, rows // step)
+        u = tall[b, pl.ds(pl.multiple_of(lax.rem(i, rows // step) * step, step), step), :].astype(F32)
+        xn[pl.ds(pl.multiple_of(i * step, step), step), :] = (u * rms_unit(u) * gains[0:1, :]).astype(BF)
+
+    gq.done()
+    for g in ffn:
+        g.stage_own()
+    scale = 1.0 / math.sqrt(HD)
+    for lo, width in ((0, 256), (256, 256), (512, 128)):
+        w = aq[:, :, :, :, lo : lo + width].reshape(d, width)
+        val = dot(xn[...], w)
+        if lo < 512:
+            for i in range(2):
+                at = lo + 128 * i
+                q[:, at : at + 128] = (rot(val[:, 128 * i : 128 * i + 128], cos[...], sin[...]) * scale).astype(BF)
+        else:
+            low = low_half(val.shape)
+            ke = jnp.where(low, rot(val, cos[...], sin[...]), 0.0)
+            vo = jnp.where(low, 0.0, val)
+            ve = pltpu.roll(vo, 64, 1)
+            kv4[0] = ke.astype(BF)
+            kv4[1] = pltpu.roll(ke, 64, 1).astype(BF)
+            kv4[2] = ve.astype(BF)
+            kv4[3] = vo.astype(BF)
+            ones2[0] = jnp.where(low, ve, 1.0).astype(BF)
+            ones2[1] = jnp.where(low, 1.0, vo).astype(BF)
+    for g in ffn:
+        g.stage_other()
+
+    @pl.loop(0, 4)
+    def _(j):
+        ln = pl.ds(pl.multiple_of(j * 128, 128), 128)
+        qp = q[:, ln]
+        low = low_half((n, 128))
+        o = []
+        for h in range(2):
+            s = dot(qp, kv4[h], NT) + bias[...]
+            e = jnp.exp(s - jnp.max(s, -1, keepdims=True)).astype(BF)
+            o.append(dot(e, ones2[h]))
+        total = jnp.where(low, pltpu.roll(o[0], 64, 1), pltpu.roll(o[1], 64, 1))
+        att[:, ln] = (jnp.where(low, o[0], o[1]) / total).astype(BF)
+
+    go.done()
+    for i in range(4):
+        w = ao[i // 2, 2 * (i % 2) : 2 * (i % 2) + 2].reshape(512, 512)
+        part[:, :, 512 * i : 512 * i + 512] = dot(att[...], w, NT).reshape(4, rows, 512).astype(BF)
+    cc = [net.put(part.at[h * 2 + (1 - c)], rc.at[i], sib) for i, h in enumerate((far, near))]
+    for g in ffn:
+        g.stage_two()
     cc[0].wait_recv()
-    add_to(ploc.at[0], [ploc.at[0], rc.at[0]], rows)
-    ch = net.put(ploc.at[0], rh, net.flip(0, 1))
-    lc[1].wait()
+    pf = part.at[far * 2 + c]
+    add_to(pf, [pf, rc.at[0]], rows)
+    ch = net.put(pf, rh, chip)
+    for (da, dh), cp in zip(FLIP8, cf):
+        cp.wait_recv()
+        blk = cot_all.at[1 - a if da else a, tt if dh else t]
+        cs.append(net.put(blk, blk, sib))
     cc[1].wait_recv()
     ch.wait_recv()
-    step = 32
+    mine_part = part.at[near * 2 + c]
 
     @pl.loop(0, rows // step)
     def _(i):
         sl = pl.ds(pl.multiple_of(i * step, step), step)
         m = (
-            tok[sl, :].astype(F32)
-            + (ploc[1, sl, :].astype(F32) + rc[1, sl, :].astype(F32))
+            tall[t, sl, :].astype(F32)
+            + (mine_part[sl, :].astype(F32) + rc[1, sl, :].astype(F32))
             + rh[sl, :].astype(F32)
         )
         mid[sl, :] = m
-        out[a, t, sl, :] = (m * rms_unit(m) * gain[...]).astype(BF)
-
-    mine = out.at[a, t]
+        xf[a, t, sl, :] = (m * rms_unit(m) * gains[1:2, :]).astype(BF)
+
+    mine = xf.at[a, t]
     got = [net.put(mine, mine, net.flip(*f)) for f in FLIP8]
-    tail = [net.put(mine, mine, net.sib())]
-    th = far * 2 + c
+    tail = [net.put(mine, mine, sib)]
     for (da, dh), cp in zip(FLIP8, got):
         cp.wait_recv()
-        blk = out.at[1 - a if da else a, th if dh else t]
-        tail.append(net.put(blk, blk, net.sib()))
-    for cp in tail:
+        blk = xf.at[1 - a if da else a, tt if dh else t]
+        tail.append(net.put(blk, blk, sib))
+    cl.wait()
+    for g in ffn:
+        g.done()
+    for cp in tail + cs:
         cp.wait_recv()
     net.finish()
 
 
-def k2(part, tok, gain):
+def m1(tok, cot, wq, wo, wg, wu, wd, gn, cos, sin, seq, blk):
     rows, d = tok.shape
+    n = 4 * rows
+    sd = jax.ShapeDtypeStruct
+    col = lambda v: v.reshape(n, 1)
+    row = lambda v: v.reshape(1, n)
     return pl.pallas_call(
-        k2_body,
-        out_shape=[jax.ShapeDtypeStruct((2, 4, rows, d), BF), jax.ShapeDtypeStruct((rows, d), F32)],
-        in_specs=[ANY, VM, VM],
-        out_specs=[VM, VM],
+        m1_body,
+        out_shape=[
+            sd((2, 4, rows, d), BF), sd((rows, d), F32), sd((n, d), BF), sd((n, 512), BF), sd((4, n, 128), BF),
+            sd((n, 512), BF), sd((8, d), F32), sd((2, 4, 4) + wq.shape, BF), sd((2, 4, 4) + wo.shape, BF),
+            sd((2, 4, rows, d), BF),
+        ] + [sd((2, 4, 4) + w.shape[1:], BF) for w in (wg, wu, wd)],
+        in_specs=[ANY] * 8 + [VM] * 6,
+        out_specs=[VM] * 9 + [ANY] * 4,
         scratch_shapes=[
-            pltpu.VMEM((2, rows, d), BF), pltpu.VMEM((2, rows, d), BF), pltpu.VMEM((rows, d), BF),
-        ] + sems(12, 2),
-        compiler_params=pltpu.CompilerParams(collective_id=2, has_side_effects=True, vmem_limit_bytes=40 << 20),
-        name="sum_norm_gather",
-    )(part, tok, gain)
+            pltpu.VMEM((4, rows, d), BF), pltpu.VMEM((2, 4, 4, 8, 128), F32), pltpu.VMEM((n, n), F32),
+            pltpu.VMEM((2, n, 128), BF), pltpu.VMEM((n, 128), F32), pltpu.VMEM((4, rows, d), BF),
+            pltpu.VMEM((2, rows, d), BF), pltpu.VMEM((rows, d), BF),
+        ] + sems(110, 12),
+        compiler_params=pltpu.CompilerParams(collective_id=1, has_side_effects=True, vmem_limit_bytes=56 << 20),
+        name="attention_forward",
+    )(tok, cot, wq, wo, wg, wu, wd, gn, cos, sin, row(seq), col(seq), row(blk), col(blk))
 
 
 def scatter8_start(net, part, ploc, rc):
@@ -451,10 +556,6 @@
     return lax.dot_general(l, r, (dims, ((), ())), preferred_element_type=F32)
 
 
-NT = ((1,), (1,))
-TN = ((0,), (0,))
-
-
 def ein(eq, l, r):
     return jnp.einsum(eq, l, r, preferred_element_type=F32)
 
@@ -475,26 +576,23 @@
     scale = 1.0 / math.sqrt(HD)
     wq = jnp.concatenate([w_query, w_key, w_value], 1)
     wo = w_out.T
-    gn = jnp.pad(jnp.stack([attn_gain, ffn_gain]), ((0, 14), (0, 64)))
-    tok, cot, wqkv, wot, wg, wu, wdt, gains = k1(
-        tokens_in, cotangent, wq, wo, halves(w_gate), halves(w_up), halves(w_down.T), gn
+    gn = jnp.pad(jnp.stack([attn_gain, ffn_gain]).astype(F32), ((0, 6), (0, 64)))
+    gn = jnp.where(lax.rem(lax.axis_index("dp"), 2) == 0, gn, jnp.roll(gn, 64, 1))
+    cosine, sine = rope_tables(positions, HD)
+    half = HD // 2
+    signed = jnp.concatenate([-sine[:, :half], sine[:, half:]], -1)
+    cos2, sin2 = jnp.concatenate([cosine] * 2, -1), jnp.concatenate([signed] * 2, -1)
+    xf, mid, xn, q, kv4, att, gains, wqkv, wot, cot, wg, wu, wdt = m1(
+        tokens_in, cotangent, wq, wo, halves(w_gate), halves(w_up), halves(w_down.T), gn,
+        cos2, sin2, seq_ids, block_ids,
     )
-    tok = tok.reshape(n, d)
     cot = cot.reshape(2 * n, d)
     wqkv = wqkv.reshape(d, -1)
     wot = wot.reshape(d, -1)
     wg, wu, wdt = (w.reshape(d, FH) for w in (wg, wu, wdt))
-    gains = gains[..., :2, :64].astype(F32)
-    g1 = gains[..., 0, :].reshape(1, d)
-    g2 = gains[..., 1, :].reshape(1, d)
-
-    inputs = tok.astype(F32)
-    xn = (inputs * rms_unit(inputs) * g1).astype(BF)
-    qkv = mm(xn, wqkv)
-    cosine, sine = rope_tables(positions, HD)
-    q = rotate(qkv[:, : hq * HD].reshape(n, hq, HD), cosine, sine).astype(BF)
-    k = rotate(qkv[:, hq * HD : hq * HD + HD].reshape(n, 1, HD), cosine, sine).astype(BF)[:, 0]
-    v = qkv[:, hq * HD + HD :].astype(BF)
+    g1, g2 = gains[0:1], gains[1:2]
+    k, v = kv4[0, :, :HD], kv4[2, :, :HD]
+    q = (q * 8).reshape(n, hq, HD)
     allowed = (seq_ids[:, None] == seq_ids[None, :]) & (block_ids[None, :] <= block_ids[:, None])
     s = jnp.where(allowed[None], ein("thd,sd->hts", q, k) * scale, -1e30)
     top = jnp.max(s, -1, keepdims=True)
@@ -502,9 +600,6 @@
     total = jnp.sum(e, -1, keepdims=True)
     p = e / total
     plow = p.astype(BF)
-    att = ein("hts,sd->thd", plow, v).astype(BF).reshape(n, hq * HD)
-    part = mm(att, wot, NT).astype(BF).reshape(4, rows, d)
-    xf, mid = k2(part, tokens_in, g2)
     xf = xf.reshape(2 * n, d)
     gate = mm(xf, wg)
     up = mm(xf, wu)

time: 486 us -> 423 us (0.87)
  Pallas kernels: 321 us -> 280 us
  matrix products: 105 us -> 94.1 us
  other arithmetic: 21.1 us -> 15.1 us
    pallas_call x2 -> x1, Pallas kernels: 168 us -> 123 us  [m1(): pl.pallas_call(m1_body, out_shape=[sd((2, 4, rows, d), BF), sd((rows, d),...]
    dot_general x15 -> x13, matrix products: 62.1 us -> 55.7 us  [mm(): return lax.dot_general(l, r, (dims, ((), ())), preferred_element_type=F32)]
    dot_general x5 -> x4, matrix products: 37.2 us -> 33.5 us  [ein(): return jnp.einsum(eq, l, r, preferred_element_type=F32)]
where the time goes in v2:
time: 423 us; the launch traced here: 415 us
  Pallas kernels  280 us (66%)
  matrix products  94.1 us (22%)
  local copies, waits for them, and re-layouts  15.7 us (4%)
  other arithmetic  15.1 us (4%)
  blocking collectives  8.86 us (2%)
    pallas_call x1, Pallas kernels, m1(): pl.pallas_call(m1_body, out_shape=[sd((2, 4, rows, d), BF), sd((rows, d),...  123 us
    pallas_call x1, Pallas kernels, k4(): pl.pallas_call(k4_body, out_shape=outs, in_specs=[ANY] * 7 + [VM] * 4, ou...  107 us
    dot_general x13, matrix products, mm(): return lax.dot_general(l, r, (dims, ((), ())), preferred_element_type=F32)  55.7 us
    pallas_call x1, Pallas kernels, k3(): pl.pallas_call(k3_body, out_shape=[jax.ShapeDtypeStruct((4, rows, d), BF)...  49.9 us
    dot_general x4, matrix products, ein(): return jnp.einsum(eq, l, r, preferred_element_type=F32)  33.5 us
    psum x1, blocking collectives, per_device(): dg1, dg2 = lax.psum((dg1, dg2), 'tensor')  8.86 us

profile of v2, /device:TPU:1, one launch (start us, length us, event | category | flops | bytes accessed | tf_op | source)
XLA Modules:
  0.0 415.2 jit_solution(51160633800049981)
XLA Ops:
  2.1 1.3 pad_select_fusion.gn
  3.4 1.6 pad_maximum_fusion.12.wq
  9.5 1.5 copy.53.blkc
  12.1 1.1 fusion.28
  13.6 1.1 pad_maximum_fusion.4
  14.8 122.7 %attention_forward.1 = (bf16[2,4,128,2048]{3,2,1,0:T(8,128)(2,1)}, f32[128,2048]{1,0:T(8,128)}, bf16[512,2048]{1,0:T(8,128)(2,1)}, bf16[512,512]{1,0:T(8,128)(2,...) custom-call(bf16[128,2048]{1,0:T(8,128)(2,1)} %tok.3, ...), custom_call_target="tpu_custom_call" | custom-call | tf_op jit(solution)/shard_map/attention_forward/pallas_call | solution.py:329
  137.5 1.5 fusion.70
  139.0 1.1 broadcast_multiply_fusion.1
  140.3 6.5 %fusion.76 = f32[1024,768]{1,0:T(8,128)S(1)} fusion(bf16[1024,2048]{1,0:T(8,128)(2,1)} %bitcast.202, bf16[2048,768]{1,0:T(8,128)(2,1)} %bitcast.208), kind=kOutput, calls=%fused_computation.120 | convolution fusion | flops 3221225472 | bytes 10485760 | tf_op jit(solution)/shard_map/dot_general | solution.py:556
  146.8 3.4 fusion.77
  150.2 4.5 %multiply_convert_fusion = (bf16[1024,768]{1,0:T(8,128)(2,1)S(1)}, bf16[1024,768]{1,0:T(8,128)(2,1)S(1)}, bf16[1024,768]{1,0:T(8,128)(2,1)S(1)}) fusion(f32[1024,768]{1,0:T(8,128)S(1)} %fusion.77, f32[1024,768]{1,0:T(8,128)S(1)} %fusion.76, bf16[1024,2048]{1,0:T(8,128)(2,1)S(1)} %bitcast.199, bf16[2048,768]{1,0:T(8,128)(2,1)S(1)} %bitcast.204), kind=kOutput, calls=%fused_computation.25 | convolution fusion | flops 3233021952 | bytes 18350080 | tf_op jit(solution)/shard_map/dot_general | solution.py:556
  154.8 5.1 %convolution_convert_fusion.1 = bf16[2048,768]{1,0:T(8,128)(2,1)} fusion(bf16[1024,2048]{1,0:T(8,128)(2,1)S(1)} %bitcast.203, bf16[1024,768]{1,0:T(8,128)(2,1)S(1)} %get-tuple-element.60), kind=kOutput, calls=%fused_computation.21 | convolution fusion | flops 3222798336 | bytes 8912896 | tf_op jit(solution)/shard_map/dot_general | solution.py:556
  159.8 5.0 %convolution_convert_fusion = bf16[1024,2048]{1,0:T(8,128)(2,1)} fusion(bf16[1024,768]{1,0:T(8,128)(2,1)S(1)} %get-tuple-element.60, bf16[2048,768]{1,0:T(8,128)(2,1)S(1)} %bitcast.209), kind=kOutput, calls=%fused_computation.17 | convolution fusion | flops 3223322624 | bytes 8912896 | tf_op jit(solution)/shard_map/dot_general | solution.py:556
  164.9 5.0 %convolution_convert_fusion.3 = bf16[2048,768]{1,0:T(8,128)(2,1)} fusion(bf16[1024,2048]{1,0:T(8,128)(2,1)S(1)} %bitcast.200, bf16[1024,768]{1,0:T(8,128)(2,1)S(1)} %get-tuple-element.61), kind=kOutput, calls=%fused_computation.23 | convolution fusion | flops 3222798336 | bytes 8912896 | tf_op jit(solution)/shard_map/dot_general | solution.py:556
  169.9 5.2 %convolution_convert_fusion.2 = bf16[2048,768]{1,0:T(8,128)(2,1)} fusion(bf16[1024,2048]{1,0:T(8,128)(2,1)S(1)} %bitcast.201, bf16[1024,768]{1,0:T(8,128)(2,1)S(1)} %get-tuple-element.62), kind=kOutput, calls=%fused_computation.22 | convolution fusion | flops 3222798336 | bytes 8912896 | tf_op jit(solution)/shard_map/dot_general | solution.py:556
  175.1 3.4 fusion.78
  178.5 5.2 %add_convert_fusion = bf16[1024,2048]{1,0:T(8,128)(2,1)S(1)} fusion(f32[1024,2048]{1,0:T(8,128)S(1)} %fusion.78, bf16[1024,768]{1,0:T(8,128)(2,1)} %copy-done.26, bf16[2048,768]{1,0:T(8,128)(2,1)S(1)} %bitcast.205), kind=kOutput, calls=%fused_computation.9 | convolution fusion | flops 3225419776 | bytes 17301504 | tf_op jit(solution)/shard_map/dot_general | solution.py:556
  183.8 49.9 %sum_normback_gather.1 = (bf16[4,128,2048]{2,1,0:T(8,128)(2,1)S(1)}, f32[128,2048]{1,0:T(8,128)S(1)}) custom-call(bf16[2,4,128,2048]{3,2,1,0:T(8,128)(2,1)S(1)} %bitcast.170, f32[128,2048]{1,0:T(8,128)S(1)} %copy-done, bf16[128,2048]{1,0:T(8,128)(2,1)S(1)} %copy-done.1, f32[1,2048]{1,0:T(1,128)S(1)} %get-tuple-element.86.gain), custom_call_target="tpu_custom_call" | custom-call | tf_op jit(solution)/shard_map/sum_normback_gather/pallas_call | solution.py:408
  233.7 1.3 convolution_convert_fusion.7
  235.1 2.6 convolution_convert_fusion.5
  237.7 4.9 %fusion.71 = (f32[8,512]{1,0:T(8,128)S(1)}, f32[8,512,512]{1,2,0:T(8,128)}) fusion(pred[512,512]{0,1:T(8,128)(4,1)S(1)} %compare_and_fusion, bf16[512,8,64]{0,2,1:T(8,128)(2,1)S(1)} %bitcast.182, bf16[4,512,128]{2,1,0:T(8,128)(2,1)S(1)} %copy-done.11), kind=kOutput, calls=%fused_computation.119 | convolution fusion | flops 276824576 | bytes 9322496 | tf_op jit(solution)/shard_map/sub | solution.py:599
  242.7 4.8 %fusion.20 = bf16[512,64]{0,1:T(8,128)(2,1)S(1)} fusion(bf16[512,8,64]{0,2,1:T(8,128)(2,1)S(1)} %bitcast.180, f32[8,512,512]{1,2,0:T(8,128)} %get-tuple-element.88, f32[8,512]{1,0:T(8,128)S(1)} %get-tuple-element.87), kind=kOutput, calls=%fused_computation.36 | convolution fusion | flops 272662528 | bytes 8994816 | tf_op jit(solution)/shard_map/hts,thd->sd/dot_general | solution.py:560
  247.4 4.5 %fusion.32 = f32[512,512,8]{1,0,2:T(8,128)} fusion(bf16[512,8,64]{0,2,1:T(8,128)(2,1)S(1)} %bitcast.181, bf16[4,512,128]{2,1,0:T(8,128)(2,1)S(1)} %copy-done.11), kind=kOutput, calls=%fused_computation.71 | convolution fusion | flops 268435456 | bytes 9043968 | tf_op jit(solution)/shard_map/thd,sd->hts/dot_general | solution.py:560
  252.0 12.2 %fusion.16 = f32[512,64]{1,0:T(8,128)S(1)} fusion(bf16[512,8,64]{0,2,1:T(8,128)(2,1)S(1)} %bitcast.183, f32[512,512,8]{1,0,2:T(8,128)} %fusion.32, f32[8,512,512]{1,2,0:T(8,128)} %get-tuple-element.88, f32[8,512]{1,0:T(8,128)S(1)} %get-tuple-element.87), kind=kOutput, calls=%fused_computation.34 | convolution fusion | flops 283120128 | bytes 17448960 | tf_op jit(solution)/shard_map/hts,thd->sd/dot_general | solution.py:560
  264.1 12.1 %broadcast_multiply_fusion = (f32[512,8,64]{0,2,1:T(8,128)S(1)}, f32[512,8,64]{0,2,1:T(8,128)S(1)}) fusion(f32[512,64]{0,1:T(8,128)S(1)} %copy.60, f32[512,512,8]{1,0,2:T(8,128)} %fusion.32, f32[8,512,512]{1,2,0:T(8,128)} %get-tuple-element.88, f32[8,512]{1,0:T(8,128)S(1)} %get-tuple-element.87, bf16[4,512,128]{2,1,0:T(8,128)(2,1)S(1)} %copy-done.11), kind=kOutput, calls=%fused_computation.43 | convolution fusion | flops 283382272 | bytes 35946496 | tf_op jit(solution)/shard_map/hts,sd->thd/dot_general | solution.py:560
  278.8 5.1 %convolution_convert_fusion.6 = bf16[512,2048]{1,0:T(8,128)(2,1)} fusion(bf16[2048,640]{1,0:T(8,128)(2,1)} %bitcast.210, bf16[512,64]{0,1:T(8,128)(2,1)S(1)} %fusion.20, bf16[512,64]{0,1:T(8,128)(2,1)S(1)} %copy.65, bf16[512,512]{0,1:T(8,128)(2,1)S(1)} %bitcast.184), kind=kOutput, calls=%fused_computation.31 | convolution fusion | flops 1345191936 | bytes 5373952 | tf_op jit(solution)/shard_map/dot_general | solution.py:556
  284.0 3.3 convolution_convert_fusion.4
  287.3 107.2 %scatter_all.1 = (bf16[2,64,768]{2,1,0:T(8,128)(2,1)}, bf16[2,64,768]{2,1,0:T(8,128)(2,1)}, bf16[2,64,768]{2,1,0:T(8,128)(2,1)}, f32[64,512]{1,0:T(8,128)}, f32[...) custom-call(bf16[2,4,4,64,768]{4,3,2,1,0:T(8,128)(2,1)} %bitcast.175, ...), custom_call_target="tpu_custom_call" | custom-call | tf_op jit(solution)/shard_map/scatter_all/pallas_call | solution.py:523
  394.6 1.2 multiply_reduce_fusion
  395.8 1.5 fusion.69
  397.4 1.6 slice.116
  403.6 8.9 %all-reduce.5 = (f32[64]{0:T(128)}, f32[64]{0:T(128)}) all-reduce(f32[64]{0:T(128)S(1)} %convert_divide_fusion.1, f32[64]{0:T(128)S(1)} %convert_divide_fusion), channel_id=1, replica_groups=mesh['dp'=32,'tensor'=4] {'tensor'}, use_global_device_ids=true, to_apply=%region_4.5 | all-reduce | flops 128 | bytes 1024 | tf_op jit(solution)/shard_map/psum | solution.py:646
  (85 shorter events, 17.2 us)
Async XLA Ops:
  0.6 11.2 %copy-start.13 = (s32[512]{0:T(512)S(1)}, s32[512]{0:T(512)}, u32[]{:S(2)}) copy-start(s32[512]{0:T(512)} %param.17) | copy-start | bytes 6148
  0.7 10.3 %copy-start.12 = (s32[512]{0:T(512)S(1)}, s32[512]{0:T(512)}, u32[]{:S(2)}) copy-start(s32[512]{0:T(512)} %param.16) | copy-start | bytes 6148
  140.3 6.5 %copy-start.16 = (bf16[2,4,128,2048]{3,2,1,0:T(8,128)(2,1)S(1)}, bf16[2,4,128,2048]{3,2,1,0:T(8,128)(2,1)}, u32[]{:S(2)}) copy-start(bf16[2,4,128,2048]{3,2,1,0:T(8,128)(2,1)} %get-tuple-element.33) | copy-start | bytes 12582916
  140.3 6.5 %copy-start.19 = (bf16[2,4,4,64,768]{4,3,2,1,0:T(8,128)(2,1)S(1)}, bf16[2,4,4,64,768]{4,3,2,1,0:T(8,128)(2,1)}, u32[]{:S(2)}) copy-start(bf16[2,4,4,64,768]{4,3,2,1,0:T(8,128)(2,1)} %get-tuple-element.37) | copy-start | bytes 9437188
  146.8 3.4 copy-start.18
  150.2 4.5 %copy-start.17 = (bf16[2,4,128,2048]{3,2,1,0:T(8,128)(2,1)S(1)}, bf16[2,4,128,2048]{3,2,1,0:T(8,128)(2,1)}, u32[]{:S(2)}) copy-start(bf16[2,4,128,2048]{3,2,1,0:T(8,128)(2,1)} %get-tuple-element.34) | copy-start | bytes 12582916
  154.7 10.1 %copy-start.24 = (bf16[1024,768]{1,0:T(8,128)(2,1)}, bf16[1024,768]{1,0:T(8,128)(2,1)S(1)}, u32[]{:S(2)}) copy-start(bf16[1024,768]{1,0:T(8,128)(2,1)S(1)} %get-tuple-element.61) | copy-start | bytes 4718596
  154.7 15.1 %copy-start.26 = (bf16[1024,768]{1,0:T(8,128)(2,1)}, bf16[1024,768]{1,0:T(8,128)(2,1)S(1)}, u32[]{:S(2)}) copy-start(bf16[1024,768]{1,0:T(8,128)(2,1)S(1)} %get-tuple-element.62) | copy-start | bytes 4718596
  154.8 5.1 %copy-start.20 = (bf16[2,4,4,64,768]{4,3,2,1,0:T(8,128)(2,1)S(1)}, bf16[2,4,4,64,768]{4,3,2,1,0:T(8,128)(2,1)}, u32[]{:S(2)}) copy-start(bf16[2,4,4,64,768]{4,3,2,1,0:T(8,128)(2,1)} %get-tuple-element.35) | copy-start | bytes 9437188
  169.9 5.2 %copy-start.25 = (bf16[1024,768]{1,0:T(8,128)(2,1)S(1)}, bf16[1024,768]{1,0:T(8,128)(2,1)}, u32[]{:S(2)}) copy-start(bf16[1024,768]{1,0:T(8,128)(2,1)} %copy-done.24) | copy-start | bytes 4718596
  178.5 5.3 %copy-start = (f32[128,2048]{1,0:T(8,128)S(1)}, f32[128,2048]{1,0:T(8,128)}, u32[]{:S(2)}) copy-start(f32[128,2048]{1,0:T(8,128)} %get-tuple-element.38.mid) | copy-start | bytes 3145732
  178.5 5.3 %copy-start.1 = (bf16[128,2048]{1,0:T(8,128)(2,1)S(1)}, bf16[128,2048]{1,0:T(8,128)(2,1)}, u32[]{:S(2)}) copy-start(bf16[128,2048]{1,0:T(8,128)(2,1)} %cot.3) | copy-start | bytes 1572868
  183.8 49.9 %copy-start.22 = (bf16[2,4,4,64,512]{4,3,2,1,0:T(8,128)(2,1)S(1)}, bf16[2,4,4,64,512]{4,3,2,1,0:T(8,128)(2,1)}, u32[]{:S(2)}) copy-start(bf16[2,4,4,64,512]{4,3,2,1,0:T(8,128)(2,1)} %get-tuple-element.45) | copy-start | bytes 6291460
  233.7 1.3 copy-start.2
  233.7 1.4 copy-start.23
  235.1 2.6 copy-start.11
  278.8 5.2 %copy-start.21 = (bf16[512,2048]{1,0:T(8,128)(2,1)S(1)}, bf16[512,2048]{1,0:T(8,128)(2,1)}, u32[]{:S(2)}) copy-start(bf16[512,2048]{1,0:T(8,128)(2,1)} %get-tuple-element.42) | copy-start | bytes 6291460
  287.3 107.3 %copy-start.7 = (bf16[64,512]{1,0:T(8,128)(2,1)S(1)}, bf16[64,512]{1,0:T(8,128)(2,1)}, u32[]{:S(2)}) copy-start(bf16[64,512]{1,0:T(8,128)(2,1)} %param.21) | copy-start | bytes 196612
  287.3 107.3 %copy-start.9 = (bf16[64,64]{1,0:T(8,128)(2,1)S(1)}, bf16[64,64]{1,0:T(8,128)(2,1)}, u32[]{:S(2)}) copy-start(bf16[64,64]{1,0:T(8,128)(2,1)} %param.23) | copy-start | bytes 24580
  287.3 107.3 %copy-start.10 = (bf16[64,64]{1,0:T(8,128)(2,1)S(1)}, bf16[64,64]{1,0:T(8,128)(2,1)}, u32[]{:S(2)}) copy-start(bf16[64,64]{1,0:T(8,128)(2,1)} %param.22) | copy-start | bytes 24580
  287.3 108.5 %copy-start.14 = (bf16[64]{0:T(256)(128)(2,1)S(1)}, bf16[64]{0:T(256)(128)(2,1)}, u32[]{:S(2)}) copy-start(bf16[64]{0:T(256)(128)(2,1)} %param.19) | copy-start | bytes 388
  287.3 115.3 %copy-start.3 = (bf16[64,1408]{1,0:T(8,128)(2,1)S(1)}, bf16[64,1408]{1,0:T(8,128)(2,1)}, u32[]{:S(2)}) copy-start(bf16[64,1408]{1,0:T(8,128)(2,1)} %param.25) | copy-start | bytes 540676
  287.3 115.3 %copy-start.4 = (bf16[64,1408]{1,0:T(8,128)(2,1)S(1)}, bf16[64,1408]{1,0:T(8,128)(2,1)}, u32[]{:S(2)}) copy-start(bf16[64,1408]{1,0:T(8,128)(2,1)} %param.26) | copy-start | bytes 540676
  394.6 9.1 %copy-start.15 = (bf16[64]{0:T(256)(128)(2,1)S(1)}, bf16[64]{0:T(256)(128)(2,1)}, u32[]{:S(2)}) copy-start(bf16[64]{0:T(256)(128)(2,1)} %param.20) | copy-start | bytes 388
  394.6 17.9 %copy-start.6 = (bf16[128,2048]{1,0:T(8,128)(2,1)S(1)}, bf16[128,2048]{1,0:T(8,128)(2,1)}, u32[]{:S(2)}) copy-start(bf16[128,2048]{1,0:T(8,128)(2,1)} %get-tuple-element.106) | copy-start | bytes 1572868
  394.6 18.7 %copy-start.5 = (bf16[128,2048]{1,0:T(8,128)(2,1)S(1)}, bf16[128,2048]{1,0:T(8,128)(2,1)}, u32[]{:S(2)}) copy-start(bf16[128,2048]{1,0:T(8,128)(2,1)} %get-tuple-element.107) | copy-start | bytes 1572868
  394.6 19.5 %copy-start.8 = (f32[64,512]{1,0:T(8,128)S(1)}, f32[64,512]{1,0:T(8,128)}, u32[]{:S(2)}) copy-start(f32[64,512]{1,0:T(8,128)} %get-tuple-element.53) | copy-start | bytes 393220

commit v3 on v2

--- a/solution.py
+++ b/solution.py
@@ -372,163 +372,242 @@
     return r * (gvec - unit * jnp.mean(gvec * unit, -1, keepdims=True))
 
 
-def k3_body(part, mid, cot, gain, out, gmid, ploc, rc, ry, send, recv, loc):
-    net = Net(send, recv, loc)
-    t, hi, c = net.t, net.hi, net.c
-    net.greet([net.sib()] + [net.flip(*f) for f in FLIP8])
-    rows = cot.shape[0]
-    cc, lc = scatter8_start(net, part, ploc, rc)
-    for cp in scatter8_send(net, cc, lc, ploc, rc, ry, rows):
-        cp.wait_recv()
-    step = 32
-
-    @pl.loop(0, rows // step)
-    def _(i):
-        sl = pl.ds(pl.multiple_of(i * step, step), step)
-        g = ploc[3, sl, :].astype(F32) + rc[3, sl, :].astype(F32)
-        for j in range(3):
-            g += ry[j, sl, :].astype(F32)
-        gm = cot[sl, :].astype(F32) + norm_back(mid[sl, :], g, gain[...])
-        gmid[sl, :] = gm
-        out[t, sl, :] = gm.astype(BF)
-
-    mine = out.at[t]
-    got = net.put(mine, mine, net.flip(0, 1))
-    tail = [net.put(mine, mine, net.sib())]
-    got.wait_recv()
-    blk = out.at[(1 - hi) * 2 + c]
-    tail.append(net.put(blk, blk, net.sib()))
-    for cp in tail:
-        cp.wait_recv()
-    net.finish()
-
-
-def k3(part, mid, cot, gain):
-    rows, d = cot.shape
-    return pl.pallas_call(
-        k3_body,
-        out_shape=[jax.ShapeDtypeStruct((4, rows, d), BF), jax.ShapeDtypeStruct((rows, d), F32)],
-        in_specs=[ANY, VM, VM, VM],
-        out_specs=[VM, VM],
-        scratch_shapes=[
-            pltpu.VMEM((4, rows, d), BF), pltpu.VMEM((4, rows, d), BF), pltpu.VMEM((3, rows, d), BF),
-        ] + sems(12, 4),
-        compiler_params=pltpu.CompilerParams(collective_id=3, has_side_effects=True, vmem_limit_bytes=40 << 20),
-        name="sum_normback_gather",
-    )(part, mid, cot, gain)
-
-
-def k4_body(
-    pg, pu, pd, po, pq, fpart, apart, mid, tok, gmid, gain,
-    og, ou, od, oo, oq, res, gtok,
-    lg, lu, ld, lo, lq, r1g, r1u, r1d, r1o, r1q, r2g, r2u, r2d, r2o, r2q, ryo, ryq,
-    ploc, rc, ry, aloc, arc, arh, send, recv, loc,
-):
-    net = Net(send, recv, loc)
-    a, z, x, hi, c = net.a, net.z, net.x, net.hi, net.c
-    net.greet(all_peers(net))
-    rows = tok.shape[0]
-    items = [
-        (pg, og, lg, r1g, r2g, None), (pu, ou, lu, r1u, r2u, None), (pd, od, ld, r1d, r2d, None),
-        (po, oo, lo, r1o, r2o, ryo), (pq, oq, lq, r1q, r2q, ryq),
-    ]
-    far, near = 1 - hi, hi
-    acc = [net.put(apart.at[h * 2 + (1 - c)], arc.at[i], net.sib()) for i, h in enumerate((far, near))]
-    alc = [net.copy(apart.at[h * 2 + c], aloc.at[i]) for i, h in enumerate((far, near))]
-    st1 = []
-    for p, o, l, r1, r2, _ in items:
-        lc = [net.copy(p.at[0, z], l.at[0]), net.copy(p.at[1, :, x], l.at[1])]
-        got = [[], []]
+class Scatter:
+    def __init__(self, net, part, r1, r2, loc=None):
+        self.net, self.part, self.r1, self.r2 = net, part, r1, r2
+        self.loc = loc
+
+    def stage_one(self):
+        net, p, r1 = self.net, self.part, self.r1
+        z, x = net.z, net.x
+        self.lc = None
+        if self.loc is not None:
+            self.lc = [net.copy(p.at[0, z], self.loc.at[0]), net.copy(p.at[1, :, x], self.loc.at[1])]
+        self.got = [[], []]
         for k, s in enumerate(ORDER):
             zz, xx = lax.rem(z + s, 4), lax.rem(x + s, 4)
-            got[0].append(net.put(p.at[0, zz], r1.at[0, k], net.zp(s)))
-            got[1].append(net.put(p.at[1, :, xx], r1.at[1, k], net.xp(s)))
-        st1.append((lc, got))
-    fcc, flc = scatter8_start(net, fpart, ploc, rc)
-    alc[0].wait()
+            self.got[0].append(net.put(p.at[0, zz], r1.at[0, k], net.zp(s)))
+            self.got[1].append(net.put(p.at[1, :, xx], r1.at[1, k], net.xp(s)))
+
+    def stage_two(self):
+        net, r1, r2 = self.net, self.r1, self.r2
+        self.nxt = []
+        for h in range(2):
+            if self.lc is not None:
+                self.lc[h].wait()
+            for cp in self.got[h]:
+                cp.wait_recv()
+            me = net.x if h == 0 else net.z
+            blocks = []
+            for b in range(4):
+                if self.loc is not None:
+                    mine = self.loc.at[h, b]
+                else:
+                    mine = self.part.at[0, net.z, b] if h == 0 else self.part.at[1, b, net.x]
+                dst = r1.at[h, 0, b]
+                add_to(dst, [mine] + [r1.at[h, k, b] for k in range(3)], 64)
+            self.nxt.append([
+                net.put(r1.at[h, 0, lax.rem(me + s, 4)], r2.at[h, k], net.xp(s) if h == 0 else net.zp(s))
+                for k, s in enumerate(ORDER)
+            ])
+
+    def stage_y(self, dst):
+        net, r1, r2 = self.net, self.r1, self.r2
+        for h in range(2):
+            for cp in self.nxt[h]:
+                cp.wait_recv()
+            me = net.x if h == 0 else net.z
+            add_to(r2.at[h, 0], [r1.at[h, 0, me]] + [r2.at[h, k] for k in range(3)], 64)
+        self.yc = net.put(r2.at[1 - net.a, 0], dst, net.flip(1, 0))
+
+
+def m3_body(names, *refs):
+    r = dict(zip(names, refs))
+    net = Net(r["send"], r["recv"], r["loc"])
+    a, z, x, t, hi, c = net.a, net.z, net.x, net.t, net.hi, net.c
+    net.greet(all_peers(net))
+    mid, cot, tok, gains = r["mid"], r["cot"], r["tok"], r["gains"]
+    rows, d = cot.shape
+    n = 4 * rows
+    step = 32
+    far, near = 1 - hi, hi
+    sib, chip = net.sib(), net.flip(0, 1)
+    bcc, blc = scatter8_start(net, r["fback"], r["bl"], r["bc"])
+    ffn = [Scatter(net, r["p" + k], r["r1" + k], r["r2" + k], r["l" + k]) for k in "gud"]
+    for sc in ffn:
+        sc.stage_one()
+    bgot = scatter8_send(net, bcc, blc, r["bl"], r["bc"], r["by"], rows)
+    bias = r["bias"]
+    bias[...] = jnp.where(
+        (r["seqc"][...] == r["seqr"][...]) & (r["blkc"][...] <= r["blkr"][...]), jnp.float32(0.0), jnp.float32(-1e30)
+    )
+    for cp in bgot:
+        cp.wait_recv()
+    gm, gmid, bl, bc, by = r["gm"], r["gmid"], r["bl"], r["bc"], r["by"]
+
+    @pl.loop(0, rows // step)
+    def _(i):
+        sl = pl.ds(pl.multiple_of(i * step, step), step)
+        g = bl[3, sl, :].astype(F32) + bc[3, sl, :].astype(F32)
+        for j in range(3):
+            g += by[j, sl, :].astype(F32)
+        m = cot[sl, :].astype(F32) + norm_back(mid[sl, :], g, gains[1:2, :])
+        gmid[sl, :] = m
+        gm[t, sl, :] = m.astype(BF)
+
+    mine = gm.at[t]
+    mf = net.put(mine, mine, chip)
+    ms = [net.put(mine, mine, sib)]
+    fcc, flc = scatter8_start(net, r["fout"], r["fl"], r["fc"])
+    fgot = scatter8_send(net, fcc, flc, r["fl"], r["fc"], r["fy"], rows)
+    mf.wait_recv()
+    theirs = gm.at[far * 2 + c]
+    ms.append(net.put(theirs, theirs, sib))
+    for cp in ms:
+        cp.wait_recv()
+    gatt, att, q, kv4, wq, wo = r["gatt"], r["att"], r["q"], r["kv4"], r["wq"], r["wo"]
+    for i in range(2):
+        w = wo[:, :, :, :, 256 * i : 256 * i + 256].reshape(d, 256)
+        gatt[:, 256 * i : 256 * i + 256] = dot(gm[...].reshape(n, d), w).astype(BF)
+    po, pq, xn, dqkv = r["po"], r["pq"], r["xn"], r["dqkv"]
+
+    @pl.loop(0, 8)
+    def _(i):
+        ln = pl.ds(pl.multiple_of(i * 256, 256), 256)
+        left = gm[:, :, ln].reshape(n, 256)
+        po[lax.div(i, 4), lax.rem(i, 4)] = dot(left, att[...], TN).reshape(4, 64, 512).astype(BF)
+
+    so = Scatter(net, po, r["r1o"], r["r2o"])
+    so.stage_one()
+    ak, av = r["ak"], r["av"]
+    ak[...] = jnp.zeros_like(ak)
+    av[...] = jnp.zeros_like(av)
+    cos, sin = r["cos"], r["sin"]
+    low = low_half((n, 128))
+    scale = 1.0 / math.sqrt(HD)
+
+    @pl.loop(0, 4)
+    def _(j):
+        ln = pl.ds(pl.multiple_of(j * 128, 128), 128)
+        qp, gp = q[:, ln], gatt[:, ln]
+        cv, ck, gq = [], [], None
+        for h in range(2):
+            s = dot(kv4[h], qp, NT) + bias[...]
+            e = jnp.exp(s - jnp.max(s, 0, keepdims=True))
+            p = e * (1.0 / jnp.sum(e, 0, keepdims=True))
+            pg = p * dot(kv4[2 + h], gp, NT)
+            graw = (pg - p * jnp.sum(pg, 0, keepdims=True)).astype(BF)
+            cv.append(dot(p.astype(BF), gp))
+            ck.append(dot(graw, qp))
+            term = dot(kv4[h], graw, TN)
+            gq = term if gq is None else gq + term
+        av[...] += jnp.where(low, cv[0], cv[1])
+        ak[...] += jnp.where(low, ck[0], ck[1])
+        dqkv[:, ln] = (rot_back(gq.T, cos[...], sin[...]) * scale).astype(BF)
+
+    tk = ak[...] + pltpu.roll(ak[...], 64, 1)
+    tv = av[...] + pltpu.roll(av[...], 64, 1)
+    dqkv[:, 512:640] = jnp.where(low, rot_back(tk, cos[...], sin[...]), tv).astype(BF)
+
+    @pl.loop(0, 8)
+    def _(i):
+        ln = pl.ds(pl.multiple_of(i * 256, 256), 256)
+        pq[lax.div(i, 4), lax.rem(i, 4)] = dot(xn[:, ln], dqkv[...], TN).reshape(4, 64, 640).astype(BF)
+
+    sq = Scatter(net, pq, r["r1q"], r["r2q"])
+    sq.stage_one()
+    ap, arc, arh = r["ap"], r["arc"], r["arh"]
+    for i in range(4):
+        w = wq[i // 2, 2 * (i % 2) : 2 * (i % 2) + 2].reshape(512, 640)
+        ap[:, :, 512 * i : 512 * i + 512] = dot(dqkv[...], w, NT).reshape(4, rows, 512).astype(BF)
+    acc = [net.put(ap.at[h * 2 + (1 - c)], arc.at[i], sib) for i, h in enumerate((far, near))]
     acc[0].wait_recv()
-    add_to(aloc.at[0], [aloc.at[0], arc.at[0]], rows)
-    ach = net.put(aloc.at[0], arh, net.flip(0, 1))
-    fgot = scatter8_send(net, fcc, flc, ploc, rc, ry, rows)
-    alc[1].wait()
+    af = ap.at[far * 2 + c]
+    add_to(af, [af, arc.at[0]], rows)
+    ach = net.put(af, arh, chip)
+    for sc in ffn:
+        sc.stage_two()
+    so.stage_two()
+    for cp in fgot:
+        cp.wait_recv()
+    fl, fc, fy, res, gtok = r["fl"], r["fc"], r["fy"], r["res"], r["gtok"]
+
+    @pl.loop(0, rows // step)
+    def _(i):
+        sl = pl.ds(pl.multiple_of(i * step, step), step)
+        g = fl[3, sl, :].astype(F32) + fc[3, sl, :].astype(F32)
+        for j in range(3):
+            g += fy[j, sl, :].astype(F32)
+        res[sl, :] = (mid[sl, :] + g).astype(BF)
+
+    sq.stage_two()
     acc[1].wait_recv()
     ach.wait_recv()
-    step = 32
+    an = ap.at[near * 2 + c]
 
     @pl.loop(0, rows // step)
     def _(i):
         sl = pl.ds(pl.multiple_of(i * step, step), step)
-        g = aloc[1, sl, :].astype(F32) + arc[1, sl, :].astype(F32) + arh[sl, :].astype(F32)
-        gtok[sl, :] = (gmid[sl, :] + norm_back(tok[sl, :].astype(F32), g, gain[...])).astype(BF)
-
-    for cp in fgot:
-        cp.wait_recv()
-
-    @pl.loop(0, rows // step)
-    def _(i):
-        sl = pl.ds(pl.multiple_of(i * step, step), step)
-        g = ploc[3, sl, :].astype(F32) + rc[3, sl, :].astype(F32)
-        for j in range(3):
-            g += ry[j, sl, :].astype(F32)
-        res[sl, :] = (mid[sl, :] + g).astype(BF)
-
-    st2 = []
-    for (p, o, l, r1, r2, _), (lc, got) in zip(items, st1):
-        nxt = []
-        for h in range(2):
-            lc[h].wait()
-            for cp in got[h]:
-                cp.wait_recv()
-            for b in range(4):
-                add_to(l.at[h, b], [l.at[h, b]] + [r1.at[h, k, b] for k in range(3)], 64)
-            me = x if h == 0 else z
-            nxt.append([
-                net.put(l.at[h, lax.rem(me + s, 4)], r2.at[h, k], net.xp(s) if h == 0 else net.zp(s))
-                for k, s in enumerate(ORDER)
-            ])
-        st2.append(nxt)
-    st3 = []
-    for (p, o, l, r1, r2, r3), nxt in zip(items, st2):
-        for h in range(2):
-            for cp in nxt[h]:
-                cp.wait_recv()
-            me = x if h == 0 else z
-            add_to(r2.at[h, 0], [l.at[h, me]] + [r2.at[h, k] for k in range(3)], 64)
-        if r3 is None:
-            st3.append(net.put(r2.at[1 - a, 0], o.at[a], net.flip(1, 0)))
-            o[a, :, :] = r2[a, 0]
-        else:
-            st3.append(net.put(r2.at[1 - a, 0], r3, net.flip(1, 0)))
-    for (p, o, l, r1, r2, r3), cp in zip(items, st3):
-        cp.wait_recv()
-        if r3 is not None:
-            add_to(o, [r2.at[a, 0], r3], 64)
+        g = an[sl, :].astype(F32) + arc[1, sl, :].astype(F32) + arh[sl, :].astype(F32)
+        gtok[sl, :] = (gmid[sl, :] + norm_back(tok[sl, :].astype(F32), g, gains[0:1, :])).astype(BF)
+
+    outs = [r["og"], r["ou"], r["od"]]
+    for sc, o in zip(ffn, outs):
+        sc.stage_y(o.at[a])
+        o[a] = sc.r2[a, 0]
+    so.stage_y(r["yo"])
+    sq.stage_y(r["yq"])
+    for sc in ffn:
+        sc.yc.wait_recv()
+    for sc, o, y in ((so, r["oo"], r["yo"]), (sq, r["oq"], r["yq"])):
+        sc.yc.wait_recv()
+        add_to(o, [sc.r2.at[a, 0], y], 64)
     net.finish()
 
 
-def k4(grads, fpart, apart, mid, tok, gmid, gain):
+def m3(fback, fout, pg, pu, pd, mid, cot, tok, gains, xn, q, kv4, att, wq, wo, cos, sin, seq, blk):
     rows, d = tok.shape
-    widths = [g.shape[-1] for g in grads]
-    outs = [jax.ShapeDtypeStruct((2, 64, w), BF) for w in widths[:3]]
-    outs += [jax.ShapeDtypeStruct((64, w), F32) for w in widths[3:]]
-    outs += [jax.ShapeDtypeStruct((rows, d), BF)] * 2
-    scratch = [pltpu.VMEM((2, 4, 64, w), BF) for w in widths]
-    scratch += [pltpu.VMEM((2, 3, 4, 64, w), BF) for w in widths]
-    scratch += [pltpu.VMEM((2, 3, 64, w), BF) for w in widths]
-    scratch += [pltpu.VMEM((64, w), BF) for w in widths[3:]]
-    scratch += [
-        pltpu.VMEM((4, rows, d), BF), pltpu.VMEM((4, rows, d), BF), pltpu.VMEM((3, rows, d), BF),
-        pltpu.VMEM((2, rows, d), BF), pltpu.VMEM((2, rows, d), BF), pltpu.VMEM((rows, d), BF),
-    ]
-    return pl.pallas_call(
-        k4_body,
-        out_shape=outs,
-        in_specs=[ANY] * 7 + [VM] * 4,
-        out_specs=[VM] * 7,
-        scratch_shapes=scratch + sems(96, 24),
-        compiler_params=pltpu.CompilerParams(collective_id=4, has_side_effects=True, vmem_limit_bytes=56 << 20),
-        name="scatter_all",
-    )(*grads, fpart, apart, mid, tok, gmid, gain)
+    n = 4 * rows
+    sd = jax.ShapeDtypeStruct
+    v = pltpu.VMEM
+    col = lambda u: u.reshape(n, 1)
+    row = lambda u: u.reshape(1, n)
+    ins = dict(
+        fback=fback, fout=fout, pg=pg, pu=pu, pd=pd,
+        mid=mid, cot=cot, tok=tok, gains=gains, xn=xn, q=q, kv4=kv4, att=att, wq=wq, wo=wo, cos=cos, sin=sin,
+        seqr=row(seq), seqc=col(seq), blkr=row(blk), blkc=col(blk),
+    )
+    w3 = (2, 64, FH)
+    outs = dict(
+        og=sd(w3, BF), ou=sd(w3, BF), od=sd(w3, BF), oo=sd((64, 512), F32), oq=sd((64, 640), F32),
+        res=sd((rows, d), BF), gtok=sd((rows, d), BF),
+    )
+    scr = dict(
+        bl=v((4, rows, d), BF), bc=v((4, rows, d), BF), by=v((3, rows, d), BF),
+        fl=v((4, rows, d), BF), fc=v((4, rows, d), BF), fy=v((3, rows, d), BF),
+        gm=v((4, rows, d), BF), gmid=v((rows, d), F32), bias=v((n, n), F32), gatt=v((n, 512), BF),
+        dqkv=v((n, 640), BF), ak=v((n, 128), F32), av=v((n, 128), F32),
+        po=v((2, 4, 4, 64, 512), BF), pq=v((2, 4, 4, 64, 640), BF),
+        ap=v((4, rows, d), BF), arc=v((2, rows, d), BF), arh=v((rows, d), BF),
+        yo=v((64, 512), BF), yq=v((64, 640), BF),
+    )
+    for k, w in (("g", FH), ("u", FH), ("d", FH), ("o", 512), ("q", 640)):
+        scr["r1" + k] = v((2, 3, 4, 64, w), BF)
+        scr["r2" + k] = v((2, 3, 64, w), BF)
+    for k in "gud":
+        scr["l" + k] = v((2, 4, 64, FH), BF)
+    sem = sems(100, 24)
+    names = list(ins) + list(outs) + list(scr) + ["send", "recv", "loc"]
+    got = pl.pallas_call(
+        functools.partial(m3_body, names),
+        out_shape=list(outs.values()),
+        in_specs=[ANY] * 5 + [VM] * (len(ins) - 5),
+        out_specs=[VM] * len(outs),
+        scratch_shapes=list(scr.values()) + sem,
+        compiler_params=pltpu.CompilerParams(collective_id=3, has_side_effects=True, vmem_limit_bytes=62 << 20),
+        name="attention_backward",
+    )(*ins.values())
+    return dict(zip(outs, got))
 
 
 def rope_tables(places, head_width):
@@ -539,25 +618,8 @@
     return (jnp.cos(angles), jnp.sin(angles))
 
 
-def rotate(values, cosine, sine_rows):
-    half_width = values.shape[-1] // 2
-    turned = jnp.concatenate([-values[..., half_width:], values[..., :half_width]], -1)
-    return values * cosine[:, None, :] + turned * sine_rows[:, None, :]
-
-
-def rotate_back(grad_rows, cosine, sine_rows):
-    half_width = grad_rows.shape[-1] // 2
-    scaled = grad_rows * sine_rows[:, None, :]
-    turned = jnp.concatenate([scaled[..., half_width:], -scaled[..., :half_width]], -1)
-    return grad_rows * cosine[:, None, :] + turned
-
-
 def mm(l, r, dims=((1,), (0,))):
     return lax.dot_general(l, r, (dims, ((), ())), preferred_element_type=F32)
-
-
-def ein(eq, l, r):
-    return jnp.einsum(eq, l, r, preferred_element_type=F32)
 
 
 def halves(w):
@@ -573,7 +635,6 @@
     n = seq_ids.shape[0]
     ff = w_gate.shape[1]
     hq = w_query.shape[1] // HD
-    scale = 1.0 / math.sqrt(HD)
     wq = jnp.concatenate([w_query, w_key, w_value], 1)
     wo = w_out.T
     gn = jnp.pad(jnp.stack([attn_gain, ffn_gain]).astype(F32), ((0, 6), (0, 64)))
@@ -587,19 +648,7 @@
         cos2, sin2, seq_ids, block_ids,
     )
     cot = cot.reshape(2 * n, d)
-    wqkv = wqkv.reshape(d, -1)
-    wot = wot.reshape(d, -1)
     wg, wu, wdt = (w.reshape(d, FH) for w in (wg, wu, wdt))
-    g1, g2 = gains[0:1], gains[1:2]
-    k, v = kv4[0, :, :HD], kv4[2, :, :HD]
-    q = (q * 8).reshape(n, hq, HD)
-    allowed = (seq_ids[:, None] == seq_ids[None, :]) & (block_ids[None, :] <= block_ids[:, None])
-    s = jnp.where(allowed[None], ein("thd,sd->hts", q, k) * scale, -1e30)
-    top = jnp.max(s, -1, keepdims=True)
-    e = jnp.exp(s - top)
-    total = jnp.sum(e, -1, keepdims=True)
-    p = e / total
-    plow = p.astype(BF)
     xf = xf.reshape(2 * n, d)
     gate = mm(xf, wg)
     up = mm(xf, wu)
@@ -609,33 +658,17 @@
     gh = mm(cot, wdt)
     dgate = (gh * up * (sig * (1.0 + gate * (1.0 - sig)))).astype(BF)
     dup = (gh * silu).astype(BF)
-    fback = (mm(dgate, wg, NT) + mm(dup, wu, NT)).astype(BF)
-    gm_all, gmid = k3(fback.reshape(2, 4, rows, d), mid, cotangent, g2)
-    gm_all = gm_all.reshape(n, d)
-    fout = mm(hid, wdt, NT).astype(BF)
+    fback = (mm(dgate, wg, NT) + mm(dup, wu, NT)).astype(BF).reshape(2, 4, rows, d)
+    fout = mm(hid, wdt, NT).astype(BF).reshape(2, 4, rows, d)
     pd = mm(cot, hid, TN).astype(BF)
     pg = mm(xf, dgate, TN).astype(BF)
     pu = mm(xf, dup, TN).astype(BF)
-
-    gatt = mm(gm_all, wot).astype(BF)
-    po = mm(gm_all, att, TN).astype(BF)
-    gatt3 = gatt.reshape(n, hq, HD)
-    gp = ein("thd,sd->hts", gatt3, v)
-    gv = ein("hts,thd->sd", plow, gatt3).astype(BF)
-    inner = jnp.sum(p * gp, -1, keepdims=True)
-    graw = (p * (gp - inner) * scale).astype(BF)
-    gq = ein("hts,sd->thd", graw, k)
-    gk = ein("hts,thd->sd", graw, q)
-    dq = rotate_back(gq, cosine, sine).reshape(n, hq * HD).astype(BF)
-    dk = rotate_back(gk[:, None], cosine, sine)[:, 0].astype(BF)
-    dqkv = jnp.concatenate([dq, dk, gv], 1)
-    aback = mm(dqkv, wqkv, NT).astype(BF)
-    pq = mm(xn, dqkv, TN).astype(BF)
-
-    grads = [w.reshape(2, 4, 4, 64, w.shape[1]) for w in (pg, pu, pd, po, pq)]
-    og, ou, od, oo, oq, res, gtok = k4(
-        grads, fout.reshape(2, 4, rows, d), aback.reshape(4, rows, d), mid, tokens_in, gmid, g1
-    )
+    pg, pu, pd = (w.reshape(2, 4, 4, 64, FH) for w in (pg, pu, pd))
+    out = m3(
+        fback, fout, pg, pu, pd, mid, cotangent, tokens_in, gains, xn, q, kv4, att, wqkv, wot,
+        cos2, sin2, seq_ids, block_ids,
+    )
+    og, ou, od, oo, oq, res, gtok = (out[k] for k in ("og", "ou", "od", "oo", "oq", "res", "gtok"))
 
     def join(o):
         return jnp.concatenate([o[0], o[1]], 1)[:, :ff].astype(F32)

time: 423 us -> 315 us (0.74); the launches traced: 415 us -> 314 us
  matrix products: 94.1 us -> 43 us
  Pallas kernels: 280 us -> 238 us
    pallas_call x2 -> x1, Pallas kernels: 157 us -> 115 us  [m3(): pl.pallas_call(functools.partial(m3_body, names), out_shape=list(outs.val...]
    dot_general x4 -> x0, matrix products: 33.5 us -> none  [ein(): return jnp.einsum(eq, l, r, preferred_element_type=F32)]
    dot_general x13 -> x9, matrix products: 55.7 us -> 43 us  [mm(): return lax.dot_general(l, r, (dims, ((), ())), preferred_element_type=F32)]
    sub x1 -> x0, matrix products: 4.92 us -> none  [per_device(): e = jnp.exp(s - top)]
where the time goes in v3:
time: 315 us; the launch traced here: 314 us
  Pallas kernels  238 us (76%)
  matrix products  43 us (14%)
  local copies, waits for them, and re-layouts  13.5 us (4%)
  other arithmetic  11.3 us (4%)
  blocking collectives  8.04 us (3%)
    pallas_call x1, Pallas kernels, m1(): pl.pallas_call(m1_body, out_shape=[sd((2, 4, rows, d), BF), sd((rows, d),...  123 us
    pallas_call x1, Pallas kernels, m3(): pl.pallas_call(functools.partial(m3_body, names), out_shape=list(outs.val...  115 us
    dot_general x9, matrix products, mm(): return lax.dot_general(l, r, (dims, ((), ())), preferred_element_type=F32)  43 us
    psum x1, blocking collectives, per_device(): dg1, dg2 = lax.psum((dg1, dg2), 'tensor')  8.04 us

profile of v3, /device:TPU:1, one launch (start us, length us, event | category | flops | bytes accessed | tf_op | source)
XLA Modules:
  0.0 314.4 jit_solution(7131268522659180474)
XLA Ops:
  2.0 1.3 pad_select_fusion.gn
  3.4 1.6 pad_maximum_fusion.9.wq
  5.0 0.9 slice_bitcast_fusion
  6.6 0.9 slice_bitcast_fusion.8
  7.6 1.0 slice_bitcast_fusion.7
  8.5 0.8 pad_maximum_fusion.3
  9.4 1.5 copy.26.blkc.refs_20_
  11.0 0.9 copy.25.seqc.refs_18_
  11.8 1.1 fusion.1
  13.1 1.1 pad_maximum_fusion.1
  14.2 122.6 %attention_forward.1 = (bf16[2,4,128,2048]{3,2,1,0:T(8,128)(2,1)}, f32[128,2048]{1,0:T(8,128)}, bf16[512,2048]{1,0:T(8,128)(2,1)}, bf16[512,512]{1,0:T(8,128)(2,...) custom-call(bf16[128,2048]{1,0:T(8,128)(2,1)} %refs_7_.1, ...), custom_call_target="tpu_custom_call" | custom-call | tf_op jit(solution)/shard_map/attention_forward/pallas_call | solution.py:329
  136.8 6.5 %fusion.18 = f32[1024,768]{1,0:T(8,128)S(1)} fusion(bf16[1024,2048]{1,0:T(8,128)(2,1)} %bitcast.87, bf16[2048,768]{1,0:T(8,128)(2,1)} %bitcast.93), kind=kOutput, calls=%fused_computation.58 | convolution fusion | flops 3221225472 | bytes 10485760 | tf_op jit(solution)/shard_map/dot_general | solution.py:622
  143.3 3.4 %fusion.19 = f32[1024,768]{1,0:T(8,128)S(1)} fusion(bf16[1024,2048]{1,0:T(8,128)(2,1)S(1)} %bitcast.83, bf16[2048,768]{1,0:T(8,128)(2,1)S(1)} %bitcast.91), kind=kOutput, calls=%fused_computation.59 | convolution fusion | flops 3221225472 | bytes 10485760 | tf_op jit(solution)/shard_map/dot_general | solution.py:622
  146.8 4.5 %multiply_convert_fusion = (bf16[1024,768]{1,0:T(8,128)(2,1)S(1)}, bf16[1024,768]{1,0:T(8,128)(2,1)S(1)}, bf16[1024,768]{1,0:T(8,128)(2,1)S(1)}) fusion(f32[1024,768]{1,0:T(8,128)S(1)} %fusion.19, f32[1024,768]{1,0:T(8,128)S(1)} %fusion.18, bf16[1024,2048]{1,0:T(8,128)(2,1)S(1)} %bitcast.84, bf16[2048,768]{1,0:T(8,128)(2,1)S(1)} %bitcast.89), kind=kOutput, calls=%fused_computation.5 | convolution fusion | flops 3233021952 | bytes 18350080 | tf_op jit(solution)/shard_map/dot_general | solution.py:622
  151.3 5.0 %convolution_convert_fusion.1 = bf16[2048,768]{1,0:T(8,128)(2,1)} fusion(bf16[1024,2048]{1,0:T(8,128)(2,1)S(1)} %bitcast.88, bf16[1024,768]{1,0:T(8,128)(2,1)S(1)} %get-tuple-element.56), kind=kOutput, calls=%fused_computation.2 | convolution fusion | flops 3222798336 | bytes 8912896 | tf_op jit(solution)/shard_map/dot_general | solution.py:622
  156.3 5.0 %convolution_convert_fusion = bf16[1024,2048]{1,0:T(8,128)(2,1)} fusion(bf16[1024,768]{1,0:T(8,128)(2,1)S(1)} %get-tuple-element.56, bf16[2048,768]{1,0:T(8,128)(2,1)S(1)} %bitcast.94), kind=kOutput, calls=%fused_computation.1 | convolution fusion | flops 3223322624 | bytes 8912896 | tf_op jit(solution)/shard_map/dot_general | solution.py:622
  161.4 5.0 %convolution_convert_fusion.3 = bf16[2048,768]{1,0:T(8,128)(2,1)} fusion(bf16[1024,2048]{1,0:T(8,128)(2,1)S(1)} %bitcast.85, bf16[1024,768]{1,0:T(8,128)(2,1)S(1)} %get-tuple-element.57), kind=kOutput, calls=%fused_computation.4 | convolution fusion | flops 3222798336 | bytes 8912896 | tf_op jit(solution)/shard_map/dot_general | solution.py:622
  166.4 5.0 %convolution_convert_fusion.2 = bf16[2048,768]{1,0:T(8,128)(2,1)} fusion(bf16[1024,2048]{1,0:T(8,128)(2,1)S(1)} %bitcast.86, bf16[1024,768]{1,0:T(8,128)(2,1)S(1)} %get-tuple-element.58), kind=kOutput, calls=%fused_computation.3 | convolution fusion | flops 3222798336 | bytes 8912896 | tf_op jit(solution)/shard_map/dot_general | solution.py:622
  171.4 3.4 %fusion.20 = f32[1024,2048]{1,0:T(8,128)S(1)} fusion(bf16[1024,768]{1,0:T(8,128)(2,1)S(1)} %get-tuple-element.57, bf16[2048,768]{1,0:T(8,128)(2,1)S(1)} %bitcast.92), kind=kOutput, calls=%fused_computation.60 | convolution fusion | flops 3221225472 | bytes 13107200 | tf_op jit(solution)/shard_map/dot_general | solution.py:622
  174.9 5.1 %add_convert_fusion = bf16[1024,2048]{1,0:T(8,128)(2,1)} fusion(f32[1024,2048]{1,0:T(8,128)S(1)} %fusion.20, bf16[1024,768]{1,0:T(8,128)(2,1)S(1)} %get-tuple-element.58, bf16[2048,768]{1,0:T(8,128)(2,1)S(1)} %bitcast.90), kind=kOutput, calls=%fused_computation | convolution fusion | flops 3225419776 | bytes 17301504 | tf_op jit(solution)/shard_map/dot_general | solution.py:622
  180.0 115.0 %attention_backward.1 = (bf16[2,64,768]{2,1,0:T(8,128)(2,1)}, bf16[2,64,768]{2,1,0:T(8,128)(2,1)}, bf16[2,64,768]{2,1,0:T(8,128)(2,1)}, f32[64,512]{1,0:T(8,128)...) custom-call(bf16[2,4,128,2048]{3,2,1,0:T(8,128)(2,1)} %bitcast.65, ...), custom_call_target="tpu_custom_call" | custom-call | tf_op jit(solution)/shard_map/attention_backward/pallas_call | solution.py:601
  295.1 1.2 multiply_reduce_fusion
  296.3 1.5 fusion.17
  297.8 1.6 slice.84
  299.4 1.0 slice_bitcast_fusion.6
  300.3 1.0 slice_bitcast_fusion.4
  301.3 1.0 slice_bitcast_fusion.2
  302.3 0.8 convert_bitcast_fusion
  303.0 1.0 add_reduce_fusion
  304.1 8.0 %all-reduce.5 = (f32[64]{0:T(128)}, f32[64]{0:T(128)}) all-reduce(f32[64]{0:T(128)S(1)} %convert_divide_fusion.1, f32[64]{0:T(128)S(1)} %convert_divide_fusion), channel_id=1, replica_groups=mesh['dp'=32,'tensor'=4] {'tensor'}, use_global_device_ids=true, to_apply=%region_1.2 | all-reduce | flops 128 | bytes 1024 | tf_op jit(solution)/shard_map/psum | solution.py:679
  312.1 0.8 copy.32
  312.9 0.8 copy.33
  (41 shorter events, 3.1 us)
Async XLA Ops:
  0.6 10.3 %copy-start.8 = (s32[512]{0:T(512)S(1)}, s32[512]{0:T(512)}, u32[]{:S(2)}) copy-start(s32[512]{0:T(512)} %param.16) | copy-start | bytes 6148
  136.8 6.5 %copy-start.11 = (bf16[2,4,128,2048]{3,2,1,0:T(8,128)(2,1)S(1)}, bf16[2,4,128,2048]{3,2,1,0:T(8,128)(2,1)}, u32[]{:S(2)}) copy-start(bf16[2,4,128,2048]{3,2,1,0:T(8,128)(2,1)} %get-tuple-element.33) | copy-start | bytes 12582916
  136.8 6.5 %copy-start.14 = (bf16[2,4,4,64,768]{4,3,2,1,0:T(8,128)(2,1)S(1)}, bf16[2,4,4,64,768]{4,3,2,1,0:T(8,128)(2,1)}, u32[]{:S(2)}) copy-start(bf16[2,4,4,64,768]{4,3,2,1,0:T(8,128)(2,1)} %get-tuple-element.35) | copy-start | bytes 9437188
  143.3 3.4 %copy-start.13 = (bf16[2,4,4,64,768]{4,3,2,1,0:T(8,128)(2,1)S(1)}, bf16[2,4,4,64,768]{4,3,2,1,0:T(8,128)(2,1)}, u32[]{:S(2)}) copy-start(bf16[2,4,4,64,768]{4,3,2,1,0:T(8,128)(2,1)} %get-tuple-element.34) | copy-start | bytes 9437188
  146.7 4.6 %copy-start.12 = (bf16[2,4,128,2048]{3,2,1,0:T(8,128)(2,1)S(1)}, bf16[2,4,128,2048]{3,2,1,0:T(8,128)(2,1)}, u32[]{:S(2)}) copy-start(bf16[2,4,128,2048]{3,2,1,0:T(8,128)(2,1)} %get-tuple-element.31) | copy-start | bytes 12582916
  151.3 5.0 %copy-start.15 = (bf16[2,4,4,64,768]{4,3,2,1,0:T(8,128)(2,1)S(1)}, bf16[2,4,4,64,768]{4,3,2,1,0:T(8,128)(2,1)}, u32[]{:S(2)}) copy-start(bf16[2,4,4,64,768]{4,3,2,1,0:T(8,128)(2,1)} %get-tuple-element.32) | copy-start | bytes 9437188
  179.9 115.1 %copy-start.4 = (bf16[64,512]{1,0:T(8,128)(2,1)S(1)}, bf16[64,512]{1,0:T(8,128)(2,1)}, u32[]{:S(2)}) copy-start(bf16[64,512]{1,0:T(8,128)(2,1)} %param.21) | copy-start | bytes 196612
  179.9 115.1 %copy-start.6 = (bf16[64,64]{1,0:T(8,128)(2,1)S(1)}, bf16[64,64]{1,0:T(8,128)(2,1)}, u32[]{:S(2)}) copy-start(bf16[64,64]{1,0:T(8,128)(2,1)} %param.23) | copy-start | bytes 24580
  179.9 115.1 %copy-start.7 = (bf16[64,64]{1,0:T(8,128)(2,1)S(1)}, bf16[64,64]{1,0:T(8,128)(2,1)}, u32[]{:S(2)}) copy-start(bf16[64,64]{1,0:T(8,128)(2,1)} %param.22) | copy-start | bytes 24580
  179.9 116.3 %copy-start.9 = (bf16[64]{0:T(256)(128)(2,1)S(1)}, bf16[64]{0:T(256)(128)(2,1)}, u32[]{:S(2)}) copy-start(bf16[64]{0:T(256)(128)(2,1)} %param.19) | copy-start | bytes 388
  179.9 123.1 %copy-start = (bf16[64,1408]{1,0:T(8,128)(2,1)S(1)}, bf16[64,1408]{1,0:T(8,128)(2,1)}, u32[]{:S(2)}) copy-start(bf16[64,1408]{1,0:T(8,128)(2,1)} %param.25) | copy-start | bytes 540676
  179.9 123.1 %copy-start.1 = (bf16[64,1408]{1,0:T(8,128)(2,1)S(1)}, bf16[64,1408]{1,0:T(8,128)(2,1)}, u32[]{:S(2)}) copy-start(bf16[64,1408]{1,0:T(8,128)(2,1)} %param.26) | copy-start | bytes 540676
  295.0 9.1 %copy-start.10 = (bf16[64]{0:T(256)(128)(2,1)S(1)}, bf16[64]{0:T(256)(128)(2,1)}, u32[]{:S(2)}) copy-start(bf16[64]{0:T(256)(128)(2,1)} %param.20) | copy-start | bytes 388
  295.0 17.1 %copy-start.3 = (bf16[128,2048]{1,0:T(8,128)(2,1)S(1)}, bf16[128,2048]{1,0:T(8,128)(2,1)}, u32[]{:S(2)}) copy-start(bf16[128,2048]{1,0:T(8,128)(2,1)} %get-tuple-element.92) | copy-start | bytes 1572868
  295.0 17.9 %copy-start.2 = (bf16[128,2048]{1,0:T(8,128)(2,1)S(1)}, bf16[128,2048]{1,0:T(8,128)(2,1)}, u32[]{:S(2)}) copy-start(bf16[128,2048]{1,0:T(8,128)(2,1)} %get-tuple-element.93) | copy-start | bytes 1572868
  295.0 18.7 %copy-start.5 = (f32[64,512]{1,0:T(8,128)S(1)}, f32[64,512]{1,0:T(8,128)}, u32[]{:S(2)}) copy-start(f32[64,512]{1,0:T(8,128)} %get-tuple-element.49) | copy-start | bytes 393220

commit v4 on v3

--- a/solution.py
+++ b/solution.py
@@ -3,6 +3,7 @@
 
 import jax
 import jax.numpy as jnp
+import numpy as np
 from jax import lax
 from jax.experimental import pallas as pl
 from jax.experimental.pallas import tpu as pltpu
@@ -56,11 +57,17 @@
     def sib(self):
         return self.dev(c=1 - self.c)
 
-    def greet(self, peers):
+    def hello(self, peers):
         bar = pltpu.get_barrier_semaphore()
         for p in peers:
             pl.semaphore_signal(bar, inc=1, device_id=p, device_id_type=MESH)
-        pl.semaphore_wait(bar, len(peers))
+
+    def met(self, peers):
+        pl.semaphore_wait(pltpu.get_barrier_semaphore(), len(peers))
+
+    def greet(self, peers):
+        self.hello(peers)
+        self.met(peers)
 
     def put(self, src, dst, dev):
         i = self.n
@@ -80,6 +87,9 @@
         cp.start()
         return cp
 
+    def drop(self, cp):
+        self.sends = [s for s in self.sends if s is not cp]
+
     def finish(self):
         for cp in self.sends:
             cp.wait_send()
@@ -173,26 +183,59 @@
         for cp in self.st:
             cp.wait_recv()
         z, x = net.z, net.x
+        self.near = [
+            (net.put(dst.at[0, z], dst.at[0, z], net.zp(s)), net.put(dst.at[1, :, x], dst.at[1, :, x], net.xp(s)))
+            for s in (1, 3)
+        ]
+
+    def forward(self):
+        net, dst = self.net, self.dst
         self.last = []
-        for s in ORDER:
-            self.last.append(net.put(dst.at[0, z], dst.at[0, z], net.zp(s)))
-            self.last.append(net.put(dst.at[1, :, x], dst.at[1, :, x], net.xp(s)))
+        for (cz, cx), s, lo in zip(self.near, (1, 3), (0, 2)):
+            cz.wait_recv()
+            blk = dst.at[0, lax.rem(net.z + 4 - s, 4), lo : lo + 2]
+            self.last.append(net.put(blk, blk, net.zp(s)))
+            cx.wait_recv()
+            blk = dst.at[1, lo : lo + 2, lax.rem(net.x + 4 - s, 4)]
+            self.last.append(net.put(blk, blk, net.xp(s)))
 
     def done(self):
         for cp in self.last:
             cp.wait_recv()
 
 
+def pack_halves(dst, w):
+    rest = w.shape[1] - FH
+    dst[0] = w[:, :FH]
+    dst[1, :, :rest] = w[:, FH:]
+    dst[1, :, rest:] = jnp.zeros((w.shape[0], FH - rest), BF)
+
+
+def column(row, n):
+    return jnp.broadcast_to(row, (128, n)).T
+
+
 def m1_body(
-    tok, cot, wq, wo, wg, wu, wd, gn, cos, sin, seqr, seqc, blkr, blkc,
-    xf, mid, xn, q, kv4, att, gains, aq, ao, cot_all, ag, au, ad,
-    tall, an, bias, ones2, kvf, part, rc, rh, send, recv, loc,
+    tok, cot, w_q, w_k, w_v, wo, w_g, w_u, w_d, g_a, g_f, freq, seqr, blkr, posr,
+    xf, mid, xn, q, kv4, att, gains, aq, ao, cos, sin, bias_t, cot_all, ag, au, ad,
+    wq, wf, gn, tall, an, bias, ones2, part, rc, rh, send, recv, loc,
 ):
     net = Net(send, recv, loc)
     a, z, x, t, hi, c = net.a, net.z, net.x, net.t, net.hi, net.c
     rows, d = tok.shape
     n = 4 * rows
-    net.greet(all_peers(net))
+    nq = w_q.shape[1]
+    net.hello(all_peers(net))
+    lane = lax.broadcasted_iota(jnp.int32, (1, 128), 1)
+    here = lax.div(lane, HD) == lax.rem(x, 2)
+    gn[...] = jnp.zeros_like(gn)
+    for i, g in enumerate((g_a, g_f)):
+        g = g[...].astype(F32)
+        gn[i : i + 1, :] = jnp.where(here, jnp.concatenate([g, g], 1), 0.0)
+    wq[:, :nq] = w_q[...]
+    wq[:, nq : nq + HD] = w_k[...]
+    wq[:, nq + HD :] = w_v[...]
+    net.met(all_peers(net))
     far, near = 1 - hi, hi
     tt = far * 2 + c
     sib, chip = net.sib(), net.flip(0, 1)
@@ -200,19 +243,23 @@
     tf = net.put(tok, tall.at[t], chip)
     ts = [net.put(tok, tall.at[t], sib)]
     gg, gq, go = Gather(net, gn, an, False), Gather(net, wq, aq, False), Gather(net, wo, ao, False)
-    ffn = [Gather(net, w, o, True) for w, o in ((wg, ag), (wu, au), (wd, ad))]
     for g in (gg, gq, go):
         g.over_y()
         g.local()
         g.stage_own()
+    cl = net.copy(cot, cot_all.at[a, t])
+    for i, w in enumerate((w_g, w_u, w_d)):
+        pack_halves(wf.at[i], w)
+    ffn = [Gather(net, wf.at[i], o, True) for i, o in enumerate((ag, au, ad))]
     for g in ffn:
         g.local()
-    cl = net.copy(cot, cot_all.at[a, t])
-    bias[...] = jnp.where(
-        (seqc[...] == seqr[...]) & (blkr[...] <= blkc[...]), jnp.float32(0.0), jnp.float32(-1e30)
-    )
     for g in (gg, gq, go):
         g.stage_other()
+    seq, blk = seqr[...].astype(F32), blkr[...].astype(F32)
+    same = column(seq, n)[:, :1] == seq
+    blkc = column(blk, n)[:, :1]
+    bias[...] = jnp.where(same & (blk <= blkc), jnp.float32(0.0), jnp.float32(-1e30))
+    bias_t[...] = jnp.where(same & (blkc <= blk), jnp.float32(0.0), jnp.float32(-1e30))
     for g in (gg, gq, go):
         g.stage_two()
     tf.wait_recv()
@@ -221,9 +268,15 @@
     cs = [net.put(cot, cot_all.at[a, t], sib)]
     for g in ffn:
         g.over_y()
+    angles = column(posr[...].astype(F32), n) * freq[...]
+    cos[...] = jnp.cos(angles)
+    sine = jnp.sin(angles)
+    sin[...] = jnp.where(first_quarter(sine.shape), -sine, sine)
     tl.wait()
     for cp in ts:
         cp.wait_recv()
+    gg.forward()
+    gq.forward()
     gg.done()
     for i in range(16):
         k = 2 * i
@@ -237,6 +290,7 @@
         u = tall[b, pl.ds(pl.multiple_of(lax.rem(i, rows // step) * step, step), step), :].astype(F32)
         xn[pl.ds(pl.multiple_of(i * step, step), step), :] = (u * rms_unit(u) * gains[0:1, :]).astype(BF)
 
+    go.forward()
     gq.done()
     for g in ffn:
         g.stage_own()
@@ -292,6 +346,7 @@
         cs.append(net.put(blk, blk, sib))
     cc[1].wait_recv()
     ch.wait_recv()
+    ffn[0].forward()
     mine_part = part.at[near * 2 + c]
 
     @pl.loop(0, rows // step)
@@ -308,6 +363,8 @@
     mine = xf.at[a, t]
     got = [net.put(mine, mine, net.flip(*f)) for f in FLIP8]
     tail = [net.put(mine, mine, sib)]
+    ffn[1].forward()
+    ffn[2].forward()
     for (da, dh), cp in zip(FLIP8, got):
         cp.wait_recv()
         blk = xf.at[1 - a if da else a, tt if dh else t]
@@ -320,29 +377,32 @@
     net.finish()
 
 
-def m1(tok, cot, wq, wo, wg, wu, wd, gn, cos, sin, seq, blk):
+def m1(tok, cot, weights, g_a, g_f, seq, blk, pos):
     rows, d = tok.shape
     n = 4 * rows
     sd = jax.ShapeDtypeStruct
-    col = lambda v: v.reshape(n, 1)
-    row = lambda v: v.reshape(1, n)
+    v = pltpu.VMEM
+    row = lambda u: u.reshape(1, n)
+    freq = 1.0 / ROPE_BASE ** (np.arange(HD // 2, dtype=np.float32) * 2.0 / HD)
+    freq = jnp.asarray(np.tile(freq, 4)[None], F32)
+    ffn = [sd((2, 4, 4, 64, FH), BF)] * 3
     return pl.pallas_call(
         m1_body,
         out_shape=[
             sd((2, 4, rows, d), BF), sd((rows, d), F32), sd((n, d), BF), sd((n, 512), BF), sd((4, n, 128), BF),
-            sd((n, 512), BF), sd((8, d), F32), sd((2, 4, 4) + wq.shape, BF), sd((2, 4, 4) + wo.shape, BF),
-            sd((2, 4, rows, d), BF),
-        ] + [sd((2, 4, 4) + w.shape[1:], BF) for w in (wg, wu, wd)],
-        in_specs=[ANY] * 8 + [VM] * 6,
-        out_specs=[VM] * 9 + [ANY] * 4,
+            sd((n, 512), BF), sd((8, d), F32), sd((2, 4, 4, 64, 640), BF), sd((2, 4, 4, 64, 512), BF),
+            sd((n, 128), F32), sd((n, 128), F32), sd((n, n), F32), sd((2, 4, rows, d), BF),
+        ] + ffn,
+        in_specs=[ANY] * 2 + [VM] * 13,
+        out_specs=[VM] * 12 + [ANY] * 4,
         scratch_shapes=[
-            pltpu.VMEM((4, rows, d), BF), pltpu.VMEM((2, 4, 4, 8, 128), F32), pltpu.VMEM((n, n), F32),
-            pltpu.VMEM((2, n, 128), BF), pltpu.VMEM((n, 128), F32), pltpu.VMEM((4, rows, d), BF),
-            pltpu.VMEM((2, rows, d), BF), pltpu.VMEM((rows, d), BF),
-        ] + sems(110, 12),
+            v((64, 640), BF), v((3, 2, 64, FH), BF), v((8, 128), F32),
+            v((4, rows, d), BF), v((2, 4, 4, 8, 128), F32), v((n, n), F32),
+            v((2, n, 128), BF), v((4, rows, d), BF), v((2, rows, d), BF), v((rows, d), BF),
+        ] + sems(124, 12),
         compiler_params=pltpu.CompilerParams(collective_id=1, has_side_effects=True, vmem_limit_bytes=56 << 20),
         name="attention_forward",
-    )(tok, cot, wq, wo, wg, wu, wd, gn, cos, sin, row(seq), col(seq), row(blk), col(blk))
+    )(tok, cot, *weights, g_a, g_f, freq, row(seq), row(blk), row(pos))
 
 
 def scatter8_start(net, part, ploc, rc):
@@ -421,6 +481,40 @@
         self.yc = net.put(r2.at[1 - net.a, 0], dst, net.flip(1, 0))
 
 
+def weight_grad(net, left, right, out, chunk, stage, csem, ssem):
+    def load(i, k):
+        sl = pl.ds(pl.multiple_of(i * 256, 256), 256)
+        return pltpu.make_async_copy(left.at[:, sl], chunk.at[k], csem.at[k])
+
+    def save(i, k):
+        return pltpu.make_async_copy(stage.at[k], out.at[lax.div(i, 4), lax.rem(i, 4)], ssem.at[k])
+
+    load(0, 0).start()
+
+    @pl.loop(0, 4)
+    def _(j):
+        for k in range(2):
+            i = 2 * j + k
+            load(i, k).wait()
+            if k == 0:
+                load(i + 1, 1).start()
+            else:
+
+                @pl.when(j < 3)
+                def _():
+                    load(i + 1, 0).start()
+
+            @pl.when(j > 0)
+            def _():
+                save(i - 2, k).wait()
+
+            stage[k] = dot(chunk[k], right[...], TN).reshape(4, 64, FH).astype(BF)
+            save(i, k).start()
+
+    save(6, 0).wait()
+    save(7, 1).wait()
+
+
 def m3_body(names, *refs):
     r = dict(zip(names, refs))
     net = Net(r["send"], r["recv"], r["loc"])
@@ -433,14 +527,14 @@
     far, near = 1 - hi, hi
     sib, chip = net.sib(), net.flip(0, 1)
     bcc, blc = scatter8_start(net, r["fback"], r["bl"], r["bc"])
-    ffn = [Scatter(net, r["p" + k], r["r1" + k], r["r2" + k], r["l" + k]) for k in "gud"]
-    for sc in ffn:
-        sc.stage_one()
-    bgot = scatter8_send(net, bcc, blc, r["bl"], r["bc"], r["by"], rows)
     bias = r["bias"]
-    bias[...] = jnp.where(
-        (r["seqc"][...] == r["seqr"][...]) & (r["blkc"][...] <= r["blkr"][...]), jnp.float32(0.0), jnp.float32(-1e30)
-    )
+    ffn = []
+    for i, (k, left, right) in enumerate((("d", "call", "hid"), ("g", "xf", "dgate"), ("u", "xf", "dup"))):
+        weight_grad(net, r[left], r[right], r["p" + k], r["chunk"], r["stage"], r["csem"], r["ssem"])
+        ffn.append(Scatter(net, r["p" + k], r["r1" + k], r["r2" + k], r["l" + k]))
+        ffn[i].stage_one()
+        if i == 0:
+            bgot = scatter8_send(net, bcc, blc, r["bl"], r["bc"], r["by"], rows)
     for cp in bgot:
         cp.wait_recv()
     gm, gmid, bl, bc, by = r["gm"], r["gmid"], r["bl"], r["bc"], r["by"]
@@ -455,16 +549,23 @@
         gmid[sl, :] = m
         gm[t, sl, :] = m.astype(BF)
 
+    free = r["free"]
+    for f in FLIP8:
+        pl.semaphore_signal(free, inc=1, device_id=net.flip(*f), device_id_type=MESH)
     mine = gm.at[t]
     mf = net.put(mine, mine, chip)
     ms = [net.put(mine, mine, sib)]
-    fcc, flc = scatter8_start(net, r["fout"], r["fl"], r["fc"])
-    fgot = scatter8_send(net, fcc, flc, r["fl"], r["fc"], r["fy"], rows)
     mf.wait_recv()
     theirs = gm.at[far * 2 + c]
     ms.append(net.put(theirs, theirs, sib))
     for cp in ms:
         cp.wait_recv()
+    for cp in bgot:
+        cp.wait_send()
+        net.drop(cp)
+    pl.semaphore_wait(free, len(FLIP8))
+    fcc, flc = scatter8_start(net, r["fout"], bl, bc)
+    fgot = scatter8_send(net, fcc, flc, bl, bc, by, rows)
     gatt, att, q, kv4, wq, wo = r["gatt"], r["att"], r["q"], r["kv4"], r["wq"], r["wo"]
     for i in range(2):
         w = wo[:, :, :, :, 256 * i : 256 * i + 256].reshape(d, 256)
@@ -530,14 +631,14 @@
     so.stage_two()
     for cp in fgot:
         cp.wait_recv()
-    fl, fc, fy, res, gtok = r["fl"], r["fc"], r["fy"], r["res"], r["gtok"]
+    res, gtok = r["res"], r["gtok"]
 
     @pl.loop(0, rows // step)
     def _(i):
         sl = pl.ds(pl.multiple_of(i * step, step), step)
-        g = fl[3, sl, :].astype(F32) + fc[3, sl, :].astype(F32)
+        g = bl[3, sl, :].astype(F32) + bc[3, sl, :].astype(F32)
         for j in range(3):
-            g += fy[j, sl, :].astype(F32)
+            g += by[j, sl, :].astype(F32)
         res[sl, :] = (mid[sl, :] + g).astype(BF)
 
     sq.stage_two()
@@ -551,45 +652,68 @@
         g = an[sl, :].astype(F32) + arc[1, sl, :].astype(F32) + arh[sl, :].astype(F32)
         gtok[sl, :] = (gmid[sl, :] + norm_back(tok[sl, :].astype(F32), g, gains[0:1, :])).astype(BF)
 
-    outs = [r["og"], r["ou"], r["od"]]
-    for sc, o in zip(ffn, outs):
+    for sc, k in zip(ffn, "dgu"):
+        o = r["y" + k]
         sc.stage_y(o.at[a])
         o[a] = sc.r2[a, 0]
     so.stage_y(r["yo"])
     sq.stage_y(r["yq"])
+    dg = r["dg"]
     for sc in ffn:
         sc.yc.wait_recv()
-    for sc, o, y in ((so, r["oo"], r["yo"]), (sq, r["oq"], r["yq"])):
-        sc.yc.wait_recv()
-        add_to(o, [sc.r2.at[a, 0], y], 64)
+    tot = jnp.zeros((64, 128), F32)
+    for k in "gu":
+        y, w = r["y" + k], r["w_" + k]
+        for i in range(w.shape[1] // 128):
+            lo, half = 128 * i % FH, 128 * i // FH
+            tot += y[half, :, lo : lo + 128].astype(F32) * w[:, 128 * i : 128 * i + 128].astype(F32)
+    dg[1] = tot
+    so.yc.wait_recv()
+    add_to(r["oo"], [so.r2.at[a, 0], r["yo"]], 64)
+    sq.yc.wait_recv()
+    dw = sq.r2[a, 0].astype(F32) + r["yq"][...].astype(F32)
+    nq = r["oq"].shape[1]
+    dk, dv = dw[:, nq : nq + HD], dw[:, nq + HD :]
+    r["oq"][...] = dw[:, :nq]
+    r["ok"][...] = dk
+    r["ov"][...] = dv
+    tot = jnp.zeros((64, 128), F32)
+    for i in range(nq // 128):
+        sl = slice(128 * i, 128 * i + 128)
+        tot += dw[:, sl] * r["w_q"][:, sl].astype(F32)
+    small = dk * r["w_k"][...].astype(F32) + dv * r["w_v"][...].astype(F32)
+    dg[0] = tot + jnp.concatenate([small, jnp.zeros_like(small)], 1)
+    for at, peer in enumerate((sib, chip)):
+        cp = net.put(dg, r["dy"].at[at], peer)
+        cp.wait()
+        net.drop(cp)
+        dg[...] += r["dy"][at]
+    for i, (o, g) in enumerate((("dg1", "g_a"), ("dg2", "g_f"))):
+        r[o][...] = jnp.sum(dg[i].T, 0, keepdims=True) / r[g][...].astype(F32)
     net.finish()
 
 
-def m3(fback, fout, pg, pu, pd, mid, cot, tok, gains, xn, q, kv4, att, wq, wo, cos, sin, seq, blk):
-    rows, d = tok.shape
+def m3(hbm, vmem, shapes):
+    rows, d = shapes
     n = 4 * rows
     sd = jax.ShapeDtypeStruct
     v = pltpu.VMEM
-    col = lambda u: u.reshape(n, 1)
-    row = lambda u: u.reshape(1, n)
-    ins = dict(
-        fback=fback, fout=fout, pg=pg, pu=pu, pd=pd,
-        mid=mid, cot=cot, tok=tok, gains=gains, xn=xn, q=q, kv4=kv4, att=att, wq=wq, wo=wo, cos=cos, sin=sin,
-        seqr=row(seq), seqc=col(seq), blkr=row(blk), blkc=col(blk),
-    )
-    w3 = (2, 64, FH)
+    part = (2, 4, 4, 64, FH)
     outs = dict(
-        og=sd(w3, BF), ou=sd(w3, BF), od=sd(w3, BF), oo=sd((64, 512), F32), oq=sd((64, 640), F32),
-        res=sd((rows, d), BF), gtok=sd((rows, d), BF),
+        yg=sd((2, 64, FH), BF), yu=sd((2, 64, FH), BF), yd=sd((2, 64, FH), BF), oo=sd((64, 512), F32),
+        oq=sd((64, 512), F32), ok=sd((64, HD), F32), ov=sd((64, HD), F32),
+        res=sd((rows, d), BF), gtok=sd((rows, d), BF), dg1=sd((1, 64), F32), dg2=sd((1, 64), F32),
+        pg=sd(part, BF), pu=sd(part, BF), pd=sd(part, BF),
     )
     scr = dict(
         bl=v((4, rows, d), BF), bc=v((4, rows, d), BF), by=v((3, rows, d), BF),
-        fl=v((4, rows, d), BF), fc=v((4, rows, d), BF), fy=v((3, rows, d), BF),
-        gm=v((4, rows, d), BF), gmid=v((rows, d), F32), bias=v((n, n), F32), gatt=v((n, 512), BF),
+        gm=v((4, rows, d), BF), gmid=v((rows, d), F32), gatt=v((n, 512), BF),
         dqkv=v((n, 640), BF), ak=v((n, 128), F32), av=v((n, 128), F32),
         po=v((2, 4, 4, 64, 512), BF), pq=v((2, 4, 4, 64, 640), BF),
         ap=v((4, rows, d), BF), arc=v((2, rows, d), BF), arh=v((rows, d), BF),
-        yo=v((64, 512), BF), yq=v((64, 640), BF),
+        yo=v((64, 512), BF), yq=v((64, 640), BF), dg=v((2, 64, 128), F32), dy=v((2, 2, 64, 128), F32),
+        chunk=v((2, 2 * n, 256), BF), stage=v((2, 4, 64, FH), BF),
+        csem=pltpu.SemaphoreType.DMA((2,)), ssem=pltpu.SemaphoreType.DMA((2,)), free=pltpu.SemaphoreType.REGULAR,
     )
     for k, w in (("g", FH), ("u", FH), ("d", FH), ("o", 512), ("q", 640)):
         scr["r1" + k] = v((2, 3, 4, 64, w), BF)
@@ -597,34 +721,42 @@
     for k in "gud":
         scr["l" + k] = v((2, 4, 64, FH), BF)
     sem = sems(100, 24)
-    names = list(ins) + list(outs) + list(scr) + ["send", "recv", "loc"]
+    names = list(hbm) + list(vmem) + list(outs) + list(scr) + ["send", "recv", "loc"]
     got = pl.pallas_call(
         functools.partial(m3_body, names),
         out_shape=list(outs.values()),
-        in_specs=[ANY] * 5 + [VM] * (len(ins) - 5),
-        out_specs=[VM] * len(outs),
+        in_specs=[ANY] * len(hbm) + [VM] * len(vmem),
+        out_specs=[VM] * (len(outs) - 3) + [ANY] * 3,
         scratch_shapes=list(scr.values()) + sem,
         compiler_params=pltpu.CompilerParams(collective_id=3, has_side_effects=True, vmem_limit_bytes=62 << 20),
         name="attention_backward",
-    )(*ins.values())
+    )(*hbm.values(), *vmem.values())
     return dict(zip(outs, got))
-
-
-def rope_tables(places, head_width):
-    half_width = head_width // 2
-    inv_freq = 1.0 / ROPE_BASE ** (jnp.arange(half_width, dtype=F32) * 2.0 / head_width)
-    angles = places.astype(F32)[:, None] * inv_freq[None, :]
-    angles = jnp.concatenate([angles, angles], -1)
-    return (jnp.cos(angles), jnp.sin(angles))
 
 
 def mm(l, r, dims=((1,), (0,))):
     return lax.dot_general(l, r, (dims, ((), ())), preferred_element_type=F32)
 
 
-def halves(w):
-    w = jnp.pad(w, ((0, 0), (0, 2 * FH - w.shape[1])))
-    return jnp.stack([w[:, :FH], w[:, FH:]])
+def final_body(yg, yu, yd, *refs):
+    k = (len(refs) - 3) // 2
+    for y, o in zip((yg, yu, yd), refs[k : k + 3]):
+        rest = o.shape[1] - FH
+        o[:, :FH] = y[0].astype(F32)
+        o[:, FH:] = y[1, :, :rest].astype(F32)
+    for i, o in zip(refs[:k], refs[k + 3 :]):
+        o[...] = i[...]
+
+
+def final(halves, others, ff):
+    sd = jax.ShapeDtypeStruct
+    return pl.pallas_call(
+        final_body,
+        out_shape=[sd((64, ff), F32)] * 3 + [sd(o.shape, o.dtype) for o in others],
+        in_specs=[VM] * (3 + len(others)),
+        out_specs=[VM] * (3 + len(others)),
+        name="final",
+    )(*halves, *others)
 
 
 def per_device(
@@ -633,19 +765,10 @@
 ):
     rows, d = tokens_in.shape
     n = seq_ids.shape[0]
-    ff = w_gate.shape[1]
-    hq = w_query.shape[1] // HD
-    wq = jnp.concatenate([w_query, w_key, w_value], 1)
-    wo = w_out.T
-    gn = jnp.pad(jnp.stack([attn_gain, ffn_gain]).astype(F32), ((0, 6), (0, 64)))
-    gn = jnp.where(lax.rem(lax.axis_index("dp"), 2) == 0, gn, jnp.roll(gn, 64, 1))
-    cosine, sine = rope_tables(positions, HD)
-    half = HD // 2
-    signed = jnp.concatenate([-sine[:, :half], sine[:, half:]], -1)
-    cos2, sin2 = jnp.concatenate([cosine] * 2, -1), jnp.concatenate([signed] * 2, -1)
-    xf, mid, xn, q, kv4, att, gains, wqkv, wot, cot, wg, wu, wdt = m1(
-        tokens_in, cotangent, wq, wo, halves(w_gate), halves(w_up), halves(w_down.T), gn,
-        cos2, sin2, seq_ids, block_ids,
+    weights = (w_query, w_key, w_value, w_out.T, w_gate, w_up, w_down.T)
+    g_a, g_f = attn_gain.reshape(1, -1), ffn_gain.reshape(1, -1)
+    xf, mid, xn, q, kv4, att, gains, wqkv, wot, cos, sin, bias_t, cot, wg, wu, wdt = m1(
+        tokens_in, cotangent, weights, g_a, g_f, seq_ids, block_ids, positions
     )
     cot = cot.reshape(2 * n, d)
     wg, wu, wdt = (w.reshape(d, FH) for w in (wg, wu, wdt))
@@ -660,27 +783,20 @@
     dup = (gh * silu).astype(BF)
     fback = (mm(dgate, wg, NT) + mm(dup, wu, NT)).astype(BF).reshape(2, 4, rows, d)
     fout = mm(hid, wdt, NT).astype(BF).reshape(2, 4, rows, d)
-    pd = mm(cot, hid, TN).astype(BF)
-    pg = mm(xf, dgate, TN).astype(BF)
-    pu = mm(xf, dup, TN).astype(BF)
-    pg, pu, pd = (w.reshape(2, 4, 4, 64, FH) for w in (pg, pu, pd))
     out = m3(
-        fback, fout, pg, pu, pd, mid, cotangent, tokens_in, gains, xn, q, kv4, att, wqkv, wot,
-        cos2, sin2, seq_ids, block_ids,
+        dict(fback=fback, fout=fout, xf=xf, call=cot),
+        dict(
+            hid=hid, dgate=dgate, dup=dup, mid=mid, cot=cotangent, tok=tokens_in, gains=gains, xn=xn, q=q, kv4=kv4,
+            att=att, wq=wqkv, wo=wot, cos=cos, sin=sin, bias=bias_t,
+            w_q=w_query, w_k=w_key, w_v=w_value, w_g=w_gate, w_u=w_up, g_a=g_a, g_f=g_f,
+        ),
+        (rows, d),
     )
-    og, ou, od, oo, oq, res, gtok = (out[k] for k in ("og", "ou", "od", "oo", "oq", "res", "gtok"))
-
-    def join(o):
-        return jnp.concatenate([o[0], o[1]], 1)[:, :ff].astype(F32)
-
-    og, ou, od = join(og), join(ou), join(od)
-    dg1 = jnp.sum(oq * wq.astype(F32), 1) / attn_gain.astype(F32)
-    dg2 = jnp.sum(og * w_gate.astype(F32) + ou * w_up.astype(F32), 1) / ffn_gain.astype(F32)
-    dg1, dg2 = lax.psum((dg1, dg2), "tensor")
-    nq = hq * HD
-    return (
-        res, gtok, dg1, dg2, oq[:, :nq], oq[:, nq : nq + HD], oq[:, nq + HD :], oo.T, og, ou, od.T,
+    keep = ("res", "gtok", "dg1", "dg2", "oq", "ok", "ov", "oo")
+    og, ou, od, res, gtok, dg1, dg2, oq, ok, ov, oo = final(
+        [out[k] for k in ("yg", "yu", "yd")], [out[k] for k in keep], w_gate.shape[1]
     )
+    return (res, gtok, dg1.reshape(-1), dg2.reshape(-1), oq, ok, ov, oo.T, og, ou, od.T)
 
 
 def solution(mesh):

time: 315 us -> 277 us (0.88)
  matrix products: 43 us -> 27.9 us
  local copies, waits for them, and re-layouts: 13.5 us -> 0.03 us
  other arithmetic: 11.3 us -> 0 us
  Pallas kernels: 238 us -> 247 us
  blocking collectives: 8.04 us -> 0 us
    dot_general x9 -> x6, matrix products: 43 us -> 27.9 us  [mm(): return lax.dot_general(l, r, (dims, ((), ())), preferred_element_type=F32)]
    pallas_call x1, Pallas kernels: 115 us -> 129 us  [m3(): pl.pallas_call(functools.partial(m3_body, names), out_shape=list(outs.val...]
    psum x1 -> x0, blocking collectives: 8.04 us -> none  [per_device(): dg1, dg2 = lax.psum((dg1, dg2), 'tensor')]
    pallas_call x1, Pallas kernels: 123 us -> 115 us  [m1(): pl.pallas_call(m1_body, out_shape=[sd((2, 4, rows, d), BF), sd((rows, d),...]
where the time goes in v4:
time: 277 us; the launch traced here: 276 us
  Pallas kernels  247 us (89%)
  matrix products  27.9 us (10%)
    pallas_call x1, Pallas kernels, m3(): pl.pallas_call(functools.partial(m3_body, names), out_shape=list(outs.val...  129 us
    pallas_call x1, Pallas kernels, m1(): pl.pallas_call(m1_body, out_shape=[sd((2, 4, rows, d), BF), sd((rows, d),...  115 us
    dot_general x6, matrix products, mm(): return lax.dot_general(l, r, (dims, ((), ())), preferred_element_type=F32)  27.9 us

profile of v4, /device:TPU:1, one launch (start us, length us, event | category | flops | bytes accessed | tf_op | source)
XLA Modules:
  0.0 275.9 jit_solution(9573324547142124366)
XLA Ops:
  0.6 115.2 %attention_forward.1 = (bf16[2,4,128,2048]{3,2,1,0:T(8,128)(2,1)}, f32[128,2048]{1,0:T(8,128)}, bf16[512,2048]{1,0:T(8,128)(2,1)}, bf16[512,512]{1,0:T(8,128)(2,...) custom-call(bf16[128,2048]{1,0:T(8,128)(2,1)} %refs_9_.1, ...), custom_call_target="tpu_custom_call" | custom-call | tf_op jit(solution)/shard_map/attention_forward/pallas_call | solution.py:389
  115.9 0.0 copy-start.1
  115.9 0.0 copy-start.5
  115.9 6.5 %fusion.2 = f32[1024,768]{1,0:T(8,128)S(1)} fusion(bf16[1024,2048]{1,0:T(8,128)(2,1)} %bitcast.30, bf16[2048,768]{1,0:T(8,128)(2,1)} %bitcast.50), kind=kOutput, calls=%fused_computation.8 | convolution fusion | flops 3221225472 | bytes 10485760 | tf_op jit(solution)/shard_map/dot_general | solution.py:738
  122.4 0.0 copy-done.1
  122.4 0.0 copy-done.5
  122.4 0.0 copy-start
  122.4 0.0 copy-start.6
  122.4 3.4 %fusion.1 = f32[1024,768]{1,0:T(8,128)S(1)} fusion(bf16[1024,2048]{1,0:T(8,128)(2,1)S(1)} %bitcast.34, bf16[2048,768]{1,0:T(8,128)(2,1)S(1)} %bitcast.46), kind=kOutput, calls=%fused_computation.7 | convolution fusion | flops 3221225472 | bytes 10485760 | tf_op jit(solution)/shard_map/dot_general | solution.py:738
  125.9 0.0 copy-done
  125.9 0.0 copy-done.6
  125.9 0.0 copy-start.7
  125.9 4.5 %multiply_convert_fusion = (bf16[1024,768]{1,0:T(8,128)(2,1)S(1)}, bf16[1024,768]{1,0:T(8,128)(2,1)S(1)}, bf16[1024,768]{1,0:T(8,128)(2,1)S(1)}) fusion(f32[1024,768]{1,0:T(8,128)S(1)} %fusion.2, f32[1024,768]{1,0:T(8,128)S(1)} %fusion.1, bf16[1024,2048]{1,0:T(8,128)(2,1)S(1)} %bitcast.32, bf16[2048,768]{1,0:T(8,128)(2,1)S(1)} %bitcast.48), kind=kOutput, calls=%fused_computation.2 | convolution fusion | flops 3233021952 | bytes 18350080 | tf_op jit(solution)/shard_map/dot_general | solution.py:738
  130.4 0.0 copy-start.3
  130.4 0.0 copy-start.4
  130.5 0.0 copy-start.2
  130.5 0.0 copy-done.7
  130.5 3.4 %fusion.3 = f32[1024,2048]{1,0:T(8,128)S(1)} fusion(bf16[1024,768]{1,0:T(8,128)(2,1)S(1)} %get-tuple-element.88.refs_5_, bf16[2048,768]{1,0:T(8,128)(2,1)S(1)} %bitcast.51), kind=kOutput, calls=%fused_computation.9 | convolution fusion | flops 3221225472 | bytes 13107200 | tf_op jit(solution)/shard_map/dot_general | solution.py:738
  133.9 0.0 copy-done.3
  133.9 0.0 copy-done.4
  133.9 5.1 %add_convert_fusion = bf16[1024,2048]{1,0:T(8,128)(2,1)} fusion(f32[1024,2048]{1,0:T(8,128)S(1)} %fusion.3, bf16[1024,768]{1,0:T(8,128)(2,1)S(1)} %get-tuple-element.89.refs_6_, bf16[2048,768]{1,0:T(8,128)(2,1)S(1)} %bitcast.49), kind=kOutput, calls=%fused_computation | convolution fusion | flops 3225419776 | bytes 17301504 | tf_op jit(solution)/shard_map/dot_general | solution.py:738
  139.0 0.0 copy-done.2
  139.0 5.0 %convolution_convert_fusion = bf16[1024,2048]{1,0:T(8,128)(2,1)} fusion(bf16[1024,768]{1,0:T(8,128)(2,1)S(1)} %get-tuple-element.87.refs_4_, bf16[2048,768]{1,0:T(8,128)(2,1)S(1)} %bitcast.47), kind=kOutput, calls=%fused_computation.1 | convolution fusion | flops 3223322624 | bytes 8912896 | tf_op jit(solution)/shard_map/dot_general | solution.py:738
  144.0 128.8 %attention_backward.1 = (bf16[2,64,768]{2,1,0:T(8,128)(2,1)}, bf16[2,64,768]{2,1,0:T(8,128)(2,1)}, bf16[2,64,768]{2,1,0:T(8,128)(2,1)}, f32[64,512]{1,0:T(8,128)...) custom-call(bf16[2,4,128,2048]{3,2,1,0:T(8,128)(2,1)} %bitcast.35, ...), custom_call_target="tpu_custom_call" | custom-call | tf_op jit(solution)/shard_map/attention_backward/pallas_call | solution.py:725
  272.8 3.0 %final.1 = (f32[64,1408]{1,0:T(8,128)}, f32[64,1408]{1,0:T(8,128)}, f32[64,1408]{1,0:T(8,128)}, bf16[128,2048]{1,0:T(8,128)(2,1)}, bf16[128,2048]{1,0:T(8,128)(2...) custom-call(bf16[2,64,768]{2,1,0:T(8,128)(2,1)} %get-tuple-element.6, ...), custom_call_target="tpu_custom_call" | custom-call | tf_op jit(solution)/shard_map/final/pallas_call | solution.py:753
Async XLA Ops:
  115.9 6.5 %copy-start.1 = (bf16[2,4,128,2048]{3,2,1,0:T(8,128)(2,1)S(1)}, bf16[2,4,128,2048]{3,2,1,0:T(8,128)(2,1)}, u32[]{:S(2)}) copy-start(bf16[2,4,128,2048]{3,2,1,0:T(8,128)(2,1)} %get-tuple-element.49) | copy-start | bytes 12582916
  115.9 6.5 %copy-start.5 = (bf16[2,4,4,64,768]{4,3,2,1,0:T(8,128)(2,1)S(1)}, bf16[2,4,4,64,768]{4,3,2,1,0:T(8,128)(2,1)}, u32[]{:S(2)}) copy-start(bf16[2,4,4,64,768]{4,3,2,1,0:T(8,128)(2,1)} %get-tuple-element.50) | copy-start | bytes 9437188
  122.4 3.5 %copy-start = (bf16[2,4,128,2048]{3,2,1,0:T(8,128)(2,1)S(1)}, bf16[2,4,128,2048]{3,2,1,0:T(8,128)(2,1)}, u32[]{:S(2)}) copy-start(bf16[2,4,128,2048]{3,2,1,0:T(8,128)(2,1)} %get-tuple-element.51) | copy-start | bytes 12582916
  122.4 3.5 %copy-start.6 = (bf16[2,4,4,64,768]{4,3,2,1,0:T(8,128)(2,1)S(1)}, bf16[2,4,4,64,768]{4,3,2,1,0:T(8,128)(2,1)}, u32[]{:S(2)}) copy-start(bf16[2,4,4,64,768]{4,3,2,1,0:T(8,128)(2,1)} %get-tuple-element.52) | copy-start | bytes 9437188
  125.9 4.6 %copy-start.7 = (bf16[2,4,4,64,768]{4,3,2,1,0:T(8,128)(2,1)S(1)}, bf16[2,4,4,64,768]{4,3,2,1,0:T(8,128)(2,1)}, u32[]{:S(2)}) copy-start(bf16[2,4,4,64,768]{4,3,2,1,0:T(8,128)(2,1)} %get-tuple-element.53) | copy-start | bytes 9437188
  130.4 3.5 %copy-start.3 = (bf16[1024,768]{1,0:T(8,128)(2,1)}, bf16[1024,768]{1,0:T(8,128)(2,1)S(1)}, u32[]{:S(2)}) copy-start(bf16[1024,768]{1,0:T(8,128)(2,1)S(1)} %get-tuple-element.88.refs_5_) | copy-start | bytes 4718596
  130.4 3.5 %copy-start.4 = (bf16[1024,768]{1,0:T(8,128)(2,1)}, bf16[1024,768]{1,0:T(8,128)(2,1)S(1)}, u32[]{:S(2)}) copy-start(bf16[1024,768]{1,0:T(8,128)(2,1)S(1)} %get-tuple-element.89.refs_6_) | copy-start | bytes 4718596
  130.5 8.5 %copy-start.2 = (bf16[1024,768]{1,0:T(8,128)(2,1)}, bf16[1024,768]{1,0:T(8,128)(2,1)S(1)}, u32[]{:S(2)}) copy-start(bf16[1024,768]{1,0:T(8,128)(2,1)S(1)} %get-tuple-element.87.refs_4_) | copy-start | bytes 4718596
